TPU v7x, 32 devices: a whole 2x2x4 slice. The times are simulated.
32 devices in a mesh: group: 2 (over y), seq: 4 (over z), shard: 2 (over x), guide: 2 (over core).
Axes of the slice: x: 2, y: 2, z: 4, core: 2. Of those that a mesh axis runs over, the one named last changes fastest.
Arguments:
- queries: bfloat16 [2, 2, 512, 2560], P('guide', 'group', 'seq', 'shard'), parts along dimension 1, may hold values from -120 to 120
- key_vecs: bfloat16 [2, 2, 512, 2560], P('guide', 'group', 'seq', 'shard'), parts along dimension 1, may hold values from -4 to 4
- value_vecs: bfloat16 [2, 2, 512, 2560], P('guide', 'group', 'seq', 'shard'), parts along dimension 1, may hold values from -24 to 24
- residual: bfloat16 [2, 2, 512, 5120], P('guide', 'group', 'seq', 'shard'), parts along dimension 1, may hold values from -64 to 64
- w_out: bfloat16 [2560, 5120], P('shard', 'guide'), may hold values from -0.125 to 0.125
- attn_gate: float32 [2, 5120], P('group', 'shard'), parts along dimension 0, may hold values from 2 to 4
- norm_shift: float32 [2, 5120], P('group', 'shard'), parts along dimension 0, may hold values from -3 to 3
- norm_scale: float32 [2, 5120], P('group', 'shard'), parts along dimension 0, may hold values from -2.5 to 2.5
- w_head: bfloat16 [5120, 64], P('shard'), may hold values from -0.078125 to 0.078125
- noise: float32 [2, 4, 128, 64], P('group', 'seq', None, 'guide'), parts along dimension 0, may hold values from -6 to 6
- timesteps: int32 [2], P('group'), parts along dimension 0, may hold values from 100 to 980
- frame_owner: int32 [2, 4], P('group'), parts along dimension 0, may hold values from 0 to 3, each once within a row
Outputs:
- sds_grad: float32 [2, 4, 128, 64], P('group', 'seq', None, 'guide'), parts along dimension 0
There are 2 independent parts, one for each index of `group`. A program takes and returns all parts, laid end to end along the dimension named above; an argument that names none is the same for every part. Nothing has to cross between parts.
Inputs may be any that keep to these rules, and one draw needn't show every extreme that they name: `frame_owner`: each row names every owner index once.
All inputs are finite; a program needn't handle non-finite values.
Results may differ from a plain program's by a relative error of at most 0.003.
Values may be sent and summed in bfloat16 or wider, within the bound.
No kernel may reach another device: no remote copies, remote signals or barrier semaphores. Data moves between devices by JAX's collectives and lax.ppermute only.
A program may use at most 128 MiB of HBM per device.

v0:
```python
import functools

import jax
import jax.numpy as jnp
from jax import lax
from jax.experimental import pallas as pl
from jax.experimental.pallas import tpu as pltpu
from jax.sharding import PartitionSpec as P


HEAD_DIM = 128
LANES = 128
SUBLANES = 8
beta_low = 0.0001
beta_high = 0.02
guidance_scale = 3.0
norm_epsilon = 1e-06
LOG2E = 1.4426950408889634


F32 = jnp.float32
BF16 = jnp.bfloat16
VMEM_SPEC = pl.BlockSpec(memory_space=pltpu.VMEM)
SMEM_SPEC = pl.BlockSpec(memory_space=pltpu.SMEM)
HBM_SPEC = pl.BlockSpec(memory_space=pltpu.HBM)


def plan_weight(timesteps):
    steps_float = timesteps.astype(jnp.float32)
    exponent = (steps_float + 1.0) * beta_low + (beta_high - beta_low) * steps_float * (
        steps_float + 1.0
    ) / (2.0 * 999.0)
    return 1.0 - jnp.exp(-exponent)


def attend_all(query_split, keys_all, values_all):
    heads_local = query_split.shape[2]
    keys_split = keys_all.reshape(keys_all.shape[0], keys_all.shape[1], heads_local, HEAD_DIM)
    values_split = values_all.reshape(values_all.shape[0], values_all.shape[1], heads_local, HEAD_DIM)
    scores = jnp.einsum(
        "tqhd,tkhd->tqhk", query_split, keys_split, preferred_element_type=F32
    ) * HEAD_DIM ** (-0.5)
    expo = jnp.exp(scores - jnp.max(scores, axis=-1, keepdims=True))
    total = jnp.sum(expo, axis=-1)
    mixed = jnp.einsum("tqhk,tkhd->tqhd", expo.astype(BF16), values_split, preferred_element_type=F32)
    return (mixed / total[..., None]).astype(BF16)


def general_plan(
    queries, key_vecs, value_vecs, residual, w_out, attn_gate, norm_shift, norm_scale, w_head, noise,
    timesteps, frame_owner,
):
    query_local = queries[0]
    step_count, token_count, width_local = query_local.shape
    heads_local = width_local // HEAD_DIM
    attended = attend_all(
        query_local.reshape(step_count, token_count, heads_local, HEAD_DIM),
        lax.all_gather(key_vecs[0], "seq", axis=1, tiled=True),
        lax.all_gather(value_vecs[0], "seq", axis=1, tiled=True),
    )
    row_count = step_count * token_count
    both_rows = jnp.dot(
        lax.all_gather(attended.reshape(row_count, width_local), "guide", axis=0, tiled=True),
        w_out,
        preferred_element_type=F32,
    )
    half_width = w_out.shape[1]
    swapped = lax.all_to_all(
        both_rows.reshape(2, row_count, half_width), "guide", split_axis=0, concat_axis=2, tiled=True
    )
    projected = swapped.reshape(row_count, 2 * half_width)
    attn_out = lax.psum_scatter(projected, "shard", scatter_dimension=1, tiled=True)
    width_shard = attn_out.shape[1]
    width_model = width_shard * lax.axis_size("shard")
    hidden = residual[0].astype(F32) + attn_gate[:, None, :] * attn_out.reshape(
        step_count, token_count, width_shard
    )
    sum_first, sum_second = lax.psum((jnp.sum(hidden, axis=-1), jnp.sum(hidden * hidden, axis=-1)), "shard")
    mean_row = sum_first / width_model
    var_row = sum_second / width_model - mean_row * mean_row
    inv_std = lax.rsqrt(var_row + norm_epsilon)
    modulated = (hidden - mean_row[..., None]) * inv_std[..., None] * (
        1.0 + norm_scale[:, None, :]
    ) + norm_shift[:, None, :]
    partial_head = jnp.einsum(
        "tqd,dc->tqc", modulated, w_head.astype(F32), precision=lax.Precision.HIGHEST
    )
    predicted = lax.psum(partial_head, "shard")
    seq_count = lax.axis_size("seq")
    frame_group = token_count // seq_count
    frames_view = predicted.reshape(step_count, seq_count, frame_group, predicted.shape[-1])
    owner_table = (
        frame_owner[:, :, None] == jnp.arange(seq_count, dtype=jnp.int32)[None, None, :]
    ).astype(F32)
    by_owner = jnp.einsum("tfo,tfgc->togc", owner_table, frames_view, precision=lax.Precision.HIGHEST)
    arrived = lax.all_to_all(
        lax.all_to_all(by_owner[None], "seq", split_axis=2, concat_axis=3, tiled=True),
        "guide",
        split_axis=4,
        concat_axis=0,
        tiled=True,
    )
    guided = arrived[1] + guidance_scale * (arrived[0] - arrived[1])
    return plan_weight(timesteps)[:, None, None, None] * (guided - noise)


def pack_kernel(parts, half, *refs):
    q_ref, k_ref, v_ref = refs[:3]
    out_refs, sems = refs[3:-1], refs[-1]
    z = lax.axis_index("seq")
    copies = []
    for j in range(parts):
        cols = pl.ds(pl.multiple_of(lax.rem(z + j, parts) * half, LANES), half)
        copies.append(pltpu.make_async_copy(k_ref.at[:, cols], out_refs[j].at[0], sems.at[3 * j]))
        copies.append(pltpu.make_async_copy(v_ref.at[:, cols], out_refs[j].at[1], sems.at[3 * j + 1]))
        copies.append(pltpu.make_async_copy(q_ref.at[:, cols], out_refs[parts + j], sems.at[3 * j + 2]))
    for copy in copies:
        copy.start()
    for copy in copies:
        copy.wait()


def attend_kernel(parts, *refs):
    q_refs = refs[:parts]
    kv_refs = refs[parts : 3 * parts]
    o_refs = refs[3 * parts :]
    rows = q_refs[0].shape[0]
    for i in range(q_refs[0].shape[1] // HEAD_DIM):
        cols = slice(i * HEAD_DIM, (i + 1) * HEAD_DIM)
        q = jnp.concatenate([r[:, cols] for r in q_refs], axis=0)
        k = jnp.concatenate([r[0, :, cols] for r in kv_refs], axis=0)
        v = jnp.concatenate([r[1, :, cols] for r in kv_refs], axis=0)
        scores = lax.dot_general(q, k, (((1,), (1,)), ((), ())), preferred_element_type=F32)
        scores = scores * (HEAD_DIM ** (-0.5) * LOG2E)
        expo = jnp.exp2(scores - jnp.max(scores, axis=1, keepdims=True))
        total = jnp.sum(expo, axis=1, keepdims=True)
        mixed = jnp.dot(expo.astype(BF16), v, preferred_element_type=F32) / total
        for j in range(parts):
            o_refs[j][:, cols] = mixed[j * rows : (j + 1) * rows].astype(BF16)


def project(parts, half, o_refs, w_ref, cols):
    z = lax.axis_index("seq")
    total = None
    for j in range(parts):
        start = pl.multiple_of(lax.rem(z + j, parts) * half, LANES)
        term = jnp.dot(o_refs[j][...], w_ref[pl.ds(start, half), cols], preferred_element_type=F32)
        total = term if total is None else total + term
    return total


def send_kernel(parts, half, chunk, first, *refs):
    o_refs = refs[:parts]
    near_ref, far_ref, out_ref = refs[parts:]
    guide = lax.axis_index("guide")
    for value, w_ref in ((1, near_ref), (0, far_ref)):

        @pl.when(guide == value)
        def _():
            for t in range(out_ref.shape[1] // chunk):
                cols = slice(first + t * chunk, first + (t + 1) * chunk)
                out_ref[:, t * chunk : (t + 1) * chunk] = project(parts, half, o_refs, w_ref, cols).astype(BF16)


def keep_kernel(parts, half, chunk, *refs):
    o_refs = refs[:parts]
    near_ref, far_ref, res_ref, gate_ref, out_ref = refs[parts:]
    guide = lax.axis_index("guide")
    for value, w_ref in ((0, near_ref), (1, far_ref)):

        @pl.when(guide == value)
        def _():
            for t in range(out_ref.shape[1] // chunk):
                cols = slice(t * chunk, (t + 1) * chunk)
                out_ref[:, cols] = res_ref[:, cols].astype(F32) + gate_ref[:, cols] * project(
                    parts, half, o_refs, w_ref, cols
                )


def split_dot(head_t, rows):
    dims = (((1,), (1,)), ((), ()))
    high = rows.astype(BF16)
    low = (rows - high.astype(F32)).astype(BF16)
    return lax.dot_general(head_t, high, dims, preferred_element_type=F32) + lax.dot_general(
        head_t, low, dims, preferred_element_type=F32
    )


def head_rows_kernel(scale_ref, shift_ref, head_ref, out_ref):
    width = scale_ref.shape[1]
    which = lax.broadcasted_iota(jnp.int32, (LANES, width), 0)
    rows = jnp.where(which == 0, 1.0 + scale_ref[...], shift_ref[...])
    high = rows.astype(BF16)
    rest = rows - high.astype(F32)
    mid = rest.astype(BF16)
    low = (rest - mid.astype(F32)).astype(BF16)
    dims = (((1,), (1,)), ((), ()))
    total = None
    for part in (high, mid, low):
        term = lax.dot_general(head_ref[...], part, dims, preferred_element_type=F32)
        total = term if total is None else total + term
    out_ref[...] = total


def head_kernel(first, last, chunk, start, *refs):
    hid_ref, got_ref, gate_ref, scale_ref, head_ref = refs[:5]
    if first:
        out_refs = refs[5:]
    else:
        prev_refs, out_refs = refs[5:8], refs[8:]
    channels = head_ref.shape[0]
    rows = hid_ref.shape[0]
    acc_one = jnp.zeros((rows, LANES), F32) if first else prev_refs[1][...]
    acc_two = jnp.zeros((rows, LANES), F32) if first else prev_refs[2][...]
    acc_head = jnp.zeros((channels, rows), F32) if first else prev_refs[0][...]
    for t in range(got_ref.shape[1] // chunk):
        cols = slice(start + t * chunk, start + (t + 1) * chunk)
        arrived = got_ref[:, t * chunk : (t + 1) * chunk].astype(F32)
        hidden = hid_ref[:, cols] + gate_ref[:, cols] * arrived
        for s in range(chunk // LANES):
            piece = hidden[:, s * LANES : (s + 1) * LANES]
            acc_one = acc_one + piece
            acc_two = acc_two + piece * piece
        acc_head = acc_head + split_dot(head_ref[:, cols], hidden * (1.0 + scale_ref[:, cols]))
    if last:
        out_ref = out_refs[0]
        out_ref[0:channels, :] = acc_head
        sum_one = jnp.sum(acc_one.T, axis=0, keepdims=True)
        sum_two = jnp.sum(acc_two.T, axis=0, keepdims=True)
        row = lax.broadcasted_iota(jnp.int32, (SUBLANES, rows), 0)
        out_ref[channels : channels + SUBLANES, :] = jnp.where(row == 0, sum_one, sum_two)
    else:
        out_refs[0][...] = acc_head
        out_refs[1][...] = acc_one
        out_refs[2][...] = acc_two


def norm_kernel(width_model, own_ref, got_ref, rows_own_ref, rows_got_ref, keep_ref, send_ref, eps_scr):
    channels = rows_own_ref.shape[0]
    half_channels = channels // 2
    guide = lax.axis_index("guide")
    head = own_ref[0:channels, :] + got_ref[0:channels, :]
    stats = own_ref[channels : channels + SUBLANES, :] + got_ref[channels : channels + SUBLANES, :]
    mean = stats[0:1] / width_model
    var = stats[1:2] / width_model - mean * mean
    inv_std = lax.rsqrt(var + norm_epsilon)
    scaled = rows_own_ref[:, 0:1] + rows_got_ref[:, 0:1]
    shifted = rows_own_ref[:, 1:2] + rows_got_ref[:, 1:2]
    eps_scr[...] = (head - mean * scaled) * inv_std + shifted
    keep_ref[...] = eps_scr[pl.ds(pl.multiple_of(guide * half_channels, SUBLANES), half_channels), :]
    send_ref[...] = eps_scr[pl.ds(pl.multiple_of((1 - guide) * half_channels, SUBLANES), half_channels), :]


def frame_kernel(seq_count, group, owner_ref, keep_ref, got_ref, *out_refs):
    z = lax.axis_index("seq")
    first = lax.axis_index("guide") == 0
    mine, other = keep_ref[...], got_ref[...]
    eps_cond = jnp.where(first, mine, other)
    eps_free = jnp.where(first, other, mine)
    guided = eps_free + guidance_scale * (eps_cond - eps_free)
    fold = LANES // group
    rows = guided.shape[0] // fold
    lane = lax.broadcasted_iota(jnp.int32, (rows, LANES), 1) // group
    for k in range(seq_count):
        target = lax.rem(z + k, seq_count)
        frame = jnp.int32(0)
        for f in range(seq_count):
            frame = jnp.where(owner_ref[0, f] == target, f, frame)
        packed = jnp.zeros((rows, LANES), F32)
        for j in range(fold):
            shift = lax.rem((j - frame) * group + LANES, LANES)
            rolled = pltpu.roll(guided[j * rows : (j + 1) * rows], shift, axis=1)
            packed = jnp.where(lane == j, rolled, packed)
        out_refs[k][...] = packed


def final_kernel(seq_count, group, steps_ref, noise_ref, *refs):
    piece_refs, out_ref = refs[:seq_count], refs[seq_count]
    z = lax.axis_index("seq")
    fold = LANES // group
    rows = piece_refs[0].shape[0]
    lane = lax.broadcasted_iota(jnp.int32, (rows, LANES), 1) // group
    blocks = []
    for j in range(fold):
        block = jnp.zeros((rows, LANES), F32)
        for k in range(seq_count):
            source = lax.rem(z - k + seq_count, seq_count)
            shift = lax.rem((source - j) * group + LANES, LANES)
            block = jnp.where(lane == source, pltpu.roll(piece_refs[k][...], shift, axis=1), block)
        blocks.append(block)
    framed = jnp.concatenate(blocks, axis=0)
    step = jnp.full((1, 1), steps_ref[0], jnp.int32)
    out_ref[...] = plan_weight(step) * (framed - noise_ref[...])


def call(kernel, outs, args, specs=None, scratch=(), flops=0, moved=0, grant=16):
    shapes = [jax.ShapeDtypeStruct(s, d) for s, d in outs]
    return pl.pallas_call(
        kernel,
        out_shape=shapes,
        in_specs=specs or [VMEM_SPEC] * len(args),
        out_specs=[VMEM_SPEC] * len(outs),
        scratch_shapes=list(scratch),
        compiler_params=pltpu.CompilerParams(vmem_limit_bytes=grant << 20),
        cost_estimate=pl.CostEstimate(flops=flops, bytes_accessed=moved, transcendentals=0),
    )(*args)


def fast_plan(
    queries, key_vecs, value_vecs, residual, w_out, attn_gate, norm_shift, norm_scale, w_head, noise,
    timesteps, frame_owner,
):
    seq_count = lax.axis_size("seq")
    parts = seq_count // 2
    rows, width_local = queries.shape[2:]
    half = width_local // parts
    width_shard = residual.shape[3]
    channels = w_head.shape[1]
    group = rows // seq_count
    width_model = float(width_shard * lax.axis_size("shard"))
    both = [(0, 1), (1, 0)]
    axes = ("seq", "guide")

    crossed = [(x * 2 + c, x * 2 + (c + x) % 2) for x in range(2) for c in range(2)]
    straight = [(x * 2 + c, x * 2 + (c + x + 1) % 2) for x in range(2) for c in range(2)]

    packed = call(
        functools.partial(pack_kernel, parts, half),
        [((2, rows, half), BF16)] * parts + [((rows, half), BF16)] * parts,
        [
            pltpu.with_memory_space_constraint(array[0, 0], pltpu.HBM)
            for array in (queries, key_vecs, value_vecs)
        ],
        [HBM_SPEC] * 3,
        [pltpu.SemaphoreType.DMA((3 * parts,))],
        moved=12 * rows * width_local,
    )
    there = [
        [
            (z * 2 + c, (parts * c + (z + j) % parts) * 2 + z // parts)
            for z in range(seq_count)
            for c in range(2)
        ]
        for j in range(parts)
    ]
    back = [[(b, a) for a, b in pairs] for pairs in there]
    kv_own = [lax.ppermute(packed[j], axes, there[j]) for j in range(parts)]
    q_own = [lax.ppermute(packed[parts + j], axes, there[j]) for j in range(parts)]
    near_w = lax.ppermute(w_out, ("shard", "guide"), crossed)
    far_w = lax.ppermute(w_out, ("shard", "guide"), straight)
    kv_other = [lax.ppermute(block, "guide", both) for block in kv_own]

    head_t = w_head.T
    rows_own = call(
        head_rows_kernel, [((channels, LANES), F32)], [norm_scale, norm_shift, head_t],
        moved=4 * width_shard * LANES,
    )[0]
    rows_got = lax.ppermute(rows_own, "shard", both)
    *q_own, rows_own = lax.optimization_barrier((*q_own, rows_own))

    mixed = call(
        functools.partial(attend_kernel, parts),
        [((rows, half), BF16)] * parts,
        q_own + kv_own + kv_other,
        flops=8 * rows * parts * rows * parts * half,
        moved=2 * rows * half * parts * 6,
    )
    *mixed, rows_got, near_w, far_w = lax.optimization_barrier((*mixed, rows_got, near_w, far_w))
    mixed = [lax.ppermute(mixed[j], axes, back[j]) for j in range(parts)]

    chunk = 128
    pieces = 2
    width_piece = width_shard // pieces
    got = []
    for i in range(pieces):
        partial = call(
            functools.partial(send_kernel, parts, half, chunk, i * width_piece),
            [((rows, width_piece), BF16)],
            mixed + [near_w, far_w],
            flops=2 * rows * width_local * width_piece,
            moved=2 * width_local * width_piece,
        )[0]
        got.append(lax.ppermute(partial, "shard", both))
    hidden = call(
        functools.partial(keep_kernel, parts, half, chunk),
        [((rows, width_shard), F32)],
        mixed + [near_w, far_w, residual[0, 0], attn_gate],
        flops=2 * rows * width_local * width_shard,
        moved=2 * width_local * width_shard,
    )[0]
    state = []
    for i in range(pieces):
        first, last = i == 0, i == pieces - 1
        state = call(
            functools.partial(head_kernel, first, last, chunk, i * width_piece),
            [((channels + SUBLANES, rows), F32)]
            if last
            else [((channels, rows), F32), ((rows, LANES), F32), ((rows, LANES), F32)],
            [hidden, got[i], attn_gate, norm_scale, head_t] + list(state),
            flops=4 * rows * channels * width_piece,
            moved=6 * rows * width_piece,
        )
    sums = state[0]
    sums_got = lax.ppermute(sums, "shard", both)
    keep, send = call(
        functools.partial(norm_kernel, width_model),
        [((channels // 2, rows), F32)] * 2,
        [sums, sums_got, rows_own, rows_got],
        scratch=[pltpu.VMEM((channels, rows), F32)],
    )
    eps_got = lax.ppermute(send, "guide", both)
    fold = LANES // group
    frames = call(
        functools.partial(frame_kernel, seq_count, group),
        [((channels // 2 // fold, LANES), F32)] * seq_count,
        [frame_owner, keep, eps_got],
        [SMEM_SPEC, VMEM_SPEC, VMEM_SPEC],
    )
    arrived = [frames[0]] + [
        lax.ppermute(frames[k], "seq", [(z, (z + k) % seq_count) for z in range(seq_count)])
        for k in range(1, seq_count)
    ]
    out = call(
        functools.partial(final_kernel, seq_count, group),
        [((channels // 2, rows), F32)],
        [timesteps, noise[0, 0].T] + arrived,
        [SMEM_SPEC] + [VMEM_SPEC] * (seq_count + 1),
    )[0]
    return out.T[None, None]


def fast_fits(sizes, queries, residual, w_out, w_head):
    seq_count = sizes["seq"]
    step_count, rows, width_local = queries.shape[1:]
    channels = w_head.shape[1]
    if sizes["guide"] != 2 or sizes["shard"] != 2 or seq_count % 2 or step_count != 1 or rows != LANES:
        return False
    if width_local % (seq_count // 2 * HEAD_DIM) or residual.shape[3] % (4 * LANES):
        return False
    if w_out.shape[1] != residual.shape[3] or channels % (2 * SUBLANES):
        return False
    group = rows // seq_count
    if rows % seq_count or LANES % group:
        return False
    fold = LANES // group
    return channels // 2 % (fold * SUBLANES) == 0


def solution(mesh):
    sizes = dict(mesh.shape)

    def on_device(queries, key_vecs, value_vecs, residual, w_out, attn_gate, norm_shift, norm_scale, w_head, *rest):
        fits = fast_fits(sizes, queries, residual, w_out, w_head)
        plan = fast_plan if fits else general_plan
        return plan(queries, key_vecs, value_vecs, residual, w_out, attn_gate, norm_shift, norm_scale, w_head, *rest)

    return jax.shard_map(
        on_device,
        mesh=mesh,
        in_specs=(
            P("guide", "group", "seq", "shard"),
            P("guide", "group", "seq", "shard"),
            P("guide", "group", "seq", "shard"),
            P("guide", "group", "seq", "shard"),
            P("shard", "guide"),
            P("group", "shard"),
            P("group", "shard"),
            P("group", "shard"),
            P("shard", None),
            P("group", "seq", None, "guide"),
            P("group"),
            P("group", None),
        ),
        out_specs=P("group", "seq", None, "guide"),
        check_vma=False,
    )
```

profile of v0, /device:TPU:0, one launch (start us, length us, event | category | flops | bytes accessed | tf_op | source)
XLA Modules:
  0.0 79.0 jit_solution(10659779071658372194)
XLA Ops:
  0.0 3.5 %collective-permute-start.7 = (bf16[1280,2560]{1,0:T(8,128)(2,1)}, bf16[1280,2560]{1,0:T(8,128)(2,1)S(1)}, u32[]{:S(2)}, u32[]{:S(2)}) collective-permute-start(bf16[1280,2560]{1,0:T(8,128)(2,1)} %param.16), channel_id=1, source_target_pairs={{0,0},{1,1},{2,3},{3,2},{4,4},{5,5},{6,7},{7,6},{8,8},{9,9},{10,11... | collective-permute-start | bytes 19660808 | tf_op jit(solution)/shard_map/ppermute | solution.py:349
  3.5 2.4 %collective-permute-start.8 = (bf16[1280,2560]{1,0:T(8,128)(2,1)}, bf16[1280,2560]{1,0:T(8,128)(2,1)S(1)}, u32[]{:S(2)}, u32[]{:S(2)}) collective-permute-start(bf16[1280,2560]{1,0:T(8,128)(2,1)} %param.16), channel_id=1, source_target_pairs={{0,1},{1,0},{2,2},{3,3},{4,5},{5,4},{6,6},{7,7},{8,9},{9,8},{10,10... | collective-permute-start | bytes 19660808 | tf_op jit(solution)/shard_map/ppermute | solution.py:350
  5.9 1.4 %shard_map.118 = (bf16[2,128,640]{2,1,0:T(8,128)(2,1)S(1)}, bf16[2,128,640]{2,1,0:T(8,128)(2,1)S(1)}, bf16[128,640]{1,0:T(8,128)(2,1)S(1)}, bf16[128,640]{1,0:T(8,128)(2,1)S(1)}) custom-call(bf16[128,1280]{1,0:T(8,128)(2,1)} %bitcast.16, bf16[128,1280]{1,0:T(8,128)(2,1)} %bitcast.17, bf16[128,1280]{1,0:T(8,128)(2,1)} %bitcast.18), custom_call_target="tpu_custom_call" | custom-call | bytes 1966080 | tf_op jit(solution)/shard_map/pallas_call | solution.py:298
  8.0 2.6 %collective-permute-start.3 = (bf16[2,128,640]{2,1,0:T(8,128)(2,1)S(1)}, bf16[2,128,640]{2,1,0:T(8,128)(2,1)S(1)}, u32[]{:S(2)}, u32[]{:S(2)}) collective-permute-start(bf16[2,128,640]{2,1,0:T(8,128)(2,1)S(1)} %get-tuple-element.33), channel_id=1, source_target_pairs={{0,4},{1,12},{4,0},{5,8},{8,5},{9,13},{12,1},{13,9},{2,6},{3,14},{... | collective-permute-start | bytes 983048 | tf_op jit(solution)/shard_map/ppermute | solution.py:347
  11.3 15.2 %collective-permute-start.4 = (bf16[2,128,640]{2,1,0:T(8,128)(2,1)S(1)}, bf16[2,128,640]{2,1,0:T(8,128)(2,1)S(1)}, u32[]{:S(2)}, u32[]{:S(2)}) collective-permute-start(bf16[2,128,640]{2,1,0:T(8,128)(2,1)S(1)} %collective-permute-done.2.refs_2_), channel_id=1, source_target_pairs={{0,1},{1,0},{2,3},{3,2},{4,5},{5,4},{6,7},{7,6},{8,9},{9,8},{10,11... | collective-permute-start | bytes 983048 | tf_op jit(solution)/shard_map/ppermute | solution.py:351
  26.5 4.2 %collective-permute-start.1 = (bf16[128,640]{1,0:T(8,128)(2,1)S(1)}, bf16[128,640]{1,0:T(8,128)(2,1)S(1)}, u32[]{:S(2)}, u32[]{:S(2)}) collective-permute-start(bf16[128,640]{1,0:T(8,128)(2,1)S(1)} %get-tuple-element.29), channel_id=1, source_target_pairs={{0,4},{1,12},{4,0},{5,8},{8,5},{9,13},{12,1},{13,9},{2,6},{3,14},{... | collective-permute-start | bytes 491528 | tf_op jit(solution)/shard_map/ppermute | solution.py:348
  30.7 1.0 %copy-done = bf16[2560,64]{0,1:T(8,128)(2,1)S(1)} copy-done((bf16[2560,64]{0,1:T(8,128)(2,1)S(1)}, bf16[2560,64]{0,1:T(8,128)(2,1)}, u32[]{:S(2)}) %copy-start) | copy-done | bytes 327704
  33.1 0.8 shard_map.119.rows_own_ref
  34.0 1.8 %collective-permute-start.6 = (f32[64,128]{1,0:T(8,128)S(1)}, f32[64,128]{1,0:T(8,128)S(1)}, u32[]{:S(2)}, u32[]{:S(2)}) collective-permute-start(f32[64,128]{1,0:T(8,128)S(1)} %shard_map.119.rows_own_ref), channel_id=1, source_target_pairs={{0,2},{2,0},{1,3},{3,1},{4,6},{6,4},{5,7},{7,5},{8,10},{10,8},{9,1... | collective-permute-start | bytes 98312 | tf_op jit(solution)/shard_map/ppermute | solution.py:358
  35.7 1.7 %shard_map.120 = (bf16[128,640]{1,0:T(8,128)(2,1)S(1)}, bf16[128,640]{1,0:T(8,128)(2,1)S(1)}) custom-call(bf16[128,640]{1,0:T(8,128)(2,1)S(1)} %collective-permute-done.refs_0_, bf16[128,640]{1,0:T(8,128)(2,1)S(1)} %collective-permute-done.1.refs_1_, bf16[2,128,640]{2,1,0:T(8,128)(2,1)S(1)} %collective-permute-done.2.refs_2_, ...), custom_call_target="tpu_custom_call" | custom-call | flops 335544320 | bytes 1966080 | tf_op jit(solution)/shard_map/pallas_call | solution.py:298
  37.9 2.1 %collective-permute-start.10 = (bf16[128,640]{1,0:T(8,128)(2,1)S(1)}, bf16[128,640]{1,0:T(8,128)(2,1)S(1)}, u32[]{:S(2)}, u32[]{:S(2)}) collective-permute-start(bf16[128,640]{1,0:T(8,128)(2,1)S(1)} %get-tuple-element.37), channel_id=1, source_target_pairs={{4,0},{12,1},{0,4},{8,5},{5,8},{13,9},{1,12},{9,13},{6,2},{14,3},{... | collective-permute-start | bytes 491528 | tf_op jit(solution)/shard_map/ppermute | solution.py:369
  40.6 2.6 %collective-permute-done.10.refs_1_ = bf16[128,640]{1,0:T(8,128)(2,1)S(1)} collective-permute-done((bf16[128,640]{1,0:T(8,128)(2,1)S(1)}, bf16[128,640]{1,0:T(8,128)(2,1)S(1)}, u32[]{:S(2)}, u32[]{:S(2)}) %collective-permute-start.10) | collective-permute-done | bytes 163872 | tf_op jit(solution)/shard_map/ppermute | solution.py:369
  43.3 1.1 %shard_map.123 = bf16[128,1280]{1,0:T(8,128)(2,1)S(1)} custom-call(bf16[128,640]{1,0:T(8,128)(2,1)S(1)} %collective-permute-done.9.refs_0_, bf16[128,640]{1,0:T(8,128)(2,1)S(1)} %collective-permute-done.10.refs_1_, bf16[1280,2560]{1,0:T(8,128)(2,1)S(1)} %collective-permute-done.7.refs_2_, bf16[1280,2560]{1,0:T(8,128)(2,1)S(1)} %collective-permute-done.8.refs_3_), custom_call_target="tpu_custom_call" | custom-call | flops 419430400 | bytes 3276800 | tf_op jit(solution)/shard_map/pallas_call | solution.py:298
  44.4 2.1 %collective-permute-start.12 = (bf16[128,1280]{1,0:T(8,128)(2,1)S(1)}, bf16[128,1280]{1,0:T(8,128)(2,1)S(1)}, u32[]{:S(2)}, u32[]{:S(2)}) collective-permute-start(bf16[128,1280]{1,0:T(8,128)(2,1)S(1)} %shard_map.123), channel_id=1, source_target_pairs={{0,2},{2,0},{1,3},{3,1},{4,6},{6,4},{5,7},{7,5},{8,10},{10,8},{9,1... | collective-permute-start | bytes 983048 | tf_op jit(solution)/shard_map/ppermute | solution.py:383
  46.5 1.1 %shard_map.122 = bf16[128,1280]{1,0:T(8,128)(2,1)S(1)} custom-call(bf16[128,640]{1,0:T(8,128)(2,1)S(1)} %collective-permute-done.9.refs_0_, bf16[128,640]{1,0:T(8,128)(2,1)S(1)} %collective-permute-done.10.refs_1_, bf16[1280,2560]{1,0:T(8,128)(2,1)S(1)} %collective-permute-done.7.refs_2_, bf16[1280,2560]{1,0:T(8,128)(2,1)S(1)} %collective-permute-done.8.refs_3_), custom_call_target="tpu_custom_call" | custom-call | flops 419430400 | bytes 3276800 | tf_op jit(solution)/shard_map/pallas_call | solution.py:298
  47.7 2.2 %shard_map.121.refs_0_ = f32[128,2560]{1,0:T(8,128)S(1)} custom-call(bf16[128,640]{1,0:T(8,128)(2,1)S(1)} %collective-permute-done.9.refs_0_, bf16[128,640]{1,0:T(8,128)(2,1)S(1)} %collective-permute-done.10.refs_1_, bf16[1280,2560]{1,0:T(8,128)(2,1)S(1)} %collective-permute-done.7.refs_2_, bf16[1280,2560]{1,0:T(8,128)(2,1)S(1)} %collective-permute-done.8.refs_3_, ...), custom_call_target="tpu_custom_call" | custom-call | flops 838860800 | bytes 6553600 | tf_op jit(solution)/shard_map/pallas_call | solution.py:298
  49.9 1.6 %collective-permute-done.12.refs_1_ = bf16[128,1280]{1,0:T(8,128)(2,1)S(1)} collective-permute-done((bf16[128,1280]{1,0:T(8,128)(2,1)S(1)}, bf16[128,1280]{1,0:T(8,128)(2,1)S(1)}, u32[]{:S(2)}, u32[]{:S(2)}) %collective-permute-start.12) | collective-permute-done | bytes 327712 | tf_op jit(solution)/shard_map/ppermute | solution.py:383
  52.1 2.9 %collective-permute-done.11.refs_1_ = bf16[128,1280]{1,0:T(8,128)(2,1)S(1)} collective-permute-done((bf16[128,1280]{1,0:T(8,128)(2,1)S(1)}, bf16[128,1280]{1,0:T(8,128)(2,1)S(1)}, u32[]{:S(2)}, u32[]{:S(2)}) %collective-permute-start.11) | collective-permute-done | bytes 327712 | tf_op jit(solution)/shard_map/ppermute | solution.py:383
  55.6 2.1 %collective-permute-start.13 = (f32[72,128]{1,0:T(8,128)S(1)}, f32[72,128]{1,0:T(8,128)S(1)}, u32[]{:S(2)}, u32[]{:S(2)}) collective-permute-start(f32[72,128]{1,0:T(8,128)S(1)} %shard_map.125.own_ref), channel_id=1, source_target_pairs={{0,2},{2,0},{1,3},{3,1},{4,6},{6,4},{5,7},{7,5},{8,10},{10,8},{9,1... | collective-permute-start | bytes 110600 | tf_op jit(solution)/shard_map/ppermute | solution.py:404
  57.7 2.3 %collective-permute-done.13.got_ref = f32[72,128]{1,0:T(8,128)S(1)} collective-permute-done((f32[72,128]{1,0:T(8,128)S(1)}, f32[72,128]{1,0:T(8,128)S(1)}, u32[]{:S(2)}, u32[]{:S(2)}) %collective-permute-start.13) | collective-permute-done | bytes 36896 | tf_op jit(solution)/shard_map/ppermute | solution.py:404
  60.1 7.8 %collective-permute-start.14 = (f32[32,128]{1,0:T(8,128)S(1)}, f32[32,128]{1,0:T(8,128)S(1)}, u32[]{:S(2)}, u32[]{:S(2)}) collective-permute-start(f32[32,128]{1,0:T(8,128)S(1)} %get-tuple-element.46), channel_id=1, source_target_pairs={{0,1},{1,0},{2,3},{3,2},{4,5},{5,4},{6,7},{7,6},{8,9},{9,8},{10,11... | collective-permute-start | bytes 49160 | tf_op jit(solution)/shard_map/ppermute | solution.py:411
  67.9 0.8 %collective-permute-done.14.got_ref = f32[32,128]{1,0:T(8,128)S(1)} collective-permute-done((f32[32,128]{1,0:T(8,128)S(1)}, f32[32,128]{1,0:T(8,128)S(1)}, u32[]{:S(2)}, u32[]{:S(2)}) %collective-permute-start.14) | collective-permute-done | bytes 16416 | tf_op jit(solution)/shard_map/ppermute | solution.py:411
  69.7 4.9 %collective-permute-start.16 = (f32[8,128]{1,0:T(8,128)S(1)}, f32[8,128]{1,0:T(8,128)S(1)}, u32[]{:S(2)}, u32[]{:S(2)}) collective-permute-start(f32[8,128]{1,0:T(8,128)S(1)} %get-tuple-element.49), channel_id=1, source_target_pairs={{0,8},{4,12},{8,0},{12,4},{1,9},{5,13},{9,1},{13,5},{2,10},{6,14},... | collective-permute-start | bytes 12296 | tf_op jit(solution)/shard_map/ppermute | solution.py:420
  76.2 2.0 %collective-permute-done.17.refs_3_ = f32[8,128]{1,0:T(8,128)S(1)} collective-permute-done((f32[8,128]{1,0:T(8,128)S(1)}, f32[8,128]{1,0:T(8,128)S(1)}, u32[]{:S(2)}, u32[]{:S(2)}) %collective-permute-start.17) | collective-permute-done | bytes 4128 | tf_op jit(solution)/shard_map/ppermute | solution.py:420
  (39 shorter events, 8.0 us)
Async XLA Ops:
  0.0 37.9 %collective-permute-start.7 = (bf16[1280,2560]{1,0:T(8,128)(2,1)}, bf16[1280,2560]{1,0:T(8,128)(2,1)S(1)}, u32[]{:S(2)}, u32[]{:S(2)}) collective-permute-start(bf16[1280,2560]{1,0:T(8,128)(2,1)} %param.16), channel_id=1, source_target_pairs={{0,0},{1,1},{2,3},{3,2},{4,4},{5,5},{6,7},{7,6},{8,8},{9,9},{10,11... | collective-permute-start | bytes 19660808 | tf_op jit(solution)/shard_map/ppermute | solution.py:349
  3.5 34.4 %collective-permute-start.8 = (bf16[1280,2560]{1,0:T(8,128)(2,1)}, bf16[1280,2560]{1,0:T(8,128)(2,1)S(1)}, u32[]{:S(2)}, u32[]{:S(2)}) collective-permute-start(bf16[1280,2560]{1,0:T(8,128)(2,1)} %param.16), channel_id=1, source_target_pairs={{0,1},{1,0},{2,2},{3,3},{4,5},{5,4},{6,6},{7,7},{8,9},{9,8},{10,10... | collective-permute-start | bytes 19660808 | tf_op jit(solution)/shard_map/ppermute | solution.py:350
  7.3 4.0 %collective-permute-start.2 = (bf16[2,128,640]{2,1,0:T(8,128)(2,1)S(1)}, bf16[2,128,640]{2,1,0:T(8,128)(2,1)S(1)}, u32[]{:S(2)}, u32[]{:S(2)}) collective-permute-start(bf16[2,128,640]{2,1,0:T(8,128)(2,1)S(1)} %get-tuple-element.32), channel_id=1, source_target_pairs={{0,0},{1,8},{4,4},{5,12},{8,1},{9,9},{12,5},{13,13},{2,2},{3,10},{... | collective-permute-start | bytes 983048 | tf_op jit(solution)/shard_map/ppermute | solution.py:347
  8.0 18.5 %collective-permute-start.3 = (bf16[2,128,640]{2,1,0:T(8,128)(2,1)S(1)}, bf16[2,128,640]{2,1,0:T(8,128)(2,1)S(1)}, u32[]{:S(2)}, u32[]{:S(2)}) collective-permute-start(bf16[2,128,640]{2,1,0:T(8,128)(2,1)S(1)} %get-tuple-element.33), channel_id=1, source_target_pairs={{0,4},{1,12},{4,0},{5,8},{8,5},{9,13},{12,1},{13,9},{2,6},{3,14},{... | collective-permute-start | bytes 983048 | tf_op jit(solution)/shard_map/ppermute | solution.py:347
  10.6 15.9 %collective-permute-start = (bf16[128,640]{1,0:T(8,128)(2,1)S(1)}, bf16[128,640]{1,0:T(8,128)(2,1)S(1)}, u32[]{:S(2)}, u32[]{:S(2)}) collective-permute-start(bf16[128,640]{1,0:T(8,128)(2,1)S(1)} %get-tuple-element.28), channel_id=1, source_target_pairs={{0,0},{1,8},{4,4},{5,12},{8,1},{9,9},{12,5},{13,13},{2,2},{3,10},{... | collective-permute-start | bytes 491528 | tf_op jit(solution)/shard_map/ppermute | solution.py:348
  11.3 24.5 %collective-permute-start.4 = (bf16[2,128,640]{2,1,0:T(8,128)(2,1)S(1)}, bf16[2,128,640]{2,1,0:T(8,128)(2,1)S(1)}, u32[]{:S(2)}, u32[]{:S(2)}) collective-permute-start(bf16[2,128,640]{2,1,0:T(8,128)(2,1)S(1)} %collective-permute-done.2.refs_2_), channel_id=1, source_target_pairs={{0,1},{1,0},{2,3},{3,2},{4,5},{5,4},{6,7},{7,6},{8,9},{9,8},{10,11... | collective-permute-start | bytes 983048 | tf_op jit(solution)/shard_map/ppermute | solution.py:351
  26.5 9.3 %collective-permute-start.5 = (bf16[2,128,640]{2,1,0:T(8,128)(2,1)S(1)}, bf16[2,128,640]{2,1,0:T(8,128)(2,1)S(1)}, u32[]{:S(2)}, u32[]{:S(2)}) collective-permute-start(bf16[2,128,640]{2,1,0:T(8,128)(2,1)S(1)} %collective-permute-done.3.refs_3_), channel_id=1, source_target_pairs={{0,1},{1,0},{2,3},{3,2},{4,5},{5,4},{6,7},{7,6},{8,9},{9,8},{10,11... | collective-permute-start | bytes 983048 | tf_op jit(solution)/shard_map/ppermute | solution.py:351
  26.5 7.5 %collective-permute-start.1 = (bf16[128,640]{1,0:T(8,128)(2,1)S(1)}, bf16[128,640]{1,0:T(8,128)(2,1)S(1)}, u32[]{:S(2)}, u32[]{:S(2)}) collective-permute-start(bf16[128,640]{1,0:T(8,128)(2,1)S(1)} %get-tuple-element.29), channel_id=1, source_target_pairs={{0,4},{1,12},{4,0},{5,8},{8,5},{9,13},{12,1},{13,9},{2,6},{3,14},{... | collective-permute-start | bytes 491528 | tf_op jit(solution)/shard_map/ppermute | solution.py:348
  30.7 1.0 %copy-start = (bf16[2560,64]{0,1:T(8,128)(2,1)S(1)}, bf16[2560,64]{0,1:T(8,128)(2,1)}, u32[]{:S(2)}) copy-start(bf16[2560,64]{0,1:T(8,128)(2,1)} %param.20) | copy-start | bytes 983044
  34.0 3.9 %collective-permute-start.6 = (f32[64,128]{1,0:T(8,128)S(1)}, f32[64,128]{1,0:T(8,128)S(1)}, u32[]{:S(2)}, u32[]{:S(2)}) collective-permute-start(f32[64,128]{1,0:T(8,128)S(1)} %shard_map.119.rows_own_ref), channel_id=1, source_target_pairs={{0,2},{2,0},{1,3},{3,1},{4,6},{6,4},{5,7},{7,5},{8,10},{10,8},{9,1... | collective-permute-start | bytes 98312 | tf_op jit(solution)/shard_map/ppermute | solution.py:358
  37.9 5.4 %collective-permute-start.10 = (bf16[128,640]{1,0:T(8,128)(2,1)S(1)}, bf16[128,640]{1,0:T(8,128)(2,1)S(1)}, u32[]{:S(2)}, u32[]{:S(2)}) collective-permute-start(bf16[128,640]{1,0:T(8,128)(2,1)S(1)} %get-tuple-element.37), channel_id=1, source_target_pairs={{4,0},{12,1},{0,4},{8,5},{5,8},{13,9},{1,12},{9,13},{6,2},{14,3},{... | collective-permute-start | bytes 491528 | tf_op jit(solution)/shard_map/ppermute | solution.py:369
  40.0 3.3 %collective-permute-start.9 = (bf16[128,640]{1,0:T(8,128)(2,1)S(1)}, bf16[128,640]{1,0:T(8,128)(2,1)S(1)}, u32[]{:S(2)}, u32[]{:S(2)}) collective-permute-start(bf16[128,640]{1,0:T(8,128)(2,1)S(1)} %get-tuple-element.36), channel_id=1, source_target_pairs={{0,0},{8,1},{4,4},{12,5},{1,8},{9,9},{5,12},{13,13},{2,2},{10,3},{... | collective-permute-start | bytes 491528 | tf_op jit(solution)/shard_map/ppermute | solution.py:369
  44.4 3.3 %copy-start.2 = (bf16[1,1,128,2560]{3,2,1,0:T(8,128)(2,1)S(1)}, bf16[1,1,128,2560]{3,2,1,0:T(8,128)(2,1)}, u32[]{:S(2)}) copy-start(bf16[1,1,128,2560]{3,2,1,0:T(8,128)(2,1)} %param.15) | copy-start | bytes 1966084
  44.4 3.3 %copy-start.3 = (f32[1,2560]{1,0:T(1,128)S(1)}, f32[1,2560]{1,0:T(1,128)}, u32[]{:S(2)}) copy-start(f32[1,2560]{1,0:T(1,128)} %refs_2_.3) | copy-start | bytes 30724
  44.4 7.1 %collective-permute-start.12 = (bf16[128,1280]{1,0:T(8,128)(2,1)S(1)}, bf16[128,1280]{1,0:T(8,128)(2,1)S(1)}, u32[]{:S(2)}, u32[]{:S(2)}) collective-permute-start(bf16[128,1280]{1,0:T(8,128)(2,1)S(1)} %shard_map.123), channel_id=1, source_target_pairs={{0,2},{2,0},{1,3},{3,1},{4,6},{6,4},{5,7},{7,5},{8,10},{10,8},{9,1... | collective-permute-start | bytes 983048 | tf_op jit(solution)/shard_map/ppermute | solution.py:383
  47.6 7.5 %collective-permute-start.11 = (bf16[128,1280]{1,0:T(8,128)(2,1)S(1)}, bf16[128,1280]{1,0:T(8,128)(2,1)S(1)}, u32[]{:S(2)}, u32[]{:S(2)}) collective-permute-start(bf16[128,1280]{1,0:T(8,128)(2,1)S(1)} %shard_map.122), channel_id=1, source_target_pairs={{0,2},{2,0},{1,3},{3,1},{4,6},{6,4},{5,7},{7,5},{8,10},{10,8},{9,1... | collective-permute-start | bytes 983048 | tf_op jit(solution)/shard_map/ppermute | solution.py:383
  47.7 3.8 %copy-start.1 = (bf16[2560,64]{0,1:T(8,128)(2,1)S(1)}, bf16[2560,64]{0,1:T(8,128)(2,1)}, u32[]{:S(2)}) copy-start(bf16[2560,64]{0,1:T(8,128)(2,1)} %param.20) | copy-start | bytes 983044
  47.7 21.0 %copy-start.7 = (s32[1,4]{1,0:T(1,128)S(1)}, s32[1,4]{1,0:T(1,128)}, u32[]{:S(2)}) copy-start(s32[1,4]{1,0:T(1,128)} %owner_ref.1) | copy-start | bytes 52
  47.7 30.5 %copy-start.5 = (f32[1,1,128,32]{2,3,1,0:T(8,128)S(1)}, f32[1,1,128,32]{2,3,1,0:T(8,128)}, u32[]{:S(2)}) copy-start(f32[1,1,128,32]{2,3,1,0:T(8,128)} %param.21) | copy-start | bytes 49156
  55.6 4.4 %collective-permute-start.13 = (f32[72,128]{1,0:T(8,128)S(1)}, f32[72,128]{1,0:T(8,128)S(1)}, u32[]{:S(2)}, u32[]{:S(2)}) collective-permute-start(f32[72,128]{1,0:T(8,128)S(1)} %shard_map.125.own_ref), channel_id=1, source_target_pairs={{0,2},{2,0},{1,3},{3,1},{4,6},{6,4},{5,7},{7,5},{8,10},{10,8},{9,1... | collective-permute-start | bytes 110600 | tf_op jit(solution)/shard_map/ppermute | solution.py:404
  60.1 8.6 %collective-permute-start.14 = (f32[32,128]{1,0:T(8,128)S(1)}, f32[32,128]{1,0:T(8,128)S(1)}, u32[]{:S(2)}, u32[]{:S(2)}) collective-permute-start(f32[32,128]{1,0:T(8,128)S(1)} %get-tuple-element.46), channel_id=1, source_target_pairs={{0,1},{1,0},{2,3},{3,2},{4,5},{5,4},{6,7},{7,6},{8,9},{9,8},{10,11... | collective-permute-start | bytes 49160 | tf_op jit(solution)/shard_map/ppermute | solution.py:411
  69.4 6.3 %collective-permute-start.15 = (f32[8,128]{1,0:T(8,128)S(1)}, f32[8,128]{1,0:T(8,128)S(1)}, u32[]{:S(2)}, u32[]{:S(2)}) collective-permute-start(f32[8,128]{1,0:T(8,128)S(1)} %get-tuple-element.48), channel_id=1, source_target_pairs={{0,4},{4,8},{8,12},{12,0},{1,5},{5,9},{9,13},{13,1},{2,6},{6,10},{... | collective-permute-start | bytes 12296 | tf_op jit(solution)/shard_map/ppermute | solution.py:420
  69.7 6.5 %collective-permute-start.16 = (f32[8,128]{1,0:T(8,128)S(1)}, f32[8,128]{1,0:T(8,128)S(1)}, u32[]{:S(2)}, u32[]{:S(2)}) collective-permute-start(f32[8,128]{1,0:T(8,128)S(1)} %get-tuple-element.49), channel_id=1, source_target_pairs={{0,8},{4,12},{8,0},{12,4},{1,9},{5,13},{9,1},{13,5},{2,10},{6,14},... | collective-permute-start | bytes 12296 | tf_op jit(solution)/shard_map/ppermute | solution.py:420
  74.7 3.6 %collective-permute-start.17 = (f32[8,128]{1,0:T(8,128)S(1)}, f32[8,128]{1,0:T(8,128)S(1)}, u32[]{:S(2)}, u32[]{:S(2)}) collective-permute-start(f32[8,128]{1,0:T(8,128)S(1)} %get-tuple-element.50), channel_id=1, source_target_pairs={{0,12},{4,0},{8,4},{12,8},{1,13},{5,1},{9,5},{13,9},{2,14},{6,2},{... | collective-permute-start | bytes 12296 | tf_op jit(solution)/shard_map/ppermute | solution.py:420
  (2 other events, 1.4 us)
where the time goes:
time: 79.4 us; the launch traced here: 79 us
  starting transfers between devices  51.3 us (65%)
  waiting for transfers between devices  13.7 us (17%)
  Pallas kernels  10.8 us (14%)
  local copies, waits for them, and re-layouts  2.4 us (3%)
  between operations  0.8 us (1%)
    ppermute x2, starting transfers between devices, fast_plan(): kv_other = [lax.ppermute(block, 'guide', both) for block in kv_own]  15.2 us
    pallas_call x11, Pallas kernels, call(): pl.pallas_call(kernel, out_shape=shapes, in_specs=specs or [VMEM_SPEC] *...  10.8 us
    ppermute x1, starting transfers between devices, fast_plan(): eps_got = lax.ppermute(send, 'guide', both)  7.76 us
    ppermute x3, starting transfers between devices, fast_plan(): lax.ppermute(frames[k], 'seq', [(z, (z + k) % seq_count) for z in range(s...  5.52 us
    ppermute x2, starting transfers between devices, fast_plan(): lax.ppermute(packed[parts + j], axes, there[j])  4.89 us
    ppermute x2, waiting for transfers between devices, fast_plan(): got.append(lax.ppermute(partial, 'shard', both))  4.58 us
    ppermute x1, starting transfers between devices, fast_plan(): near_w = lax.ppermute(w_out, ('shard', 'guide'), crossed)  3.51 us
    ppermute x2, starting transfers between devices, fast_plan(): kv_own = [lax.ppermute(packed[j], axes, there[j]) for j in range(parts)]  3.32 us
  transfers between devices with their start and end apart: 18, of which 10 were waited for; matrix products, arithmetic and copies ran while one was open for 0% of the time, Pallas kernels for 10%

commit v1 on v0

--- a/solution.py
+++ b/solution.py
@@ -120,14 +120,16 @@
         copy.wait()
 
 
-def attend_kernel(parts, *refs):
-    q_refs = refs[:parts]
-    kv_refs = refs[parts : 3 * parts]
-    o_refs = refs[3 * parts :]
-    rows = q_refs[0].shape[0]
-    for i in range(q_refs[0].shape[1] // HEAD_DIM):
+def is_near(parts):
+    return lax.axis_index("seq") // parts == lax.axis_index("guide")
+
+
+def attend_kernel(parts, near_ref, far_ref, *refs):
+    kv_refs, out_ref = refs[: 2 * parts], refs[2 * parts]
+    near = is_near(parts)
+    for i in range(near_ref.shape[1] // HEAD_DIM):
         cols = slice(i * HEAD_DIM, (i + 1) * HEAD_DIM)
-        q = jnp.concatenate([r[:, cols] for r in q_refs], axis=0)
+        q = jnp.where(near, near_ref[:, cols], far_ref[:, cols])
         k = jnp.concatenate([r[0, :, cols] for r in kv_refs], axis=0)
         v = jnp.concatenate([r[1, :, cols] for r in kv_refs], axis=0)
         scores = lax.dot_general(q, k, (((1,), (1,)), ((), ())), preferred_element_type=F32)
@@ -135,23 +137,27 @@
         expo = jnp.exp2(scores - jnp.max(scores, axis=1, keepdims=True))
         total = jnp.sum(expo, axis=1, keepdims=True)
         mixed = jnp.dot(expo.astype(BF16), v, preferred_element_type=F32) / total
-        for j in range(parts):
-            o_refs[j][:, cols] = mixed[j * rows : (j + 1) * rows].astype(BF16)
-
-
-def project(parts, half, o_refs, w_ref, cols):
+        out_ref[:, cols] = mixed.astype(BF16)
+
+
+def attended_rows(parts, o_refs):
+    near = is_near(parts)
+    return [jnp.where(near, o_refs[j][...], o_refs[parts + j][...]) for j in range(parts)]
+
+
+def project(parts, half, attended, w_ref, cols):
     z = lax.axis_index("seq")
     total = None
     for j in range(parts):
         start = pl.multiple_of(lax.rem(z + j, parts) * half, LANES)
-        term = jnp.dot(o_refs[j][...], w_ref[pl.ds(start, half), cols], preferred_element_type=F32)
+        term = jnp.dot(attended[j], w_ref[pl.ds(start, half), cols], preferred_element_type=F32)
         total = term if total is None else total + term
     return total
 
 
 def send_kernel(parts, half, chunk, first, *refs):
-    o_refs = refs[:parts]
-    near_ref, far_ref, out_ref = refs[parts:]
+    near_ref, far_ref, out_ref = refs[2 * parts :]
+    attended = attended_rows(parts, refs[: 2 * parts])
     guide = lax.axis_index("guide")
     for value, w_ref in ((1, near_ref), (0, far_ref)):
 
@@ -159,12 +165,12 @@
         def _():
             for t in range(out_ref.shape[1] // chunk):
                 cols = slice(first + t * chunk, first + (t + 1) * chunk)
-                out_ref[:, t * chunk : (t + 1) * chunk] = project(parts, half, o_refs, w_ref, cols).astype(BF16)
+                out_ref[:, t * chunk : (t + 1) * chunk] = project(parts, half, attended, w_ref, cols).astype(BF16)
 
 
 def keep_kernel(parts, half, chunk, *refs):
-    o_refs = refs[:parts]
-    near_ref, far_ref, res_ref, gate_ref, out_ref = refs[parts:]
+    near_ref, far_ref, res_ref, gate_ref, out_ref = refs[2 * parts :]
+    attended = attended_rows(parts, refs[: 2 * parts])
     guide = lax.axis_index("guide")
     for value, w_ref in ((0, near_ref), (1, far_ref)):
 
@@ -173,7 +179,7 @@
             for t in range(out_ref.shape[1] // chunk):
                 cols = slice(t * chunk, (t + 1) * chunk)
                 out_ref[:, cols] = res_ref[:, cols].astype(F32) + gate_ref[:, cols] * project(
-                    parts, half, o_refs, w_ref, cols
+                    parts, half, attended, w_ref, cols
                 )
 
 
@@ -343,12 +349,17 @@
         ]
         for j in range(parts)
     ]
-    back = [[(b, a) for a, b in pairs] for pairs in there]
-    kv_own = [lax.ppermute(packed[j], axes, there[j]) for j in range(parts)]
-    q_own = [lax.ppermute(packed[parts + j], axes, there[j]) for j in range(parts)]
+    close = [[(a, b) for a, b in pairs if a // 2 // parts == a % 2] for pairs in there]
+    apart = [[(a, b) for a, b in pairs if a // 2 // parts != a % 2] for pairs in there]
+    q_near, q_far, kv_own, kv_other = [packed[parts]], [], [], []
+    for j in range(1, parts):
+        q_near.append(lax.ppermute(packed[parts + j], axes, close[j]))
     near_w = lax.ppermute(w_out, ("shard", "guide"), crossed)
     far_w = lax.ppermute(w_out, ("shard", "guide"), straight)
-    kv_other = [lax.ppermute(block, "guide", both) for block in kv_own]
+    for j in range(parts):
+        kv_own.append(lax.ppermute(packed[j], axes, there[j]))
+        kv_other.append(lax.ppermute(kv_own[j], "guide", both))
+        q_far.append(lax.ppermute(packed[parts + j], axes, apart[j]))
 
     head_t = w_head.T
     rows_own = call(
@@ -356,17 +367,20 @@
         moved=4 * width_shard * LANES,
     )[0]
     rows_got = lax.ppermute(rows_own, "shard", both)
-    *q_own, rows_own = lax.optimization_barrier((*q_own, rows_own))
-
-    mixed = call(
-        functools.partial(attend_kernel, parts),
-        [((rows, half), BF16)] * parts,
-        q_own + kv_own + kv_other,
-        flops=8 * rows * parts * rows * parts * half,
-        moved=2 * rows * half * parts * 6,
-    )
-    *mixed, rows_got, near_w, far_w = lax.optimization_barrier((*mixed, rows_got, near_w, far_w))
-    mixed = [lax.ppermute(mixed[j], axes, back[j]) for j in range(parts)]
+    q_near[0], rows_own = lax.optimization_barrier((q_near[0], rows_own))
+
+    o_near, o_far = [], []
+    for j in range(parts):
+        block = call(
+            functools.partial(attend_kernel, parts),
+            [((rows, half), BF16)],
+            [q_near[j], q_far[j]] + kv_own + kv_other,
+            flops=8 * rows * rows * parts * half,
+            moved=2 * rows * half * parts * 5,
+        )[0]
+        o_far.append(lax.ppermute(block, axes, [(b, a) for a, b in apart[j]]))
+        o_near.append(block if j == 0 else lax.ppermute(block, axes, [(b, a) for a, b in close[j]]))
+    mixed = o_near + o_far
 
     chunk = 128
     pieces = 2

time: 79.4 us -> 87.4 us (1.10)
  waiting for transfers between devices: 13.7 us -> 17.3 us
  starting transfers between devices: 51.3 us -> 54.2 us
  Pallas kernels: 10.8 us -> 12.1 us
    ppermute x1, waiting for transfers between devices: 0.48 us -> 4.19 us  [fast_plan(): rows_got = lax.ppermute(rows_own, 'shard', both)]
    ppermute x8 -> x10, waiting for transfers between devices: 2.77 us -> 5.57 us  [the longest x1 5.55 us: fast_plan(): lax.ppermute(block, axes, [(b, a) for a, b in close[j]])]
    ppermute x8 -> x10, starting transfers between devices: 26.1 us -> 28.6 us  [the longest x2 14.1 us: fast_plan(): kv_other.append(lax.ppermute(kv_own[j], 'guide', both))]
    ppermute x1, waiting for transfers between devices: 2.34 us -> 0.01 us  [fast_plan(): sums_got = lax.ppermute(sums, 'shard', both)]
    ppermute x1, starting transfers between devices: 1.75 us -> 0.08 us  [fast_plan(): rows_got = lax.ppermute(rows_own, 'shard', both)]
    ppermute x1, starting transfers between devices: 7.76 us -> 9.41 us  [fast_plan(): eps_got = lax.ppermute(send, 'guide', both)]
    pallas_call x11 -> x12, Pallas kernels: 10.8 us -> 12.1 us  [call(): pl.pallas_call(kernel, out_shape=shapes, in_specs=specs or [VMEM_SPEC] *...]
    unnamed x16 -> x18, local copies, waits for them, and re-layouts: 2.4 us -> 2.41 us
  transfers between devices with their start and end apart: 18 -> 20, of which waited for: 10 -> 7; matrix products, arithmetic and copies ran while one was open for 0% -> 0% of each run, Pallas kernels for 10% -> 10%
where the time goes in v1:
time: 87.4 us; the launch traced here: 86.9 us
  starting transfers between devices  54.2 us (62%)
  waiting for transfers between devices  17.3 us (20%)
  Pallas kernels  12.1 us (14%)
  local copies, waits for them, and re-layouts  2.41 us (3%)
  between operations  0.92 us (1%)
    ppermute x2, starting transfers between devices, fast_plan(): kv_other.append(lax.ppermute(kv_own[j], 'guide', both))  14.1 us
    pallas_call x12, Pallas kernels, call(): pl.pallas_call(kernel, out_shape=shapes, in_specs=specs or [VMEM_SPEC] *...  12.1 us
    ppermute x1, starting transfers between devices, fast_plan(): eps_got = lax.ppermute(send, 'guide', both)  9.41 us
    ppermute x1, starting transfers between devices, fast_plan(): q_near.append(lax.ppermute(packed[parts + j], axes, close[j]))  6.14 us
    ppermute x3, starting transfers between devices, fast_plan(): lax.ppermute(frames[k], 'seq', [(z, (z + k) % seq_count) for z in range(s...  5.92 us
    ppermute x1, waiting for transfers between devices, fast_plan(): lax.ppermute(block, axes, [(b, a) for a, b in close[j]])  5.55 us
    ppermute x2, waiting for transfers between devices, fast_plan(): got.append(lax.ppermute(partial, 'shard', both))  4.49 us
    ppermute x1, waiting for transfers between devices, fast_plan(): rows_got = lax.ppermute(rows_own, 'shard', both)  4.19 us
  transfers between devices with their start and end apart: 20, of which 7 were waited for; matrix products, arithmetic and copies ran while one was open for 0% of the time, Pallas kernels for 10%

profile of v1, /device:TPU:0, one launch (start us, length us, event | category | flops | bytes accessed | tf_op | source)
XLA Modules:
  0.0 86.9 jit_solution(5382096694972564666)
XLA Ops:
  0.0 3.5 %collective-permute-start.10 = (bf16[1280,2560]{1,0:T(8,128)(2,1)}, bf16[1280,2560]{1,0:T(8,128)(2,1)S(1)}, u32[]{:S(2)}, u32[]{:S(2)}) collective-permute-start(bf16[1280,2560]{1,0:T(8,128)(2,1)} %param.16), channel_id=1, source_target_pairs={{0,0},{1,1},{2,3},{3,2},{4,4},{5,5},{6,7},{7,6},{8,8},{9,9},{10,11... | collective-permute-start | bytes 19660808 | tf_op jit(solution)/shard_map/ppermute | solution.py:357
  3.5 2.4 %collective-permute-start.11 = (bf16[1280,2560]{1,0:T(8,128)(2,1)}, bf16[1280,2560]{1,0:T(8,128)(2,1)S(1)}, u32[]{:S(2)}, u32[]{:S(2)}) collective-permute-start(bf16[1280,2560]{1,0:T(8,128)(2,1)} %param.16), channel_id=1, source_target_pairs={{0,1},{1,0},{2,2},{3,3},{4,5},{5,4},{6,6},{7,7},{8,9},{9,8},{10,10... | collective-permute-start | bytes 19660808 | tf_op jit(solution)/shard_map/ppermute | solution.py:358
  5.9 1.4 %shard_map.118 = (bf16[2,128,640]{2,1,0:T(8,128)(2,1)S(1)}, bf16[2,128,640]{2,1,0:T(8,128)(2,1)S(1)}, bf16[128,640]{1,0:T(8,128)(2,1)S(1)}, bf16[128,640]{1,0:T(8,128)(2,1)S(1)}) custom-call(bf16[128,1280]{1,0:T(8,128)(2,1)} %bitcast.16, bf16[128,1280]{1,0:T(8,128)(2,1)} %bitcast.17, bf16[128,1280]{1,0:T(8,128)(2,1)} %bitcast.18), custom_call_target="tpu_custom_call" | custom-call | bytes 1966080 | tf_op jit(solution)/shard_map/pallas_call | solution.py:304
  8.0 2.6 %collective-permute-start.2 = (bf16[2,128,640]{2,1,0:T(8,128)(2,1)S(1)}, bf16[2,128,640]{2,1,0:T(8,128)(2,1)S(1)}, u32[]{:S(2)}, u32[]{:S(2)}) collective-permute-start(bf16[2,128,640]{2,1,0:T(8,128)(2,1)S(1)} %get-tuple-element.23), channel_id=1, source_target_pairs={{0,4},{1,12},{4,0},{5,8},{8,5},{9,13},{12,1},{13,9},{2,6},{3,14},{... | collective-permute-start | bytes 983048 | tf_op jit(solution)/shard_map/ppermute | solution.py:360
  10.6 14.1 %collective-permute-start.3 = (bf16[2,128,640]{2,1,0:T(8,128)(2,1)S(1)}, bf16[2,128,640]{2,1,0:T(8,128)(2,1)S(1)}, u32[]{:S(2)}, u32[]{:S(2)}) collective-permute-start(bf16[2,128,640]{2,1,0:T(8,128)(2,1)S(1)} %collective-permute-done.1.refs_0_), channel_id=1, source_target_pairs={{0,1},{1,0},{2,3},{3,2},{4,5},{5,4},{6,7},{7,6},{8,9},{9,8},{10,11... | collective-permute-start | bytes 983048 | tf_op jit(solution)/shard_map/ppermute | solution.py:361
  25.4 6.1 %collective-permute-start.5 = (bf16[128,640]{1,0:T(8,128)(2,1)S(1)}, bf16[128,640]{1,0:T(8,128)(2,1)S(1)}, u32[]{:S(2)}, u32[]{:S(2)}) collective-permute-start(bf16[128,640]{1,0:T(8,128)(2,1)S(1)} %get-tuple-element.24), channel_id=1, source_target_pairs={{0,4},{4,0},{9,13},{13,9},{2,6},{6,2},{11,15},{15,11},{16,20},{20,... | collective-permute-start | bytes 491528 | tf_op jit(solution)/shard_map/ppermute | solution.py:356
  32.2 1.0 %copy-done = bf16[2560,64]{0,1:T(8,128)(2,1)S(1)} copy-done((bf16[2560,64]{0,1:T(8,128)(2,1)S(1)}, bf16[2560,64]{0,1:T(8,128)(2,1)}, u32[]{:S(2)}) %copy-start) | copy-done | bytes 327704
  35.4 1.5 %shard_map.120.refs_0_ = bf16[128,640]{1,0:T(8,128)(2,1)S(1)} custom-call(bf16[128,640]{1,0:T(8,128)(2,1)S(1)} %get-tuple-element.21.near_ref, bf16[128,640]{1,0:T(8,128)(2,1)S(1)} %collective-permute-done.far_ref, bf16[2,128,640]{2,1,0:T(8,128)(2,1)S(1)} %collective-permute-done.1.refs_0_, bf16[2,128,640]{2,1,0:T(8,128)(2,1)S(1)} %collective-permute-done.2.refs_1_, ...), custom_call_target="tpu_custom_call" | custom-call | flops 167772160 | bytes 1638400 | tf_op jit(solution)/shard_map/pallas_call | solution.py:304
  37.6 1.5 %shard_map.121 = bf16[128,640]{1,0:T(8,128)(2,1)S(1)} custom-call(bf16[128,640]{1,0:T(8,128)(2,1)S(1)} %collective-permute-done.5.near_ref, bf16[128,640]{1,0:T(8,128)(2,1)S(1)} %collective-permute-done.6.far_ref, bf16[2,128,640]{2,1,0:T(8,128)(2,1)S(1)} %collective-permute-done.1.refs_0_, bf16[2,128,640]{2,1,0:T(8,128)(2,1)S(1)} %collective-permute-done.2.refs_1_, ...), custom_call_target="tpu_custom_call" | custom-call | flops 167772160 | bytes 1638400 | tf_op jit(solution)/shard_map/pallas_call | solution.py:304
  39.0 2.4 %collective-permute-start.7 = (bf16[128,640]{1,0:T(8,128)(2,1)S(1)}, bf16[128,640]{1,0:T(8,128)(2,1)S(1)}, u32[]{:S(2)}, u32[]{:S(2)}) collective-permute-start(bf16[128,640]{1,0:T(8,128)(2,1)S(1)} %shard_map.121), channel_id=1, source_target_pairs={{4,0},{0,4},{13,9},{9,13},{6,2},{2,6},{15,11},{11,15},{20,16},{16,... | collective-permute-start | bytes 491528 | tf_op jit(solution)/shard_map/ppermute | solution.py:382
  42.1 5.5 %collective-permute-done.7.refs_1_ = bf16[128,640]{1,0:T(8,128)(2,1)S(1)} collective-permute-done((bf16[128,640]{1,0:T(8,128)(2,1)S(1)}, bf16[128,640]{1,0:T(8,128)(2,1)S(1)}, u32[]{:S(2)}, u32[]{:S(2)}) %collective-permute-start.7) | collective-permute-done | bytes 163872 | tf_op jit(solution)/shard_map/ppermute | solution.py:382
  47.7 1.1 %shard_map.124 = bf16[128,1280]{1,0:T(8,128)(2,1)S(1)} custom-call(bf16[128,640]{1,0:T(8,128)(2,1)S(1)} %shard_map.120.refs_0_, bf16[128,640]{1,0:T(8,128)(2,1)S(1)} %collective-permute-done.7.refs_1_, bf16[128,640]{1,0:T(8,128)(2,1)S(1)} %collective-permute-done.8.refs_2_, bf16[128,640]{1,0:T(8,128)(2,1)S(1)} %collective-permute-done.9.refs_3_, ...), custom_call_target="tpu_custom_call" | custom-call | flops 419430400 | bytes 3276800 | tf_op jit(solution)/shard_map/pallas_call | solution.py:304
  48.8 2.1 %collective-permute-start.13 = (bf16[128,1280]{1,0:T(8,128)(2,1)S(1)}, bf16[128,1280]{1,0:T(8,128)(2,1)S(1)}, u32[]{:S(2)}, u32[]{:S(2)}) collective-permute-start(bf16[128,1280]{1,0:T(8,128)(2,1)S(1)} %shard_map.124), channel_id=1, source_target_pairs={{0,2},{2,0},{1,3},{3,1},{4,6},{6,4},{5,7},{7,5},{8,10},{10,8},{9,1... | collective-permute-start | bytes 983048 | tf_op jit(solution)/shard_map/ppermute | solution.py:397
  50.9 1.1 %shard_map.123 = bf16[128,1280]{1,0:T(8,128)(2,1)S(1)} custom-call(bf16[128,640]{1,0:T(8,128)(2,1)S(1)} %shard_map.120.refs_0_, bf16[128,640]{1,0:T(8,128)(2,1)S(1)} %collective-permute-done.7.refs_1_, bf16[128,640]{1,0:T(8,128)(2,1)S(1)} %collective-permute-done.8.refs_2_, bf16[128,640]{1,0:T(8,128)(2,1)S(1)} %collective-permute-done.9.refs_3_, ...), custom_call_target="tpu_custom_call" | custom-call | flops 419430400 | bytes 3276800 | tf_op jit(solution)/shard_map/pallas_call | solution.py:304
  52.2 2.2 %shard_map.122.refs_0_ = f32[128,2560]{1,0:T(8,128)S(1)} custom-call(bf16[128,640]{1,0:T(8,128)(2,1)S(1)} %shard_map.120.refs_0_, bf16[128,640]{1,0:T(8,128)(2,1)S(1)} %collective-permute-done.7.refs_1_, bf16[128,640]{1,0:T(8,128)(2,1)S(1)} %collective-permute-done.8.refs_2_, bf16[128,640]{1,0:T(8,128)(2,1)S(1)} %collective-permute-done.9.refs_3_, ...), custom_call_target="tpu_custom_call" | custom-call | flops 838860800 | bytes 6553600 | tf_op jit(solution)/shard_map/pallas_call | solution.py:304
  54.4 1.6 %collective-permute-done.13.refs_1_ = bf16[128,1280]{1,0:T(8,128)(2,1)S(1)} collective-permute-done((bf16[128,1280]{1,0:T(8,128)(2,1)S(1)}, bf16[128,1280]{1,0:T(8,128)(2,1)S(1)}, u32[]{:S(2)}, u32[]{:S(2)}) %collective-permute-start.13) | collective-permute-done | bytes 327712 | tf_op jit(solution)/shard_map/ppermute | solution.py:397
  56.5 2.9 %collective-permute-done.12.refs_1_ = bf16[128,1280]{1,0:T(8,128)(2,1)S(1)} collective-permute-done((bf16[128,1280]{1,0:T(8,128)(2,1)S(1)}, bf16[128,1280]{1,0:T(8,128)(2,1)S(1)}, u32[]{:S(2)}, u32[]{:S(2)}) %collective-permute-start.12) | collective-permute-done | bytes 327712 | tf_op jit(solution)/shard_map/ppermute | solution.py:397
  60.0 2.1 %collective-permute-start.14 = (f32[72,128]{1,0:T(8,128)S(1)}, f32[72,128]{1,0:T(8,128)S(1)}, u32[]{:S(2)}, u32[]{:S(2)}) collective-permute-start(f32[72,128]{1,0:T(8,128)S(1)} %shard_map.126.own_ref), channel_id=1, source_target_pairs={{0,2},{2,0},{1,3},{3,1},{4,6},{6,4},{5,7},{7,5},{8,10},{10,8},{9,1... | collective-permute-start | bytes 110600 | tf_op jit(solution)/shard_map/ppermute | solution.py:418
  62.2 4.2 %collective-permute-done.15.rows_got_ref = f32[64,128]{1,0:T(8,128)S(1)} collective-permute-done((f32[64,128]{1,0:T(8,128)S(1)}, f32[64,128]{1,0:T(8,128)S(1)}, u32[]{:S(2)}, u32[]{:S(2)}) %collective-permute-start.15) | collective-permute-done | bytes 32800 | tf_op jit(solution)/shard_map/ppermute | solution.py:369
  66.5 9.4 %collective-permute-start.16 = (f32[32,128]{1,0:T(8,128)S(1)}, f32[32,128]{1,0:T(8,128)S(1)}, u32[]{:S(2)}, u32[]{:S(2)}) collective-permute-start(f32[32,128]{1,0:T(8,128)S(1)} %get-tuple-element.30), channel_id=1, source_target_pairs={{0,1},{1,0},{2,3},{3,2},{4,5},{5,4},{6,7},{7,6},{8,9},{9,8},{10,11... | collective-permute-start | bytes 49160 | tf_op jit(solution)/shard_map/ppermute | solution.py:425
  75.9 0.8 collective-permute-done.16.got_ref
  77.4 0.9 %collective-permute-start.17 = (f32[8,128]{1,0:T(8,128)S(1)}, f32[8,128]{1,0:T(8,128)S(1)}, u32[]{:S(2)}, u32[]{:S(2)}) collective-permute-start(f32[8,128]{1,0:T(8,128)S(1)} %get-tuple-element.32), channel_id=1, source_target_pairs={{0,4},{4,8},{8,12},{12,0},{1,5},{5,9},{9,13},{13,1},{2,6},{6,10},{... | collective-permute-start | bytes 12296 | tf_op jit(solution)/shard_map/ppermute | solution.py:434
  78.3 4.3 %collective-permute-start.18 = (f32[8,128]{1,0:T(8,128)S(1)}, f32[8,128]{1,0:T(8,128)S(1)}, u32[]{:S(2)}, u32[]{:S(2)}) collective-permute-start(f32[8,128]{1,0:T(8,128)S(1)} %get-tuple-element.33), channel_id=1, source_target_pairs={{0,8},{4,12},{8,0},{12,4},{1,9},{5,13},{9,1},{13,5},{2,10},{6,14},... | collective-permute-start | bytes 12296 | tf_op jit(solution)/shard_map/ppermute | solution.py:434
  84.2 2.0 %collective-permute-done.19.refs_3_ = f32[8,128]{1,0:T(8,128)S(1)} collective-permute-done((f32[8,128]{1,0:T(8,128)S(1)}, f32[8,128]{1,0:T(8,128)S(1)}, u32[]{:S(2)}, u32[]{:S(2)}) %collective-permute-start.19) | collective-permute-done | bytes 4128 | tf_op jit(solution)/shard_map/ppermute | solution.py:434
  (46 shorter events, 9.3 us)
Async XLA Ops:
  0.0 47.7 %collective-permute-start.10 = (bf16[1280,2560]{1,0:T(8,128)(2,1)}, bf16[1280,2560]{1,0:T(8,128)(2,1)S(1)}, u32[]{:S(2)}, u32[]{:S(2)}) collective-permute-start(bf16[1280,2560]{1,0:T(8,128)(2,1)} %param.16), channel_id=1, source_target_pairs={{0,0},{1,1},{2,3},{3,2},{4,4},{5,5},{6,7},{7,6},{8,8},{9,9},{10,11... | collective-permute-start | bytes 19660808 | tf_op jit(solution)/shard_map/ppermute | solution.py:357
  3.5 44.1 %collective-permute-start.11 = (bf16[1280,2560]{1,0:T(8,128)(2,1)}, bf16[1280,2560]{1,0:T(8,128)(2,1)S(1)}, u32[]{:S(2)}, u32[]{:S(2)}) collective-permute-start(bf16[1280,2560]{1,0:T(8,128)(2,1)} %param.16), channel_id=1, source_target_pairs={{0,1},{1,0},{2,2},{3,3},{4,5},{5,4},{6,6},{7,7},{8,9},{9,8},{10,10... | collective-permute-start | bytes 19660808 | tf_op jit(solution)/shard_map/ppermute | solution.py:358
  7.3 3.3 %collective-permute-start.1 = (bf16[2,128,640]{2,1,0:T(8,128)(2,1)S(1)}, bf16[2,128,640]{2,1,0:T(8,128)(2,1)S(1)}, u32[]{:S(2)}, u32[]{:S(2)}) collective-permute-start(bf16[2,128,640]{2,1,0:T(8,128)(2,1)S(1)} %get-tuple-element.22), channel_id=1, source_target_pairs={{0,0},{1,8},{4,4},{5,12},{8,1},{9,9},{12,5},{13,13},{2,2},{3,10},{... | collective-permute-start | bytes 983048 | tf_op jit(solution)/shard_map/ppermute | solution.py:360
  8.0 16.7 %collective-permute-start.2 = (bf16[2,128,640]{2,1,0:T(8,128)(2,1)S(1)}, bf16[2,128,640]{2,1,0:T(8,128)(2,1)S(1)}, u32[]{:S(2)}, u32[]{:S(2)}) collective-permute-start(bf16[2,128,640]{2,1,0:T(8,128)(2,1)S(1)} %get-tuple-element.23), channel_id=1, source_target_pairs={{0,4},{1,12},{4,0},{5,8},{8,5},{9,13},{12,1},{13,9},{2,6},{3,14},{... | collective-permute-start | bytes 983048 | tf_op jit(solution)/shard_map/ppermute | solution.py:360
  10.6 20.9 %collective-permute-start.3 = (bf16[2,128,640]{2,1,0:T(8,128)(2,1)S(1)}, bf16[2,128,640]{2,1,0:T(8,128)(2,1)S(1)}, u32[]{:S(2)}, u32[]{:S(2)}) collective-permute-start(bf16[2,128,640]{2,1,0:T(8,128)(2,1)S(1)} %collective-permute-done.1.refs_0_), channel_id=1, source_target_pairs={{0,1},{1,0},{2,3},{3,2},{4,5},{5,4},{6,7},{7,6},{8,9},{9,8},{10,11... | collective-permute-start | bytes 983048 | tf_op jit(solution)/shard_map/ppermute | solution.py:361
  24.7 10.7 %collective-permute-start.4 = (bf16[2,128,640]{2,1,0:T(8,128)(2,1)S(1)}, bf16[2,128,640]{2,1,0:T(8,128)(2,1)S(1)}, u32[]{:S(2)}, u32[]{:S(2)}) collective-permute-start(bf16[2,128,640]{2,1,0:T(8,128)(2,1)S(1)} %collective-permute-done.2.refs_1_), channel_id=1, source_target_pairs={{0,1},{1,0},{2,3},{3,2},{4,5},{5,4},{6,7},{7,6},{8,9},{9,8},{10,11... | collective-permute-start | bytes 983048 | tf_op jit(solution)/shard_map/ppermute | solution.py:361
  24.7 0.7 collective-permute-start
  25.4 12.2 %collective-permute-start.5 = (bf16[128,640]{1,0:T(8,128)(2,1)S(1)}, bf16[128,640]{1,0:T(8,128)(2,1)S(1)}, u32[]{:S(2)}, u32[]{:S(2)}) collective-permute-start(bf16[128,640]{1,0:T(8,128)(2,1)S(1)} %get-tuple-element.24), channel_id=1, source_target_pairs={{0,4},{4,0},{9,13},{13,9},{2,6},{6,2},{11,15},{15,11},{16,20},{20,... | collective-permute-start | bytes 491528 | tf_op jit(solution)/shard_map/ppermute | solution.py:356
  31.5 6.0 %collective-permute-start.6 = (bf16[128,640]{1,0:T(8,128)(2,1)S(1)}, bf16[128,640]{1,0:T(8,128)(2,1)S(1)}, u32[]{:S(2)}, u32[]{:S(2)}) collective-permute-start(bf16[128,640]{1,0:T(8,128)(2,1)S(1)} %get-tuple-element.24), channel_id=1, source_target_pairs={{1,12},{5,8},{8,5},{12,1},{3,14},{7,10},{10,7},{14,3},{17,28},{21,... | collective-permute-start | bytes 491528 | tf_op jit(solution)/shard_map/ppermute | solution.py:362
  36.9 5.2 %collective-permute-start.8 = (bf16[128,640]{1,0:T(8,128)(2,1)S(1)}, bf16[128,640]{1,0:T(8,128)(2,1)S(1)}, u32[]{:S(2)}, u32[]{:S(2)}) collective-permute-start(bf16[128,640]{1,0:T(8,128)(2,1)S(1)} %shard_map.120.refs_0_), channel_id=1, source_target_pairs={{8,1},{12,5},{1,8},{5,12},{10,3},{14,7},{3,10},{7,14},{24,17},{28,... | collective-permute-start | bytes 491528 | tf_op jit(solution)/shard_map/ppermute | solution.py:381
  39.0 8.6 %collective-permute-start.7 = (bf16[128,640]{1,0:T(8,128)(2,1)S(1)}, bf16[128,640]{1,0:T(8,128)(2,1)S(1)}, u32[]{:S(2)}, u32[]{:S(2)}) collective-permute-start(bf16[128,640]{1,0:T(8,128)(2,1)S(1)} %shard_map.121), channel_id=1, source_target_pairs={{4,0},{0,4},{13,9},{9,13},{6,2},{2,6},{15,11},{11,15},{20,16},{16,... | collective-permute-start | bytes 491528 | tf_op jit(solution)/shard_map/ppermute | solution.py:382
  41.4 6.2 %collective-permute-start.9 = (bf16[128,640]{1,0:T(8,128)(2,1)S(1)}, bf16[128,640]{1,0:T(8,128)(2,1)S(1)}, u32[]{:S(2)}, u32[]{:S(2)}) collective-permute-start(bf16[128,640]{1,0:T(8,128)(2,1)S(1)} %shard_map.121), channel_id=1, source_target_pairs={{12,1},{8,5},{5,8},{1,12},{14,3},{10,7},{7,10},{3,14},{28,17},{24,... | collective-permute-start | bytes 491528 | tf_op jit(solution)/shard_map/ppermute | solution.py:381
  48.8 7.1 %collective-permute-start.13 = (bf16[128,1280]{1,0:T(8,128)(2,1)S(1)}, bf16[128,1280]{1,0:T(8,128)(2,1)S(1)}, u32[]{:S(2)}, u32[]{:S(2)}) collective-permute-start(bf16[128,1280]{1,0:T(8,128)(2,1)S(1)} %shard_map.124), channel_id=1, source_target_pairs={{0,2},{2,0},{1,3},{3,1},{4,6},{6,4},{5,7},{7,5},{8,10},{10,8},{9,1... | collective-permute-start | bytes 983048 | tf_op jit(solution)/shard_map/ppermute | solution.py:397
  52.0 7.4 %collective-permute-start.12 = (bf16[128,1280]{1,0:T(8,128)(2,1)S(1)}, bf16[128,1280]{1,0:T(8,128)(2,1)S(1)}, u32[]{:S(2)}, u32[]{:S(2)}) collective-permute-start(bf16[128,1280]{1,0:T(8,128)(2,1)S(1)} %shard_map.123), channel_id=1, source_target_pairs={{0,2},{2,0},{1,3},{3,1},{4,6},{6,4},{5,7},{7,5},{8,10},{10,8},{9,1... | collective-permute-start | bytes 983048 | tf_op jit(solution)/shard_map/ppermute | solution.py:397
  52.1 3.8 %copy-start.1 = (bf16[2560,64]{0,1:T(8,128)(2,1)S(1)}, bf16[2560,64]{0,1:T(8,128)(2,1)}, u32[]{:S(2)}) copy-start(bf16[2560,64]{0,1:T(8,128)(2,1)} %param.20) | copy-start | bytes 983044
  52.1 3.8 %copy-start.5 = (f32[1,2560]{1,0:T(1,128)S(1)}, f32[1,2560]{1,0:T(1,128)}, u32[]{:S(2)}) copy-start(f32[1,2560]{1,0:T(1,128)} %refs_3_.3) | copy-start | bytes 30724
  52.1 24.6 %copy-start.8 = (s32[1,4]{1,0:T(1,128)S(1)}, s32[1,4]{1,0:T(1,128)}, u32[]{:S(2)}) copy-start(s32[1,4]{1,0:T(1,128)} %owner_ref.1) | copy-start | bytes 52
  52.1 34.1 %copy-start.6 = (f32[1,1,128,32]{2,3,1,0:T(8,128)S(1)}, f32[1,1,128,32]{2,3,1,0:T(8,128)}, u32[]{:S(2)}) copy-start(f32[1,1,128,32]{2,3,1,0:T(8,128)} %param.21) | copy-start | bytes 49156
  60.0 6.3 %collective-permute-start.14 = (f32[72,128]{1,0:T(8,128)S(1)}, f32[72,128]{1,0:T(8,128)S(1)}, u32[]{:S(2)}, u32[]{:S(2)}) collective-permute-start(f32[72,128]{1,0:T(8,128)S(1)} %shard_map.126.own_ref), channel_id=1, source_target_pairs={{0,2},{2,0},{1,3},{3,1},{4,6},{6,4},{5,7},{7,5},{8,10},{10,8},{9,1... | collective-permute-start | bytes 110600 | tf_op jit(solution)/shard_map/ppermute | solution.py:418
  62.1 4.3 %collective-permute-start.15 = (f32[64,128]{1,0:T(8,128)S(1)}, f32[64,128]{1,0:T(8,128)S(1)}, u32[]{:S(2)}, u32[]{:S(2)}) collective-permute-start(f32[64,128]{1,0:T(8,128)S(1)} %shard_map.119.rows_own_ref), channel_id=1, source_target_pairs={{0,2},{2,0},{1,3},{3,1},{4,6},{6,4},{5,7},{7,5},{8,10},{10,8},{9,1... | collective-permute-start | bytes 98312 | tf_op jit(solution)/shard_map/ppermute | solution.py:369
  66.5 10.2 %collective-permute-start.16 = (f32[32,128]{1,0:T(8,128)S(1)}, f32[32,128]{1,0:T(8,128)S(1)}, u32[]{:S(2)}, u32[]{:S(2)}) collective-permute-start(f32[32,128]{1,0:T(8,128)S(1)} %get-tuple-element.30), channel_id=1, source_target_pairs={{0,1},{1,0},{2,3},{3,2},{4,5},{5,4},{6,7},{7,6},{8,9},{9,8},{10,11... | collective-permute-start | bytes 49160 | tf_op jit(solution)/shard_map/ppermute | solution.py:425
  77.4 6.6 %collective-permute-start.17 = (f32[8,128]{1,0:T(8,128)S(1)}, f32[8,128]{1,0:T(8,128)S(1)}, u32[]{:S(2)}, u32[]{:S(2)}) collective-permute-start(f32[8,128]{1,0:T(8,128)S(1)} %get-tuple-element.32), channel_id=1, source_target_pairs={{0,4},{4,8},{8,12},{12,0},{1,5},{5,9},{9,13},{13,1},{2,6},{6,10},{... | collective-permute-start | bytes 12296 | tf_op jit(solution)/shard_map/ppermute | solution.py:434
  78.3 5.9 %collective-permute-start.18 = (f32[8,128]{1,0:T(8,128)S(1)}, f32[8,128]{1,0:T(8,128)S(1)}, u32[]{:S(2)}, u32[]{:S(2)}) collective-permute-start(f32[8,128]{1,0:T(8,128)S(1)} %get-tuple-element.33), channel_id=1, source_target_pairs={{0,8},{4,12},{8,0},{12,4},{1,9},{5,13},{9,1},{13,5},{2,10},{6,14},... | collective-permute-start | bytes 12296 | tf_op jit(solution)/shard_map/ppermute | solution.py:434
  82.6 3.6 %collective-permute-start.19 = (f32[8,128]{1,0:T(8,128)S(1)}, f32[8,128]{1,0:T(8,128)S(1)}, u32[]{:S(2)}, u32[]{:S(2)}) collective-permute-start(f32[8,128]{1,0:T(8,128)S(1)} %get-tuple-element.34), channel_id=1, source_target_pairs={{0,12},{4,0},{8,4},{12,8},{1,13},{5,1},{9,5},{13,9},{2,14},{6,2},{... | collective-permute-start | bytes 12296 | tf_op jit(solution)/shard_map/ppermute | solution.py:434
  (5 other events, 9.0 us)

commit v2 on v0

--- a/solution.py
+++ b/solution.py
@@ -106,52 +106,66 @@
 
 def pack_kernel(parts, half, *refs):
     q_ref, k_ref, v_ref = refs[:3]
-    out_refs, sems = refs[3:-1], refs[-1]
+    pair_refs, own_ref, full_refs, sems = refs[3 : 3 + parts], refs[3 + parts], refs[4 + parts : -1], refs[-1]
     z = lax.axis_index("seq")
     copies = []
+
+    def copy(source, cols, target):
+        copies.append(pltpu.make_async_copy(source.at[:, cols], target, sems.at[len(copies)]))
+        copies[-1].start()
+
     for j in range(parts):
         cols = pl.ds(pl.multiple_of(lax.rem(z + j, parts) * half, LANES), half)
-        copies.append(pltpu.make_async_copy(k_ref.at[:, cols], out_refs[j].at[0], sems.at[3 * j]))
-        copies.append(pltpu.make_async_copy(v_ref.at[:, cols], out_refs[j].at[1], sems.at[3 * j + 1]))
-        copies.append(pltpu.make_async_copy(q_ref.at[:, cols], out_refs[parts + j], sems.at[3 * j + 2]))
-    for copy in copies:
-        copy.start()
-    for copy in copies:
-        copy.wait()
+        copy(k_ref, cols, pair_refs[j].at[0])
+        copy(v_ref, cols, pair_refs[j].at[1])
+        if j == 0:
+            copy(q_ref, cols, own_ref)
+        else:
+            for i, source in enumerate((k_ref, v_ref, q_ref)):
+                copy(source, cols, full_refs[j - 1].at[i])
+    for started in copies:
+        started.wait()
 
 
 def attend_kernel(parts, *refs):
-    q_refs = refs[:parts]
-    kv_refs = refs[parts : 3 * parts]
-    o_refs = refs[3 * parts :]
-    rows = q_refs[0].shape[0]
-    for i in range(q_refs[0].shape[1] // HEAD_DIM):
+    own_q_ref, own_kv_ref = refs[:2]
+    near_refs = refs[2 : 1 + parts]
+    far_refs = [refs[1 + parts + i * parts : 1 + parts + (i + 1) * parts] for i in range(2)]
+    out_refs = refs[1 + 3 * parts :]
+    rows = own_q_ref.shape[0]
+    first = lax.axis_index("guide") == 0
+    for i in range(own_q_ref.shape[1] // HEAD_DIM):
         cols = slice(i * HEAD_DIM, (i + 1) * HEAD_DIM)
-        q = jnp.concatenate([r[:, cols] for r in q_refs], axis=0)
-        k = jnp.concatenate([r[0, :, cols] for r in kv_refs], axis=0)
-        v = jnp.concatenate([r[1, :, cols] for r in kv_refs], axis=0)
-        scores = lax.dot_general(q, k, (((1,), (1,)), ((), ())), preferred_element_type=F32)
+
+        def gather(which):
+            blocks = [own_kv_ref[which, :, cols]] + [r[which, :, cols] for r in near_refs]
+            for a, b in zip(*far_refs):
+                blocks.append(jnp.where(first, a[which, :, cols], b[which, :, cols]))
+            return jnp.concatenate(blocks, axis=0)
+
+        q = jnp.concatenate([own_q_ref[:, cols]] + [r[2, :, cols] for r in near_refs], axis=0)
+        scores = lax.dot_general(q, gather(0), (((1,), (1,)), ((), ())), preferred_element_type=F32)
         scores = scores * (HEAD_DIM ** (-0.5) * LOG2E)
         expo = jnp.exp2(scores - jnp.max(scores, axis=1, keepdims=True))
         total = jnp.sum(expo, axis=1, keepdims=True)
-        mixed = jnp.dot(expo.astype(BF16), v, preferred_element_type=F32) / total
+        mixed = jnp.dot(expo.astype(BF16), gather(1), preferred_element_type=F32) / total
         for j in range(parts):
-            o_refs[j][:, cols] = mixed[j * rows : (j + 1) * rows].astype(BF16)
-
-
-def project(parts, half, o_refs, w_ref, cols):
+            out_refs[j][:, cols] = mixed[j * rows : (j + 1) * rows].astype(BF16)
+
+
+def project(parts, half, attended, w_ref, cols):
     z = lax.axis_index("seq")
     total = None
     for j in range(parts):
         start = pl.multiple_of(lax.rem(z + j, parts) * half, LANES)
-        term = jnp.dot(o_refs[j][...], w_ref[pl.ds(start, half), cols], preferred_element_type=F32)
+        term = jnp.dot(attended[j], w_ref[pl.ds(start, half), cols], preferred_element_type=F32)
         total = term if total is None else total + term
     return total
 
 
 def send_kernel(parts, half, chunk, first, *refs):
-    o_refs = refs[:parts]
     near_ref, far_ref, out_ref = refs[parts:]
+    attended = [r[...] for r in refs[:parts]]
     guide = lax.axis_index("guide")
     for value, w_ref in ((1, near_ref), (0, far_ref)):
 
@@ -159,12 +173,12 @@
         def _():
             for t in range(out_ref.shape[1] // chunk):
                 cols = slice(first + t * chunk, first + (t + 1) * chunk)
-                out_ref[:, t * chunk : (t + 1) * chunk] = project(parts, half, o_refs, w_ref, cols).astype(BF16)
+                out_ref[:, t * chunk : (t + 1) * chunk] = project(parts, half, attended, w_ref, cols).astype(BF16)
 
 
 def keep_kernel(parts, half, chunk, *refs):
-    o_refs = refs[:parts]
     near_ref, far_ref, res_ref, gate_ref, out_ref = refs[parts:]
+    attended = [r[...] for r in refs[:parts]]
     guide = lax.axis_index("guide")
     for value, w_ref in ((0, near_ref), (1, far_ref)):
 
@@ -173,7 +187,7 @@
             for t in range(out_ref.shape[1] // chunk):
                 cols = slice(t * chunk, (t + 1) * chunk)
                 out_ref[:, cols] = res_ref[:, cols].astype(F32) + gate_ref[:, cols] * project(
-                    parts, half, o_refs, w_ref, cols
+                    parts, half, attended, w_ref, cols
                 )
 
 
@@ -262,7 +276,7 @@
     rows = guided.shape[0] // fold
     lane = lax.broadcasted_iota(jnp.int32, (rows, LANES), 1) // group
     for k in range(seq_count):
-        target = lax.rem(z + k, seq_count)
+        target = z ^ k
         frame = jnp.int32(0)
         for f in range(seq_count):
             frame = jnp.where(owner_ref[0, f] == target, f, frame)
@@ -284,7 +298,7 @@
     for j in range(fold):
         block = jnp.zeros((rows, LANES), F32)
         for k in range(seq_count):
-            source = lax.rem(z - k + seq_count, seq_count)
+            source = z ^ k
             shift = lax.rem((source - j) * group + LANES, LANES)
             block = jnp.where(lane == source, pltpu.roll(piece_refs[k][...], shift, axis=1), block)
         blocks.append(block)
@@ -319,36 +333,36 @@
     group = rows // seq_count
     width_model = float(width_shard * lax.axis_size("shard"))
     both = [(0, 1), (1, 0)]
-    axes = ("seq", "guide")
 
     crossed = [(x * 2 + c, x * 2 + (c + x) % 2) for x in range(2) for c in range(2)]
     straight = [(x * 2 + c, x * 2 + (c + x + 1) % 2) for x in range(2) for c in range(2)]
 
     packed = call(
         functools.partial(pack_kernel, parts, half),
-        [((2, rows, half), BF16)] * parts + [((rows, half), BF16)] * parts,
+        [((2, rows, half), BF16)] * parts + [((rows, half), BF16)] + [((3, rows, half), BF16)] * (parts - 1),
         [
             pltpu.with_memory_space_constraint(array[0, 0], pltpu.HBM)
             for array in (queries, key_vecs, value_vecs)
         ],
         [HBM_SPEC] * 3,
-        [pltpu.SemaphoreType.DMA((3 * parts,))],
+        [pltpu.SemaphoreType.DMA((5 * parts,))],
         moved=12 * rows * width_local,
     )
-    there = [
-        [
-            (z * 2 + c, (parts * c + (z + j) % parts) * 2 + z // parts)
-            for z in range(seq_count)
-            for c in range(2)
-        ]
-        for j in range(parts)
-    ]
-    back = [[(b, a) for a, b in pairs] for pairs in there]
-    kv_own = [lax.ppermute(packed[j], axes, there[j]) for j in range(parts)]
-    q_own = [lax.ppermute(packed[parts + j], axes, there[j]) for j in range(parts)]
+    kv_sent, q_own, full_sent = packed[:parts], packed[parts], packed[parts + 1 :]
+
+    def to_part(z, j, across):
+        return (z // parts + across) % 2 * parts + (z + j) % parts
+
+    def far_pairs(j, core):
+        return [(z * 2 + core, to_part(z, j, 1) * 2 + core) for z in range(seq_count)]
+
+    axes = ("seq", "guide")
+    near_pairs = [[(z, to_part(z, j, 0)) for z in range(seq_count)] for j in range(parts)]
+    far = [[lax.ppermute(kv_sent[j], axes, far_pairs(j, 0)) for j in range(parts)]]
+    near = [lax.ppermute(full_sent[j - 1], "seq", near_pairs[j]) for j in range(1, parts)]
     near_w = lax.ppermute(w_out, ("shard", "guide"), crossed)
     far_w = lax.ppermute(w_out, ("shard", "guide"), straight)
-    kv_other = [lax.ppermute(block, "guide", both) for block in kv_own]
+    far.append([lax.ppermute(kv_sent[j], axes, far_pairs(j, 1)) for j in range(parts)])
 
     head_t = w_head.T
     rows_own = call(
@@ -356,17 +370,16 @@
         moved=4 * width_shard * LANES,
     )[0]
     rows_got = lax.ppermute(rows_own, "shard", both)
-    *q_own, rows_own = lax.optimization_barrier((*q_own, rows_own))
+    q_own, rows_own = lax.optimization_barrier((q_own, rows_own))
 
     mixed = call(
         functools.partial(attend_kernel, parts),
         [((rows, half), BF16)] * parts,
-        q_own + kv_own + kv_other,
+        [q_own, kv_sent[0]] + near + far[0] + far[1],
         flops=8 * rows * parts * rows * parts * half,
         moved=2 * rows * half * parts * 6,
     )
-    *mixed, rows_got, near_w, far_w = lax.optimization_barrier((*mixed, rows_got, near_w, far_w))
-    mixed = [lax.ppermute(mixed[j], axes, back[j]) for j in range(parts)]
+    mixed = [mixed[0]] + [lax.ppermute(mixed[j], "seq", [(b, a) for a, b in near_pairs[j]]) for j in range(1, parts)]
 
     chunk = 128
     pieces = 2
@@ -417,7 +430,7 @@
         [SMEM_SPEC, VMEM_SPEC, VMEM_SPEC],
     )
     arrived = [frames[0]] + [
-        lax.ppermute(frames[k], "seq", [(z, (z + k) % seq_count) for z in range(seq_count)])
+        lax.ppermute(frames[k], "seq", [(z, z ^ k) for z in range(seq_count)])
         for k in range(1, seq_count)
     ]
     out = call(
@@ -433,7 +446,7 @@
     seq_count = sizes["seq"]
     step_count, rows, width_local = queries.shape[1:]
     channels = w_head.shape[1]
-    if sizes["guide"] != 2 or sizes["shard"] != 2 or seq_count % 2 or step_count != 1 or rows != LANES:
+    if seq_count < 2 or sizes["guide"] != 2 or sizes["shard"] != 2 or seq_count & (seq_count - 1) or step_count != 1 or rows != LANES:
         return False
     if width_local % (seq_count // 2 * HEAD_DIM) or residual.shape[3] % (4 * LANES):
         return False

time: 79.4 us -> 87.1 us (1.097)
  waiting for transfers between devices: 13.7 us -> 37.4 us
  starting transfers between devices: 51.3 us -> 35.3 us
    ppermute x11 -> x9, waiting for transfers between devices: 5.48 us -> 23.3 us  [the longest x2 17 us: fast_plan(): lax.ppermute(kv_sent[j], axes, far_pairs(j, 0))]
    ppermute x1, starting transfers between devices: 7.76 us -> 0.07 us  [fast_plan(): eps_got = lax.ppermute(send, 'guide', both)]
    ppermute x11 -> x9, starting transfers between devices: 31.6 us -> 25.1 us  [the longest x2 11.7 us: fast_plan(): lax.ppermute(kv_sent[j], axes, far_pairs(j, 0))]
    ppermute x2, waiting for transfers between devices: 4.58 us -> 9.49 us  [fast_plan(): got.append(lax.ppermute(partial, 'shard', both))]
    ppermute x1, waiting for transfers between devices: 0.48 us -> 3.39 us  [fast_plan(): rows_got = lax.ppermute(rows_own, 'shard', both)]
    ppermute x1, waiting for transfers between devices: 2.34 us -> 0.01 us  [fast_plan(): sums_got = lax.ppermute(sums, 'shard', both)]
    ppermute x1, starting transfers between devices: 1.75 us -> 0.53 us  [fast_plan(): rows_got = lax.ppermute(rows_own, 'shard', both)]
    unnamed x16 -> x18, local copies, waits for them, and re-layouts: 2.4 us -> 2.4 us
  transfers between devices with their start and end apart: 18 -> 16, of which waited for: 10 -> 9; matrix products, arithmetic and copies ran while one was open for 0% -> 0% of each run, Pallas kernels for 10% -> 9%
where the time goes in v2:
time: 87.1 us; the launch traced here: 86.7 us
  waiting for transfers between devices  37.4 us (43%)
  starting transfers between devices  35.3 us (41%)
  Pallas kernels  10.8 us (12%)
  local copies, waits for them, and re-layouts  2.4 us (3%)
    ppermute x2, waiting for transfers between devices, fast_plan(): lax.ppermute(kv_sent[j], axes, far_pairs(j, 0))  17 us
    ppermute x2, starting transfers between devices, fast_plan(): lax.ppermute(kv_sent[j], axes, far_pairs(j, 0))  11.7 us
    pallas_call x11, Pallas kernels, call(): pl.pallas_call(kernel, out_shape=shapes, in_specs=specs or [VMEM_SPEC] *...  10.8 us
    ppermute x2, waiting for transfers between devices, fast_plan(): got.append(lax.ppermute(partial, 'shard', both))  9.49 us
    ppermute x1, starting transfers between devices, fast_plan(): lax.ppermute(mixed[j], 'seq', [(b, a) for a, b in near_pairs[j]])  5.93 us
    ppermute x3, starting transfers between devices, fast_plan(): lax.ppermute(frames[k], 'seq', [(z, z ^ k) for z in range(seq_count)])  4.45 us
    ppermute x1, waiting for transfers between devices, fast_plan(): lax.ppermute(mixed[j], 'seq', [(b, a) for a, b in near_pairs[j]])  3.64 us
    ppermute x1, starting transfers between devices, fast_plan(): near_w = lax.ppermute(w_out, ('shard', 'guide'), crossed)  3.51 us
  transfers between devices with their start and end apart: 16, of which 9 were waited for; matrix products, arithmetic and copies ran while one was open for 0% of the time, Pallas kernels for 9%

profile of v2, /device:TPU:0, one launch (start us, length us, event | category | flops | bytes accessed | tf_op | source)
XLA Modules:
  0.0 86.7 jit_solution(7696028232348899048)
XLA Ops:
  0.0 3.5 %collective-permute-start.6 = (bf16[1280,2560]{1,0:T(8,128)(2,1)}, bf16[1280,2560]{1,0:T(8,128)(2,1)S(1)}, u32[]{:S(2)}, u32[]{:S(2)}) collective-permute-start(bf16[1280,2560]{1,0:T(8,128)(2,1)} %param.16), channel_id=1, source_target_pairs={{0,0},{1,1},{2,3},{3,2},{4,4},{5,5},{6,7},{7,6},{8,8},{9,9},{10,11... | collective-permute-start | bytes 19660808 | tf_op jit(solution)/shard_map/ppermute | solution.py:363
  3.5 2.4 %collective-permute-start.7 = (bf16[1280,2560]{1,0:T(8,128)(2,1)}, bf16[1280,2560]{1,0:T(8,128)(2,1)S(1)}, u32[]{:S(2)}, u32[]{:S(2)}) collective-permute-start(bf16[1280,2560]{1,0:T(8,128)(2,1)} %param.16), channel_id=1, source_target_pairs={{0,1},{1,0},{2,2},{3,3},{4,5},{5,4},{6,6},{7,7},{8,9},{9,8},{10,10... | collective-permute-start | bytes 19660808 | tf_op jit(solution)/shard_map/ppermute | solution.py:364
  5.9 1.5 %shard_map.118 = (bf16[2,128,640]{2,1,0:T(8,128)(2,1)S(1)}, bf16[2,128,640]{2,1,0:T(8,128)(2,1)S(1)}, bf16[128,640]{1,0:T(8,128)(2,1)S(1)}, bf16[3,128,640]{2,1,0:T(8,128)(2,1)S(1)}) custom-call(bf16[128,1280]{1,0:T(8,128)(2,1)} %bitcast.16, bf16[128,1280]{1,0:T(8,128)(2,1)} %bitcast.17, bf16[128,1280]{1,0:T(8,128)(2,1)} %bitcast.18), custom_call_target="tpu_custom_call" | custom-call | bytes 1966080 | tf_op jit(solution)/shard_map/pallas_call | solution.py:312
  7.4 5.5 %collective-permute-start.1 = (bf16[2,128,640]{2,1,0:T(8,128)(2,1)S(1)}, bf16[2,128,640]{2,1,0:T(8,128)(2,1)S(1)}, u32[]{:S(2)}, u32[]{:S(2)}) collective-permute-start(bf16[2,128,640]{2,1,0:T(8,128)(2,1)S(1)} %get-tuple-element.24.refs_1_), channel_id=1, source_target_pairs={{0,8},{4,12},{8,0},{12,4},{2,10},{6,14},{10,2},{14,6},{16,24},{20,... | collective-permute-start | bytes 983048 | tf_op jit(solution)/shard_map/ppermute | solution.py:361
  13.6 1.6 %collective-permute-start = (bf16[3,128,640]{2,1,0:T(8,128)(2,1)S(1)}, bf16[3,128,640]{2,1,0:T(8,128)(2,1)S(1)}, u32[]{:S(2)}, u32[]{:S(2)}) collective-permute-start(bf16[3,128,640]{2,1,0:T(8,128)(2,1)S(1)} %get-tuple-element.25), channel_id=1, source_target_pairs={{0,4},{4,0},{8,12},{12,8},{1,5},{5,1},{9,13},{13,9},{2,6},{6,2},{1... | collective-permute-start | bytes 1474568 | tf_op jit(solution)/shard_map/ppermute | solution.py:362
  15.2 12.8 %collective-permute-done.1.refs_3_ = bf16[2,128,640]{2,1,0:T(8,128)(2,1)S(1)} collective-permute-done((bf16[2,128,640]{2,1,0:T(8,128)(2,1)S(1)}, bf16[2,128,640]{2,1,0:T(8,128)(2,1)S(1)}, u32[]{:S(2)}, u32[]{:S(2)}) %collective-permute-start.1) | collective-permute-done | bytes 327712 | tf_op jit(solution)/shard_map/ppermute | solution.py:361
  28.1 6.2 %collective-permute-start.2 = (bf16[2,128,640]{2,1,0:T(8,128)(2,1)S(1)}, bf16[2,128,640]{2,1,0:T(8,128)(2,1)S(1)}, u32[]{:S(2)}, u32[]{:S(2)}) collective-permute-start(bf16[2,128,640]{2,1,0:T(8,128)(2,1)S(1)} %get-tuple-element.26), channel_id=1, source_target_pairs={{0,12},{4,8},{8,4},{12,0},{2,14},{6,10},{10,6},{14,2},{16,28},{20,... | collective-permute-start | bytes 983048 | tf_op jit(solution)/shard_map/ppermute | solution.py:361
  35.0 1.0 %copy-done = bf16[2560,64]{0,1:T(8,128)(2,1)S(1)} copy-done((bf16[2560,64]{0,1:T(8,128)(2,1)S(1)}, bf16[2560,64]{0,1:T(8,128)(2,1)}, u32[]{:S(2)}) %copy-start) | copy-done | bytes 327704
  38.1 4.1 %collective-permute-done.2.refs_4_ = bf16[2,128,640]{2,1,0:T(8,128)(2,1)S(1)} collective-permute-done((bf16[2,128,640]{2,1,0:T(8,128)(2,1)S(1)}, bf16[2,128,640]{2,1,0:T(8,128)(2,1)S(1)}, u32[]{:S(2)}, u32[]{:S(2)}) %collective-permute-start.2) | collective-permute-done | bytes 327712 | tf_op jit(solution)/shard_map/ppermute | solution.py:361
  42.3 1.7 %shard_map.120 = (bf16[128,640]{1,0:T(8,128)(2,1)S(1)}, bf16[128,640]{1,0:T(8,128)(2,1)S(1)}) custom-call(bf16[128,640]{1,0:T(8,128)(2,1)S(1)} %get-tuple-element.23.refs_0_, bf16[2,128,640]{2,1,0:T(8,128)(2,1)S(1)} %get-tuple-element.24.refs_1_, bf16[3,128,640]{2,1,0:T(8,128)(2,1)S(1)} %collective-permute-done.refs_2_, ...), custom_call_target="tpu_custom_call" | custom-call | flops 335544320 | bytes 1966080 | tf_op jit(solution)/shard_map/pallas_call | solution.py:312
  44.0 5.9 %collective-permute-start.5 = (bf16[128,640]{1,0:T(8,128)(2,1)S(1)}, bf16[128,640]{1,0:T(8,128)(2,1)S(1)}, u32[]{:S(2)}, u32[]{:S(2)}) collective-permute-start(bf16[128,640]{1,0:T(8,128)(2,1)S(1)} %get-tuple-element.28), channel_id=1, source_target_pairs={{4,0},{0,4},{12,8},{8,12},{5,1},{1,5},{13,9},{9,13},{6,2},{2,6},{1... | collective-permute-start | bytes 491528 | tf_op jit(solution)/shard_map/ppermute | solution.py:382
  49.9 3.6 %collective-permute-done.5.refs_1_ = bf16[128,640]{1,0:T(8,128)(2,1)S(1)} collective-permute-done((bf16[128,640]{1,0:T(8,128)(2,1)S(1)}, bf16[128,640]{1,0:T(8,128)(2,1)S(1)}, u32[]{:S(2)}, u32[]{:S(2)}) %collective-permute-start.5) | collective-permute-done | bytes 163872 | tf_op jit(solution)/shard_map/ppermute | solution.py:382
  53.6 1.1 %shard_map.123 = bf16[128,1280]{1,0:T(8,128)(2,1)S(1)} custom-call(bf16[128,640]{1,0:T(8,128)(2,1)S(1)} %get-tuple-element.27.refs_0_, bf16[128,640]{1,0:T(8,128)(2,1)S(1)} %collective-permute-done.5.refs_1_, bf16[1280,2560]{1,0:T(8,128)(2,1)S(1)} %collective-permute-done.6.refs_2_, bf16[1280,2560]{1,0:T(8,128)(2,1)S(1)} %collective-permute-done.7.refs_3_), custom_call_target="tpu_custom_call" | custom-call | flops 419430400 | bytes 3276800 | tf_op jit(solution)/shard_map/pallas_call | solution.py:312
  54.7 1.6 %collective-permute-start.9 = (bf16[128,1280]{1,0:T(8,128)(2,1)S(1)}, bf16[128,1280]{1,0:T(8,128)(2,1)S(1)}, u32[]{:S(2)}, u32[]{:S(2)}) collective-permute-start(bf16[128,1280]{1,0:T(8,128)(2,1)S(1)} %shard_map.123), channel_id=1, source_target_pairs={{0,2},{2,0},{1,3},{3,1},{4,6},{6,4},{5,7},{7,5},{8,10},{10,8},{9,1... | collective-permute-start | bytes 983048 | tf_op jit(solution)/shard_map/ppermute | solution.py:396
  56.3 1.1 %shard_map.122 = bf16[128,1280]{1,0:T(8,128)(2,1)S(1)} custom-call(bf16[128,640]{1,0:T(8,128)(2,1)S(1)} %get-tuple-element.27.refs_0_, bf16[128,640]{1,0:T(8,128)(2,1)S(1)} %collective-permute-done.5.refs_1_, bf16[1280,2560]{1,0:T(8,128)(2,1)S(1)} %collective-permute-done.6.refs_2_, bf16[1280,2560]{1,0:T(8,128)(2,1)S(1)} %collective-permute-done.7.refs_3_), custom_call_target="tpu_custom_call" | custom-call | flops 419430400 | bytes 3276800 | tf_op jit(solution)/shard_map/pallas_call | solution.py:312
  58.0 2.0 %shard_map.121.refs_0_ = f32[128,2560]{1,0:T(8,128)S(1)} custom-call(bf16[128,640]{1,0:T(8,128)(2,1)S(1)} %get-tuple-element.27.refs_0_, bf16[128,640]{1,0:T(8,128)(2,1)S(1)} %collective-permute-done.5.refs_1_, bf16[1280,2560]{1,0:T(8,128)(2,1)S(1)} %collective-permute-done.6.refs_2_, bf16[1280,2560]{1,0:T(8,128)(2,1)S(1)} %collective-permute-done.7.refs_3_, ...), custom_call_target="tpu_custom_call" | custom-call | flops 838860800 | bytes 6553600 | tf_op jit(solution)/shard_map/pallas_call | solution.py:312
  60.0 5.3 %collective-permute-done.9.refs_1_ = bf16[128,1280]{1,0:T(8,128)(2,1)S(1)} collective-permute-done((bf16[128,1280]{1,0:T(8,128)(2,1)S(1)}, bf16[128,1280]{1,0:T(8,128)(2,1)S(1)}, u32[]{:S(2)}, u32[]{:S(2)}) %collective-permute-start.9) | collective-permute-done | bytes 327712 | tf_op jit(solution)/shard_map/ppermute | solution.py:396
  65.9 4.2 %collective-permute-done.8.refs_1_ = bf16[128,1280]{1,0:T(8,128)(2,1)S(1)} collective-permute-done((bf16[128,1280]{1,0:T(8,128)(2,1)S(1)}, bf16[128,1280]{1,0:T(8,128)(2,1)S(1)}, u32[]{:S(2)}, u32[]{:S(2)}) %collective-permute-start.8) | collective-permute-done | bytes 327712 | tf_op jit(solution)/shard_map/ppermute | solution.py:396
  70.7 1.6 %collective-permute-start.10 = (f32[72,128]{1,0:T(8,128)S(1)}, f32[72,128]{1,0:T(8,128)S(1)}, u32[]{:S(2)}, u32[]{:S(2)}) collective-permute-start(f32[72,128]{1,0:T(8,128)S(1)} %shard_map.125.own_ref), channel_id=1, source_target_pairs={{0,2},{2,0},{1,3},{3,1},{4,6},{6,4},{5,7},{7,5},{8,10},{10,8},{9,1... | collective-permute-start | bytes 110600 | tf_op jit(solution)/shard_map/ppermute | solution.py:417
  72.8 3.4 %collective-permute-done.11.rows_got_ref = f32[64,128]{1,0:T(8,128)S(1)} collective-permute-done((f32[64,128]{1,0:T(8,128)S(1)}, f32[64,128]{1,0:T(8,128)S(1)}, u32[]{:S(2)}, u32[]{:S(2)}) %collective-permute-start.11) | collective-permute-done | bytes 32800 | tf_op jit(solution)/shard_map/ppermute | solution.py:372
  76.3 1.2 %collective-permute-done.12.got_ref = f32[32,128]{1,0:T(8,128)S(1)} collective-permute-done((f32[32,128]{1,0:T(8,128)S(1)}, f32[32,128]{1,0:T(8,128)S(1)}, u32[]{:S(2)}, u32[]{:S(2)}) %collective-permute-start.12) | collective-permute-done | bytes 16416 | tf_op jit(solution)/shard_map/ppermute | solution.py:424
  78.1 1.5 %collective-permute-start.13 = (f32[8,128]{1,0:T(8,128)S(1)}, f32[8,128]{1,0:T(8,128)S(1)}, u32[]{:S(2)}, u32[]{:S(2)}) collective-permute-start(f32[8,128]{1,0:T(8,128)S(1)} %get-tuple-element.36), channel_id=1, source_target_pairs={{0,4},{4,0},{8,12},{12,8},{1,5},{5,1},{9,13},{13,9},{2,6},{6,2},{1... | collective-permute-start | bytes 12296 | tf_op jit(solution)/shard_map/ppermute | solution.py:433
  80.5 2.1 %collective-permute-start.15 = (f32[8,128]{1,0:T(8,128)S(1)}, f32[8,128]{1,0:T(8,128)S(1)}, u32[]{:S(2)}, u32[]{:S(2)}) collective-permute-start(f32[8,128]{1,0:T(8,128)S(1)} %get-tuple-element.38), channel_id=1, source_target_pairs={{0,12},{4,8},{8,4},{12,0},{1,13},{5,9},{9,5},{13,1},{2,14},{6,10},... | collective-permute-start | bytes 12296 | tf_op jit(solution)/shard_map/ppermute | solution.py:433
  84.2 1.7 %collective-permute-done.15.refs_3_ = f32[8,128]{1,0:T(8,128)S(1)} collective-permute-done((f32[8,128]{1,0:T(8,128)S(1)}, f32[8,128]{1,0:T(8,128)S(1)}, u32[]{:S(2)}, u32[]{:S(2)}) %collective-permute-start.15) | collective-permute-done | bytes 4128 | tf_op jit(solution)/shard_map/ppermute | solution.py:433
  (37 shorter events, 9.2 us)
Async XLA Ops:
  0.0 53.6 %collective-permute-start.6 = (bf16[1280,2560]{1,0:T(8,128)(2,1)}, bf16[1280,2560]{1,0:T(8,128)(2,1)S(1)}, u32[]{:S(2)}, u32[]{:S(2)}) collective-permute-start(bf16[1280,2560]{1,0:T(8,128)(2,1)} %param.16), channel_id=1, source_target_pairs={{0,0},{1,1},{2,3},{3,2},{4,4},{5,5},{6,7},{7,6},{8,8},{9,9},{10,11... | collective-permute-start | bytes 19660808 | tf_op jit(solution)/shard_map/ppermute | solution.py:363
  3.5 50.1 %collective-permute-start.7 = (bf16[1280,2560]{1,0:T(8,128)(2,1)}, bf16[1280,2560]{1,0:T(8,128)(2,1)S(1)}, u32[]{:S(2)}, u32[]{:S(2)}) collective-permute-start(bf16[1280,2560]{1,0:T(8,128)(2,1)} %param.16), channel_id=1, source_target_pairs={{0,1},{1,0},{2,2},{3,3},{4,5},{5,4},{6,6},{7,7},{8,9},{9,8},{10,10... | collective-permute-start | bytes 19660808 | tf_op jit(solution)/shard_map/ppermute | solution.py:364
  7.4 20.7 %collective-permute-start.1 = (bf16[2,128,640]{2,1,0:T(8,128)(2,1)S(1)}, bf16[2,128,640]{2,1,0:T(8,128)(2,1)S(1)}, u32[]{:S(2)}, u32[]{:S(2)}) collective-permute-start(bf16[2,128,640]{2,1,0:T(8,128)(2,1)S(1)} %get-tuple-element.24.refs_1_), channel_id=1, source_target_pairs={{0,8},{4,12},{8,0},{12,4},{2,10},{6,14},{10,2},{14,6},{16,24},{20,... | collective-permute-start | bytes 983048 | tf_op jit(solution)/shard_map/ppermute | solution.py:361
  12.9 21.4 %collective-permute-start.3 = (bf16[2,128,640]{2,1,0:T(8,128)(2,1)S(1)}, bf16[2,128,640]{2,1,0:T(8,128)(2,1)S(1)}, u32[]{:S(2)}, u32[]{:S(2)}) collective-permute-start(bf16[2,128,640]{2,1,0:T(8,128)(2,1)S(1)} %get-tuple-element.24.refs_1_), channel_id=1, source_target_pairs={{1,9},{5,13},{9,1},{13,5},{3,11},{7,15},{11,3},{15,7},{17,25},{21,... | collective-permute-start | bytes 983048 | tf_op jit(solution)/shard_map/ppermute | solution.py:365
  13.6 28.7 %collective-permute-start = (bf16[3,128,640]{2,1,0:T(8,128)(2,1)S(1)}, bf16[3,128,640]{2,1,0:T(8,128)(2,1)S(1)}, u32[]{:S(2)}, u32[]{:S(2)}) collective-permute-start(bf16[3,128,640]{2,1,0:T(8,128)(2,1)S(1)} %get-tuple-element.25), channel_id=1, source_target_pairs={{0,4},{4,0},{8,12},{12,8},{1,5},{5,1},{9,13},{13,9},{2,6},{6,2},{1... | collective-permute-start | bytes 1474568 | tf_op jit(solution)/shard_map/ppermute | solution.py:362
  28.1 14.2 %collective-permute-start.2 = (bf16[2,128,640]{2,1,0:T(8,128)(2,1)S(1)}, bf16[2,128,640]{2,1,0:T(8,128)(2,1)S(1)}, u32[]{:S(2)}, u32[]{:S(2)}) collective-permute-start(bf16[2,128,640]{2,1,0:T(8,128)(2,1)S(1)} %get-tuple-element.26), channel_id=1, source_target_pairs={{0,12},{4,8},{8,4},{12,0},{2,14},{6,10},{10,6},{14,2},{16,28},{20,... | collective-permute-start | bytes 983048 | tf_op jit(solution)/shard_map/ppermute | solution.py:361
  34.3 8.0 %collective-permute-start.4 = (bf16[2,128,640]{2,1,0:T(8,128)(2,1)S(1)}, bf16[2,128,640]{2,1,0:T(8,128)(2,1)S(1)}, u32[]{:S(2)}, u32[]{:S(2)}) collective-permute-start(bf16[2,128,640]{2,1,0:T(8,128)(2,1)S(1)} %get-tuple-element.26), channel_id=1, source_target_pairs={{1,13},{5,9},{9,5},{13,1},{3,15},{7,11},{11,7},{15,3},{17,29},{21,... | collective-permute-start | bytes 983048 | tf_op jit(solution)/shard_map/ppermute | solution.py:365
  35.0 1.0 %copy-start = (bf16[2560,64]{0,1:T(8,128)(2,1)S(1)}, bf16[2560,64]{0,1:T(8,128)(2,1)}, u32[]{:S(2)}) copy-start(bf16[2560,64]{0,1:T(8,128)(2,1)} %param.20) | copy-start | bytes 983044
  35.9 0.7 copy-start.4
  44.0 9.6 %collective-permute-start.5 = (bf16[128,640]{1,0:T(8,128)(2,1)S(1)}, bf16[128,640]{1,0:T(8,128)(2,1)S(1)}, u32[]{:S(2)}, u32[]{:S(2)}) collective-permute-start(bf16[128,640]{1,0:T(8,128)(2,1)S(1)} %get-tuple-element.28), channel_id=1, source_target_pairs={{4,0},{0,4},{12,8},{8,12},{5,1},{1,5},{13,9},{9,13},{6,2},{2,6},{1... | collective-permute-start | bytes 491528 | tf_op jit(solution)/shard_map/ppermute | solution.py:382
  54.7 3.3 %copy-start.2 = (bf16[1,1,128,2560]{3,2,1,0:T(8,128)(2,1)S(1)}, bf16[1,1,128,2560]{3,2,1,0:T(8,128)(2,1)}, u32[]{:S(2)}) copy-start(bf16[1,1,128,2560]{3,2,1,0:T(8,128)(2,1)} %param.15) | copy-start | bytes 1966084
  54.7 3.3 %copy-start.3 = (f32[1,2560]{1,0:T(1,128)S(1)}, f32[1,2560]{1,0:T(1,128)}, u32[]{:S(2)}) copy-start(f32[1,2560]{1,0:T(1,128)} %refs_2_.3) | copy-start | bytes 30724
  54.7 10.6 %collective-permute-start.9 = (bf16[128,1280]{1,0:T(8,128)(2,1)S(1)}, bf16[128,1280]{1,0:T(8,128)(2,1)S(1)}, u32[]{:S(2)}, u32[]{:S(2)}) collective-permute-start(bf16[128,1280]{1,0:T(8,128)(2,1)S(1)} %shard_map.123), channel_id=1, source_target_pairs={{0,2},{2,0},{1,3},{3,1},{4,6},{6,4},{5,7},{7,5},{8,10},{10,8},{9,1... | collective-permute-start | bytes 983048 | tf_op jit(solution)/shard_map/ppermute | solution.py:396
  57.4 12.7 %collective-permute-start.8 = (bf16[128,1280]{1,0:T(8,128)(2,1)S(1)}, bf16[128,1280]{1,0:T(8,128)(2,1)S(1)}, u32[]{:S(2)}, u32[]{:S(2)}) collective-permute-start(bf16[128,1280]{1,0:T(8,128)(2,1)S(1)} %shard_map.122), channel_id=1, source_target_pairs={{0,2},{2,0},{1,3},{3,1},{4,6},{6,4},{5,7},{7,5},{8,10},{10,8},{9,1... | collective-permute-start | bytes 983048 | tf_op jit(solution)/shard_map/ppermute | solution.py:396
  58.0 7.4 %copy-start.1 = (bf16[2560,64]{0,1:T(8,128)(2,1)S(1)}, bf16[2560,64]{0,1:T(8,128)(2,1)}, u32[]{:S(2)}) copy-start(bf16[2560,64]{0,1:T(8,128)(2,1)} %param.20) | copy-start | bytes 983044
  58.0 7.4 %copy-start.5 = (f32[1,2560]{1,0:T(1,128)S(1)}, f32[1,2560]{1,0:T(1,128)}, u32[]{:S(2)}) copy-start(f32[1,2560]{1,0:T(1,128)} %refs_3_.3) | copy-start | bytes 30724
  58.0 19.5 %copy-start.8 = (s32[1,4]{1,0:T(1,128)S(1)}, s32[1,4]{1,0:T(1,128)}, u32[]{:S(2)}) copy-start(s32[1,4]{1,0:T(1,128)} %owner_ref.1) | copy-start | bytes 52
  58.0 27.9 %copy-start.6 = (f32[1,1,128,32]{2,3,1,0:T(8,128)S(1)}, f32[1,1,128,32]{2,3,1,0:T(8,128)}, u32[]{:S(2)}) copy-start(f32[1,1,128,32]{2,3,1,0:T(8,128)} %param.21) | copy-start | bytes 49156
  70.7 5.5 %collective-permute-start.10 = (f32[72,128]{1,0:T(8,128)S(1)}, f32[72,128]{1,0:T(8,128)S(1)}, u32[]{:S(2)}, u32[]{:S(2)}) collective-permute-start(f32[72,128]{1,0:T(8,128)S(1)} %shard_map.125.own_ref), channel_id=1, source_target_pairs={{0,2},{2,0},{1,3},{3,1},{4,6},{6,4},{5,7},{7,5},{8,10},{10,8},{9,1... | collective-permute-start | bytes 110600 | tf_op jit(solution)/shard_map/ppermute | solution.py:417
  72.2 3.9 %collective-permute-start.11 = (f32[64,128]{1,0:T(8,128)S(1)}, f32[64,128]{1,0:T(8,128)S(1)}, u32[]{:S(2)}, u32[]{:S(2)}) collective-permute-start(f32[64,128]{1,0:T(8,128)S(1)} %shard_map.119.rows_own_ref), channel_id=1, source_target_pairs={{0,2},{2,0},{1,3},{3,1},{4,6},{6,4},{5,7},{7,5},{8,10},{10,8},{9,1... | collective-permute-start | bytes 98312 | tf_op jit(solution)/shard_map/ppermute | solution.py:372
  76.2 1.2 %collective-permute-start.12 = (f32[32,128]{1,0:T(8,128)S(1)}, f32[32,128]{1,0:T(8,128)S(1)}, u32[]{:S(2)}, u32[]{:S(2)}) collective-permute-start(f32[32,128]{1,0:T(8,128)S(1)} %get-tuple-element.34), channel_id=1, source_target_pairs={{0,1},{1,0},{2,3},{3,2},{4,5},{5,4},{6,7},{7,6},{8,9},{9,8},{10,11... | collective-permute-start | bytes 49160 | tf_op jit(solution)/shard_map/ppermute | solution.py:424
  78.1 5.1 %collective-permute-start.13 = (f32[8,128]{1,0:T(8,128)S(1)}, f32[8,128]{1,0:T(8,128)S(1)}, u32[]{:S(2)}, u32[]{:S(2)}) collective-permute-start(f32[8,128]{1,0:T(8,128)S(1)} %get-tuple-element.36), channel_id=1, source_target_pairs={{0,4},{4,0},{8,12},{12,8},{1,5},{5,1},{9,13},{13,9},{2,6},{6,2},{1... | collective-permute-start | bytes 12296 | tf_op jit(solution)/shard_map/ppermute | solution.py:433
  79.7 4.5 %collective-permute-start.14 = (f32[8,128]{1,0:T(8,128)S(1)}, f32[8,128]{1,0:T(8,128)S(1)}, u32[]{:S(2)}, u32[]{:S(2)}) collective-permute-start(f32[8,128]{1,0:T(8,128)S(1)} %get-tuple-element.37), channel_id=1, source_target_pairs={{0,8},{4,12},{8,0},{12,4},{1,9},{5,13},{9,1},{13,5},{2,10},{6,14},... | collective-permute-start | bytes 12296 | tf_op jit(solution)/shard_map/ppermute | solution.py:433
  80.5 5.4 %collective-permute-start.15 = (f32[8,128]{1,0:T(8,128)S(1)}, f32[8,128]{1,0:T(8,128)S(1)}, u32[]{:S(2)}, u32[]{:S(2)}) collective-permute-start(f32[8,128]{1,0:T(8,128)S(1)} %get-tuple-element.38), channel_id=1, source_target_pairs={{0,12},{4,8},{8,4},{12,0},{1,13},{5,9},{9,5},{13,1},{2,14},{6,10},... | collective-permute-start | bytes 12296 | tf_op jit(solution)/shard_map/ppermute | solution.py:433
  (1 other events, 0.7 us)

commit v3 on v0

--- a/solution.py
+++ b/solution.py
@@ -104,16 +104,16 @@
     return plan_weight(timesteps)[:, None, None, None] * (guided - noise)
 
 
-def pack_kernel(parts, half, *refs):
-    q_ref, k_ref, v_ref = refs[:3]
-    out_refs, sems = refs[3:-1], refs[-1]
+def pack_kernel(parts, half, count, *refs):
+    source_refs, out_refs, sems = refs[:count], refs[count:-1], refs[-1]
     z = lax.axis_index("seq")
     copies = []
     for j in range(parts):
         cols = pl.ds(pl.multiple_of(lax.rem(z + j, parts) * half, LANES), half)
-        copies.append(pltpu.make_async_copy(k_ref.at[:, cols], out_refs[j].at[0], sems.at[3 * j]))
-        copies.append(pltpu.make_async_copy(v_ref.at[:, cols], out_refs[j].at[1], sems.at[3 * j + 1]))
-        copies.append(pltpu.make_async_copy(q_ref.at[:, cols], out_refs[parts + j], sems.at[3 * j + 2]))
+        for i in range(count):
+            copies.append(
+                pltpu.make_async_copy(source_refs[i].at[:, cols], out_refs[j].at[i], sems.at[j * count + i])
+            )
     for copy in copies:
         copy.start()
     for copy in copies:
@@ -124,10 +124,10 @@
     q_refs = refs[:parts]
     kv_refs = refs[parts : 3 * parts]
     o_refs = refs[3 * parts :]
-    rows = q_refs[0].shape[0]
-    for i in range(q_refs[0].shape[1] // HEAD_DIM):
+    rows = q_refs[0].shape[1]
+    for i in range(q_refs[0].shape[2] // HEAD_DIM):
         cols = slice(i * HEAD_DIM, (i + 1) * HEAD_DIM)
-        q = jnp.concatenate([r[:, cols] for r in q_refs], axis=0)
+        q = jnp.concatenate([r[0, :, cols] for r in q_refs], axis=0)
         k = jnp.concatenate([r[0, :, cols] for r in kv_refs], axis=0)
         v = jnp.concatenate([r[1, :, cols] for r in kv_refs], axis=0)
         scores = lax.dot_general(q, k, (((1,), (1,)), ((), ())), preferred_element_type=F32)
@@ -186,7 +186,13 @@
     )
 
 
-def head_rows_kernel(scale_ref, shift_ref, head_ref, out_ref):
+def early_kernel(seq_count, scale_ref, shift_ref, head_ref, owner_ref, steps_ref, out_ref, chosen_ref, weight_ref):
+    z = lax.axis_index("seq")
+    for k in range(seq_count):
+        for f in range(seq_count):
+            here = jnp.where(owner_ref[0, f] == z ^ k, 1.0, 0.0)
+            chosen_ref[k * seq_count + f : k * seq_count + f + 1, :] = jnp.full((1, LANES), here, F32)
+    weight_ref[...] = plan_weight(jnp.full((SUBLANES, LANES), steps_ref[0], jnp.int32))
     width = scale_ref.shape[1]
     which = lax.broadcasted_iota(jnp.int32, (LANES, width), 0)
     rows = jnp.where(which == 0, 1.0 + scale_ref[...], shift_ref[...])
@@ -251,8 +257,7 @@
     send_ref[...] = eps_scr[pl.ds(pl.multiple_of((1 - guide) * half_channels, SUBLANES), half_channels), :]
 
 
-def frame_kernel(seq_count, group, owner_ref, keep_ref, got_ref, *out_refs):
-    z = lax.axis_index("seq")
+def frame_kernel(seq_count, group, chosen_ref, keep_ref, got_ref, *out_refs):
     first = lax.axis_index("guide") == 0
     mine, other = keep_ref[...], got_ref[...]
     eps_cond = jnp.where(first, mine, other)
@@ -261,36 +266,35 @@
     fold = LANES // group
     rows = guided.shape[0] // fold
     lane = lax.broadcasted_iota(jnp.int32, (rows, LANES), 1) // group
+    packed = []
+    for f in range(seq_count):
+        block = jnp.zeros((rows, LANES), F32)
+        for j in range(fold):
+            piece = guided[j * rows : (j + 1) * rows]
+            shift = (j - f) * group % LANES
+            block = jnp.where(lane == j, pltpu.roll(piece, shift, axis=1) if shift else piece, block)
+        packed.append(block)
     for k in range(seq_count):
-        target = lax.rem(z + k, seq_count)
-        frame = jnp.int32(0)
-        for f in range(seq_count):
-            frame = jnp.where(owner_ref[0, f] == target, f, frame)
-        packed = jnp.zeros((rows, LANES), F32)
-        for j in range(fold):
-            shift = lax.rem((j - frame) * group + LANES, LANES)
-            rolled = pltpu.roll(guided[j * rows : (j + 1) * rows], shift, axis=1)
-            packed = jnp.where(lane == j, rolled, packed)
-        out_refs[k][...] = packed
-
-
-def final_kernel(seq_count, group, steps_ref, noise_ref, *refs):
+        block = packed[0]
+        for f in range(1, seq_count):
+            block = jnp.where(chosen_ref[k * seq_count + f : k * seq_count + f + 1, :] > 0.5, packed[f], block)
+        out_refs[k][...] = block
+
+
+def final_kernel(seq_count, group, weight_ref, noise_ref, *refs):
     piece_refs, out_ref = refs[:seq_count], refs[seq_count]
     z = lax.axis_index("seq")
     fold = LANES // group
     rows = piece_refs[0].shape[0]
     lane = lax.broadcasted_iota(jnp.int32, (rows, LANES), 1) // group
-    blocks = []
     for j in range(fold):
         block = jnp.zeros((rows, LANES), F32)
         for k in range(seq_count):
-            source = lax.rem(z - k + seq_count, seq_count)
+            source = z ^ k
             shift = lax.rem((source - j) * group + LANES, LANES)
             block = jnp.where(lane == source, pltpu.roll(piece_refs[k][...], shift, axis=1), block)
-        blocks.append(block)
-    framed = jnp.concatenate(blocks, axis=0)
-    step = jnp.full((1, 1), steps_ref[0], jnp.int32)
-    out_ref[...] = plan_weight(step) * (framed - noise_ref[...])
+        part = slice(j * rows, (j + 1) * rows)
+        out_ref[part, :] = weight_ref[0:1, :] * (block - noise_ref[part, :])
 
 
 def call(kernel, outs, args, specs=None, scratch=(), flops=0, moved=0, grant=16):
@@ -324,17 +328,17 @@
     crossed = [(x * 2 + c, x * 2 + (c + x) % 2) for x in range(2) for c in range(2)]
     straight = [(x * 2 + c, x * 2 + (c + x + 1) % 2) for x in range(2) for c in range(2)]
 
-    packed = call(
-        functools.partial(pack_kernel, parts, half),
-        [((2, rows, half), BF16)] * parts + [((rows, half), BF16)] * parts,
-        [
-            pltpu.with_memory_space_constraint(array[0, 0], pltpu.HBM)
-            for array in (queries, key_vecs, value_vecs)
-        ],
-        [HBM_SPEC] * 3,
-        [pltpu.SemaphoreType.DMA((3 * parts,))],
-        moved=12 * rows * width_local,
-    )
+    def pack(*arrays):
+        return call(
+            functools.partial(pack_kernel, parts, half, len(arrays)),
+            [((len(arrays), rows, half), BF16)] * parts,
+            [pltpu.with_memory_space_constraint(array[0, 0], pltpu.HBM) for array in arrays],
+            [HBM_SPEC] * len(arrays),
+            [pltpu.SemaphoreType.DMA((parts * len(arrays),))],
+            moved=4 * len(arrays) * rows * width_local,
+        )
+
+    kv_sent = pack(key_vecs, value_vecs)
     there = [
         [
             (z * 2 + c, (parts * c + (z + j) % parts) * 2 + z // parts)
@@ -344,17 +348,21 @@
         for j in range(parts)
     ]
     back = [[(b, a) for a, b in pairs] for pairs in there]
-    kv_own = [lax.ppermute(packed[j], axes, there[j]) for j in range(parts)]
-    q_own = [lax.ppermute(packed[parts + j], axes, there[j]) for j in range(parts)]
+    kv_own = [lax.ppermute(kv_sent[j], axes, there[j]) for j in range(parts)]
+    q_sent = pack(queries)
+    q_own = [lax.ppermute(q_sent[j], axes, there[j]) for j in range(parts)]
     near_w = lax.ppermute(w_out, ("shard", "guide"), crossed)
     far_w = lax.ppermute(w_out, ("shard", "guide"), straight)
     kv_other = [lax.ppermute(block, "guide", both) for block in kv_own]
 
     head_t = w_head.T
-    rows_own = call(
-        head_rows_kernel, [((channels, LANES), F32)], [norm_scale, norm_shift, head_t],
+    rows_own, chosen, weight = call(
+        functools.partial(early_kernel, seq_count),
+        [((channels, LANES), F32), ((seq_count * seq_count, LANES), F32), ((SUBLANES, LANES), F32)],
+        [norm_scale, norm_shift, head_t, frame_owner, timesteps],
+        [VMEM_SPEC] * 3 + [SMEM_SPEC] * 2,
         moved=4 * width_shard * LANES,
-    )[0]
+    )
     rows_got = lax.ppermute(rows_own, "shard", both)
     *q_own, rows_own = lax.optimization_barrier((*q_own, rows_own))
 
@@ -365,11 +373,10 @@
         flops=8 * rows * parts * rows * parts * half,
         moved=2 * rows * half * parts * 6,
     )
-    *mixed, rows_got, near_w, far_w = lax.optimization_barrier((*mixed, rows_got, near_w, far_w))
     mixed = [lax.ppermute(mixed[j], axes, back[j]) for j in range(parts)]
 
     chunk = 128
-    pieces = 2
+    pieces = 4
     width_piece = width_shard // pieces
     got = []
     for i in range(pieces):
@@ -413,18 +420,16 @@
     frames = call(
         functools.partial(frame_kernel, seq_count, group),
         [((channels // 2 // fold, LANES), F32)] * seq_count,
-        [frame_owner, keep, eps_got],
-        [SMEM_SPEC, VMEM_SPEC, VMEM_SPEC],
+        [chosen, keep, eps_got],
     )
     arrived = [frames[0]] + [
-        lax.ppermute(frames[k], "seq", [(z, (z + k) % seq_count) for z in range(seq_count)])
+        lax.ppermute(frames[k], "seq", [(z, z ^ k) for z in range(seq_count)])
         for k in range(1, seq_count)
     ]
     out = call(
         functools.partial(final_kernel, seq_count, group),
         [((channels // 2, rows), F32)],
-        [timesteps, noise[0, 0].T] + arrived,
-        [SMEM_SPEC] + [VMEM_SPEC] * (seq_count + 1),
+        [weight, noise[0, 0].T] + arrived,
     )[0]
     return out.T[None, None]
 
@@ -433,7 +438,7 @@
     seq_count = sizes["seq"]
     step_count, rows, width_local = queries.shape[1:]
     channels = w_head.shape[1]
-    if sizes["guide"] != 2 or sizes["shard"] != 2 or seq_count % 2 or step_count != 1 or rows != LANES:
+    if seq_count < 2 or sizes["guide"] != 2 or sizes["shard"] != 2 or seq_count & (seq_count - 1) or step_count != 1 or rows != LANES:
         return False
     if width_local % (seq_count // 2 * HEAD_DIM) or residual.shape[3] % (4 * LANES):
         return False

time: 79.4 us -> 80.1 us (level)
  starting transfers between devices: 51.3 us -> 48.2 us
  Pallas kernels: 10.8 us -> 12.3 us
  waiting for transfers between devices: 13.7 us -> 15.2 us
    ppermute x2 -> x4, waiting for transfers between devices: 4.58 us -> 1.87 us  [fast_plan(): got.append(lax.ppermute(partial, 'shard', both))]
    ppermute x1, waiting for transfers between devices: 0.48 us -> 3.02 us  [fast_plan(): rows_got = lax.ppermute(rows_own, 'shard', both)]
    ppermute x2, waiting for transfers between devices: 2.63 us -> 5.03 us  [fast_plan(): mixed = [lax.ppermute(mixed[j], axes, back[j]) for j in range(parts)]]
    ppermute x1, waiting for transfers between devices: 2.34 us -> 0.01 us  [fast_plan(): sums_got = lax.ppermute(sums, 'shard', both)]
    ppermute x2 -> x4, starting transfers between devices: 2.18 us -> 4.31 us  [fast_plan(): got.append(lax.ppermute(partial, 'shard', both))]
    ppermute x2, starting transfers between devices: 2.72 us -> 1.02 us  [fast_plan(): mixed = [lax.ppermute(mixed[j], axes, back[j]) for j in range(parts)]]
    ppermute x1, starting transfers between devices: 7.76 us -> 6.08 us  [fast_plan(): eps_got = lax.ppermute(send, 'guide', both)]
    ppermute x7, waiting for transfers between devices: 2.84 us -> 4.42 us  [the longest x3 4.41 us: fast_plan(): lax.ppermute(frames[k], 'seq', [(z, z ^ k) for z in range(seq_count)])]
  transfers between devices with their start and end apart: 18 -> 20, of which waited for: 10 -> 7; matrix products, arithmetic and copies ran while one was open for 0% -> 0% of each run, Pallas kernels for 10% -> 13%
where the time goes in v3:
time: 80.1 us; the launch traced here: 79.7 us
  starting transfers between devices  48.2 us (60%)
  waiting for transfers between devices  15.2 us (19%)
  Pallas kernels  12.3 us (15%)
  local copies, waits for them, and re-layouts  3.05 us (4%)
  between operations  0.9 us (1%)
    ppermute x2, starting transfers between devices, fast_plan(): kv_other = [lax.ppermute(block, 'guide', both) for block in kv_own]  14.2 us
    pallas_call x16, Pallas kernels, call(): pl.pallas_call(kernel, out_shape=shapes, in_specs=specs or [VMEM_SPEC] *...  12.3 us
    ppermute x3, starting transfers between devices, fast_plan(): lax.ppermute(frames[k], 'seq', [(z, z ^ k) for z in range(seq_count)])  6.46 us
    ppermute x1, starting transfers between devices, fast_plan(): eps_got = lax.ppermute(send, 'guide', both)  6.08 us
    ppermute x2, waiting for transfers between devices, fast_plan(): mixed = [lax.ppermute(mixed[j], axes, back[j]) for j in range(parts)]  5.03 us
    ppermute x2, starting transfers between devices, fast_plan(): q_own = [lax.ppermute(q_sent[j], axes, there[j]) for j in range(parts)]  4.9 us
    ppermute x3, waiting for transfers between devices, fast_plan(): lax.ppermute(frames[k], 'seq', [(z, z ^ k) for z in range(seq_count)])  4.41 us
    ppermute x4, starting transfers between devices, fast_plan(): got.append(lax.ppermute(partial, 'shard', both))  4.31 us
  transfers between devices with their start and end apart: 20, of which 7 were waited for; matrix products, arithmetic and copies ran while one was open for 0% of the time, Pallas kernels for 13%

profile of v3, /device:TPU:0, one launch (start us, length us, event | category | flops | bytes accessed | tf_op | source)
XLA Modules:
  0.0 79.7 jit_solution(4519534267913144464)
XLA Ops:
  0.0 3.5 %collective-permute-start.8 = (bf16[1280,2560]{1,0:T(8,128)(2,1)}, bf16[1280,2560]{1,0:T(8,128)(2,1)S(1)}, u32[]{:S(2)}, u32[]{:S(2)}) collective-permute-start(bf16[1280,2560]{1,0:T(8,128)(2,1)} %param.16), channel_id=1, source_target_pairs={{0,0},{1,1},{2,3},{3,2},{4,4},{5,5},{6,7},{7,6},{8,8},{9,9},{10,11... | collective-permute-start | bytes 19660808 | tf_op jit(solution)/shard_map/ppermute | solution.py:354
  3.5 2.4 %collective-permute-start.9 = (bf16[1280,2560]{1,0:T(8,128)(2,1)}, bf16[1280,2560]{1,0:T(8,128)(2,1)S(1)}, u32[]{:S(2)}, u32[]{:S(2)}) collective-permute-start(bf16[1280,2560]{1,0:T(8,128)(2,1)} %param.16), channel_id=1, source_target_pairs={{0,1},{1,0},{2,2},{3,3},{4,5},{5,4},{6,6},{7,7},{8,9},{9,8},{10,10... | collective-permute-start | bytes 19660808 | tf_op jit(solution)/shard_map/ppermute | solution.py:355
  5.9 1.2 %shard_map.120 = (bf16[2,128,640]{2,1,0:T(8,128)(2,1)S(1)}, bf16[2,128,640]{2,1,0:T(8,128)(2,1)S(1)}) custom-call(bf16[128,1280]{1,0:T(8,128)(2,1)} %bitcast.18, bf16[128,1280]{1,0:T(8,128)(2,1)} %bitcast.19), custom_call_target="tpu_custom_call" | custom-call | bytes 1310720 | tf_op jit(solution)/shard_map/pallas_call | solution.py:302
  7.8 2.6 %collective-permute-start.3 = (bf16[2,128,640]{2,1,0:T(8,128)(2,1)S(1)}, bf16[2,128,640]{2,1,0:T(8,128)(2,1)S(1)}, u32[]{:S(2)}, u32[]{:S(2)}) collective-permute-start(bf16[2,128,640]{2,1,0:T(8,128)(2,1)S(1)} %get-tuple-element.40), channel_id=1, source_target_pairs={{0,4},{1,12},{4,0},{5,8},{8,5},{9,13},{12,1},{13,9},{2,6},{3,14},{... | collective-permute-start | bytes 983048 | tf_op jit(solution)/shard_map/ppermute | solution.py:351
  10.4 1.0 %shard_map.119 = (bf16[1,128,640]{2,1,0:T(8,128)(2,1)S(1)}, bf16[1,128,640]{2,1,0:T(8,128)(2,1)S(1)}) custom-call(bf16[128,1280]{1,0:T(8,128)(2,1)} %bitcast.20), custom_call_target="tpu_custom_call" | custom-call | bytes 655360 | tf_op jit(solution)/shard_map/pallas_call | solution.py:302
  12.1 14.2 %collective-permute-start.4 = (bf16[2,128,640]{2,1,0:T(8,128)(2,1)S(1)}, bf16[2,128,640]{2,1,0:T(8,128)(2,1)S(1)}, u32[]{:S(2)}, u32[]{:S(2)}) collective-permute-start(bf16[2,128,640]{2,1,0:T(8,128)(2,1)S(1)} %collective-permute-done.2.refs_2_), channel_id=1, source_target_pairs={{0,1},{1,0},{2,3},{3,2},{4,5},{5,4},{6,7},{7,6},{8,9},{9,8},{10,11... | collective-permute-start | bytes 983048 | tf_op jit(solution)/shard_map/ppermute | solution.py:356
  26.3 4.2 %collective-permute-start.1 = (bf16[1,128,640]{2,1,0:T(8,128)(2,1)S(1)}, bf16[1,128,640]{2,1,0:T(8,128)(2,1)S(1)}, u32[]{:S(2)}, u32[]{:S(2)}) collective-permute-start(bf16[1,128,640]{2,1,0:T(8,128)(2,1)S(1)} %get-tuple-element.35), channel_id=1, source_target_pairs={{0,4},{1,12},{4,0},{5,8},{8,5},{9,13},{12,1},{13,9},{2,6},{3,14},{... | collective-permute-start | bytes 491528 | tf_op jit(solution)/shard_map/ppermute | solution.py:353
  31.2 1.0 %copy-done = bf16[2560,64]{0,1:T(8,128)(2,1)S(1)} copy-done((bf16[2560,64]{0,1:T(8,128)(2,1)S(1)}, bf16[2560,64]{0,1:T(8,128)(2,1)}, u32[]{:S(2)}) %copy-start) | copy-done | bytes 327704
  34.2 1.3 %shard_map.118 = (f32[64,128]{1,0:T(8,128)S(1)}, f32[16,128]{1,0:T(8,128)S(1)}, f32[8,128]{1,0:T(8,128)S(1)}) custom-call(f32[1,2560]{1,0:T(1,128)S(1)} %copy-done.4, f32[1,2560]{1,0:T(1,128)S(1)} %copy-done.7, bf16[64,2560]{1,0:T(8,128)(2,1)S(1)} %bitcast.11, s32[1,4]{1,0:T(1,128)S(1)} %copy-done.8, s32[1]{0:T(128)S(6)} %copy.13.steps_ref), custom_call_target="tpu_custom_call" | custom-call | bytes 1310720 | tf_op jit(solution)/shard_map/pallas_call | solution.py:302
  35.6 1.7 %shard_map.121 = (bf16[128,640]{1,0:T(8,128)(2,1)S(1)}, bf16[128,640]{1,0:T(8,128)(2,1)S(1)}) custom-call(bf16[1,128,640]{2,1,0:T(8,128)(2,1)S(1)} %collective-permute-done.refs_0_, bf16[1,128,640]{2,1,0:T(8,128)(2,1)S(1)} %collective-permute-done.1.refs_1_, bf16[2,128,640]{2,1,0:T(8,128)(2,1)S(1)} %collective-permute-done.2.refs_2_, ...), custom_call_target="tpu_custom_call" | custom-call | flops 335544320 | bytes 1966080 | tf_op jit(solution)/shard_map/pallas_call | solution.py:302
  38.3 5.0 %collective-permute-done.7.refs_1_ = bf16[128,640]{1,0:T(8,128)(2,1)S(1)} collective-permute-done((bf16[128,640]{1,0:T(8,128)(2,1)S(1)}, bf16[128,640]{1,0:T(8,128)(2,1)S(1)}, u32[]{:S(2)}, u32[]{:S(2)}) %collective-permute-start.7) | collective-permute-done | bytes 163872 | tf_op jit(solution)/shard_map/ppermute | solution.py:376
  44.0 1.8 %collective-permute-start.13 = (bf16[128,640]{1,0:T(8,128)(2,1)S(1)}, bf16[128,640]{1,0:T(8,128)(2,1)S(1)}, u32[]{:S(2)}, u32[]{:S(2)}) collective-permute-start(bf16[128,640]{1,0:T(8,128)(2,1)S(1)} %shard_map.126), channel_id=1, source_target_pairs={{0,2},{2,0},{1,3},{3,1},{4,6},{6,4},{5,7},{7,5},{8,10},{10,8},{9,1... | collective-permute-start | bytes 491528 | tf_op jit(solution)/shard_map/ppermute | solution.py:390
  47.4 1.8 %collective-permute-start.11 = (bf16[128,640]{1,0:T(8,128)(2,1)S(1)}, bf16[128,640]{1,0:T(8,128)(2,1)S(1)}, u32[]{:S(2)}, u32[]{:S(2)}) collective-permute-start(bf16[128,640]{1,0:T(8,128)(2,1)S(1)} %shard_map.124), channel_id=1, source_target_pairs={{0,2},{2,0},{1,3},{3,1},{4,6},{6,4},{5,7},{7,5},{8,10},{10,8},{9,1... | collective-permute-start | bytes 491528 | tf_op jit(solution)/shard_map/ppermute | solution.py:390
  50.2 2.4 %shard_map.122.refs_0_ = f32[128,2560]{1,0:T(8,128)S(1)} custom-call(bf16[128,640]{1,0:T(8,128)(2,1)S(1)} %collective-permute-done.6.refs_0_, bf16[128,640]{1,0:T(8,128)(2,1)S(1)} %collective-permute-done.7.refs_1_, bf16[1280,2560]{1,0:T(8,128)(2,1)S(1)} %collective-permute-done.8.refs_2_, bf16[1280,2560]{1,0:T(8,128)(2,1)S(1)} %collective-permute-done.9.refs_3_, ...), custom_call_target="tpu_custom_call" | custom-call | flops 838860800 | bytes 6553600 | tf_op jit(solution)/shard_map/pallas_call | solution.py:302
  53.9 1.7 %collective-permute-done.10.refs_1_ = bf16[128,640]{1,0:T(8,128)(2,1)S(1)} collective-permute-done((bf16[128,640]{1,0:T(8,128)(2,1)S(1)}, bf16[128,640]{1,0:T(8,128)(2,1)S(1)}, u32[]{:S(2)}, u32[]{:S(2)}) %collective-permute-start.10) | collective-permute-done | bytes 163872 | tf_op jit(solution)/shard_map/ppermute | solution.py:390
  55.9 0.9 %collective-permute-start.14 = (f32[72,128]{1,0:T(8,128)S(1)}, f32[72,128]{1,0:T(8,128)S(1)}, u32[]{:S(2)}, u32[]{:S(2)}) collective-permute-start(f32[72,128]{1,0:T(8,128)S(1)} %shard_map.130.own_ref), channel_id=1, source_target_pairs={{0,2},{2,0},{1,3},{3,1},{4,6},{6,4},{5,7},{7,5},{8,10},{10,8},{9,1... | collective-permute-start | bytes 110600 | tf_op jit(solution)/shard_map/ppermute | solution.py:411
  56.8 1.2 %collective-permute-start.15 = (f32[64,128]{1,0:T(8,128)S(1)}, f32[64,128]{1,0:T(8,128)S(1)}, u32[]{:S(2)}, u32[]{:S(2)}) collective-permute-start(f32[64,128]{1,0:T(8,128)S(1)} %get-tuple-element.52.rows_own_ref), channel_id=1, source_target_pairs={{0,2},{2,0},{1,3},{3,1},{4,6},{6,4},{5,7},{7,5},{8,10},{10,8},{9,1... | collective-permute-start | bytes 98312 | tf_op jit(solution)/shard_map/ppermute | solution.py:366
  58.0 3.0 %collective-permute-done.15.rows_got_ref = f32[64,128]{1,0:T(8,128)S(1)} collective-permute-done((f32[64,128]{1,0:T(8,128)S(1)}, f32[64,128]{1,0:T(8,128)S(1)}, u32[]{:S(2)}, u32[]{:S(2)}) %collective-permute-start.15) | collective-permute-done | bytes 32800 | tf_op jit(solution)/shard_map/ppermute | solution.py:366
  61.1 6.1 %collective-permute-start.16 = (f32[32,128]{1,0:T(8,128)S(1)}, f32[32,128]{1,0:T(8,128)S(1)}, u32[]{:S(2)}, u32[]{:S(2)}) collective-permute-start(f32[32,128]{1,0:T(8,128)S(1)} %get-tuple-element.54), channel_id=1, source_target_pairs={{0,1},{1,0},{2,3},{3,2},{4,5},{5,4},{6,7},{7,6},{8,9},{9,8},{10,11... | collective-permute-start | bytes 49160 | tf_op jit(solution)/shard_map/ppermute | solution.py:418
  67.2 0.8 %collective-permute-done.16.got_ref = f32[32,128]{1,0:T(8,128)S(1)} collective-permute-done((f32[32,128]{1,0:T(8,128)S(1)}, f32[32,128]{1,0:T(8,128)S(1)}, u32[]{:S(2)}, u32[]{:S(2)}) %collective-permute-start.16) | collective-permute-done | bytes 16416 | tf_op jit(solution)/shard_map/ppermute | solution.py:418
  68.1 2.7 %collective-permute-start.17 = (f32[8,128]{1,0:T(8,128)S(1)}, f32[8,128]{1,0:T(8,128)S(1)}, u32[]{:S(2)}, u32[]{:S(2)}) collective-permute-start(f32[8,128]{1,0:T(8,128)S(1)} %get-tuple-element.56), channel_id=1, source_target_pairs={{0,4},{4,0},{8,12},{12,8},{1,5},{5,1},{9,13},{13,9},{2,6},{6,2},{1... | collective-permute-start | bytes 12296 | tf_op jit(solution)/shard_map/ppermute | solution.py:426
  70.8 2.8 %collective-permute-start.18 = (f32[8,128]{1,0:T(8,128)S(1)}, f32[8,128]{1,0:T(8,128)S(1)}, u32[]{:S(2)}, u32[]{:S(2)}) collective-permute-start(f32[8,128]{1,0:T(8,128)S(1)} %get-tuple-element.57), channel_id=1, source_target_pairs={{0,8},{4,12},{8,0},{12,4},{1,9},{5,13},{9,1},{13,5},{2,10},{6,14},... | collective-permute-start | bytes 12296 | tf_op jit(solution)/shard_map/ppermute | solution.py:426
  73.6 1.0 %collective-permute-start.19 = (f32[8,128]{1,0:T(8,128)S(1)}, f32[8,128]{1,0:T(8,128)S(1)}, u32[]{:S(2)}, u32[]{:S(2)}) collective-permute-start(f32[8,128]{1,0:T(8,128)S(1)} %get-tuple-element.58), channel_id=1, source_target_pairs={{0,12},{4,8},{8,4},{12,0},{1,13},{5,9},{9,5},{13,1},{2,14},{6,10},... | collective-permute-start | bytes 12296 | tf_op jit(solution)/shard_map/ppermute | solution.py:426
  75.3 3.7 %collective-permute-done.19.refs_3_ = f32[8,128]{1,0:T(8,128)S(1)} collective-permute-done((f32[8,128]{1,0:T(8,128)S(1)}, f32[8,128]{1,0:T(8,128)S(1)}, u32[]{:S(2)}, u32[]{:S(2)}) %collective-permute-start.19) | collective-permute-done | bytes 4128 | tf_op jit(solution)/shard_map/ppermute | solution.py:426
  (50 shorter events, 10.9 us)
Async XLA Ops:
  0.0 43.3 %collective-permute-start.8 = (bf16[1280,2560]{1,0:T(8,128)(2,1)}, bf16[1280,2560]{1,0:T(8,128)(2,1)S(1)}, u32[]{:S(2)}, u32[]{:S(2)}) collective-permute-start(bf16[1280,2560]{1,0:T(8,128)(2,1)} %param.16), channel_id=1, source_target_pairs={{0,0},{1,1},{2,3},{3,2},{4,4},{5,5},{6,7},{7,6},{8,8},{9,9},{10,11... | collective-permute-start | bytes 19660808 | tf_op jit(solution)/shard_map/ppermute | solution.py:354
  3.5 39.8 %collective-permute-start.9 = (bf16[1280,2560]{1,0:T(8,128)(2,1)}, bf16[1280,2560]{1,0:T(8,128)(2,1)S(1)}, u32[]{:S(2)}, u32[]{:S(2)}) collective-permute-start(bf16[1280,2560]{1,0:T(8,128)(2,1)} %param.16), channel_id=1, source_target_pairs={{0,1},{1,0},{2,2},{3,3},{4,5},{5,4},{6,6},{7,7},{8,9},{9,8},{10,10... | collective-permute-start | bytes 19660808 | tf_op jit(solution)/shard_map/ppermute | solution.py:355
  7.1 5.0 %collective-permute-start.2 = (bf16[2,128,640]{2,1,0:T(8,128)(2,1)S(1)}, bf16[2,128,640]{2,1,0:T(8,128)(2,1)S(1)}, u32[]{:S(2)}, u32[]{:S(2)}) collective-permute-start(bf16[2,128,640]{2,1,0:T(8,128)(2,1)S(1)} %get-tuple-element.39), channel_id=1, source_target_pairs={{0,0},{1,8},{4,4},{5,12},{8,1},{9,9},{12,5},{13,13},{2,2},{3,10},{... | collective-permute-start | bytes 983048 | tf_op jit(solution)/shard_map/ppermute | solution.py:351
  7.8 18.5 %collective-permute-start.3 = (bf16[2,128,640]{2,1,0:T(8,128)(2,1)S(1)}, bf16[2,128,640]{2,1,0:T(8,128)(2,1)S(1)}, u32[]{:S(2)}, u32[]{:S(2)}) collective-permute-start(bf16[2,128,640]{2,1,0:T(8,128)(2,1)S(1)} %get-tuple-element.40), channel_id=1, source_target_pairs={{0,4},{1,12},{4,0},{5,8},{8,5},{9,13},{12,1},{13,9},{2,6},{3,14},{... | collective-permute-start | bytes 983048 | tf_op jit(solution)/shard_map/ppermute | solution.py:351
  11.5 14.9 %collective-permute-start = (bf16[1,128,640]{2,1,0:T(8,128)(2,1)S(1)}, bf16[1,128,640]{2,1,0:T(8,128)(2,1)S(1)}, u32[]{:S(2)}, u32[]{:S(2)}) collective-permute-start(bf16[1,128,640]{2,1,0:T(8,128)(2,1)S(1)} %get-tuple-element.34), channel_id=1, source_target_pairs={{0,0},{1,8},{4,4},{5,12},{8,1},{9,9},{12,5},{13,13},{2,2},{3,10},{... | collective-permute-start | bytes 491528 | tf_op jit(solution)/shard_map/ppermute | solution.py:353
  12.1 23.4 %collective-permute-start.4 = (bf16[2,128,640]{2,1,0:T(8,128)(2,1)S(1)}, bf16[2,128,640]{2,1,0:T(8,128)(2,1)S(1)}, u32[]{:S(2)}, u32[]{:S(2)}) collective-permute-start(bf16[2,128,640]{2,1,0:T(8,128)(2,1)S(1)} %collective-permute-done.2.refs_2_), channel_id=1, source_target_pairs={{0,1},{1,0},{2,3},{3,2},{4,5},{5,4},{6,7},{7,6},{8,9},{9,8},{10,11... | collective-permute-start | bytes 983048 | tf_op jit(solution)/shard_map/ppermute | solution.py:356
  26.3 9.3 %collective-permute-start.5 = (bf16[2,128,640]{2,1,0:T(8,128)(2,1)S(1)}, bf16[2,128,640]{2,1,0:T(8,128)(2,1)S(1)}, u32[]{:S(2)}, u32[]{:S(2)}) collective-permute-start(bf16[2,128,640]{2,1,0:T(8,128)(2,1)S(1)} %collective-permute-done.3.refs_3_), channel_id=1, source_target_pairs={{0,1},{1,0},{2,3},{3,2},{4,5},{5,4},{6,7},{7,6},{8,9},{9,8},{10,11... | collective-permute-start | bytes 983048 | tf_op jit(solution)/shard_map/ppermute | solution.py:356
  26.3 9.2 %collective-permute-start.1 = (bf16[1,128,640]{2,1,0:T(8,128)(2,1)S(1)}, bf16[1,128,640]{2,1,0:T(8,128)(2,1)S(1)}, u32[]{:S(2)}, u32[]{:S(2)}) collective-permute-start(bf16[1,128,640]{2,1,0:T(8,128)(2,1)S(1)} %get-tuple-element.35), channel_id=1, source_target_pairs={{0,4},{1,12},{4,0},{5,8},{8,5},{9,13},{12,1},{13,9},{2,6},{3,14},{... | collective-permute-start | bytes 491528 | tf_op jit(solution)/shard_map/ppermute | solution.py:353
  37.2 1.0 %collective-permute-start.6 = (bf16[128,640]{1,0:T(8,128)(2,1)S(1)}, bf16[128,640]{1,0:T(8,128)(2,1)S(1)}, u32[]{:S(2)}, u32[]{:S(2)}) collective-permute-start(bf16[128,640]{1,0:T(8,128)(2,1)S(1)} %get-tuple-element.41), channel_id=1, source_target_pairs={{0,0},{8,1},{4,4},{12,5},{1,8},{9,9},{5,12},{13,13},{2,2},{10,3},{... | collective-permute-start | bytes 491528 | tf_op jit(solution)/shard_map/ppermute | solution.py:376
  37.9 5.4 %collective-permute-start.7 = (bf16[128,640]{1,0:T(8,128)(2,1)S(1)}, bf16[128,640]{1,0:T(8,128)(2,1)S(1)}, u32[]{:S(2)}, u32[]{:S(2)}) collective-permute-start(bf16[128,640]{1,0:T(8,128)(2,1)S(1)} %get-tuple-element.42), channel_id=1, source_target_pairs={{4,0},{12,1},{0,4},{8,5},{5,8},{13,9},{1,12},{9,13},{6,2},{14,3},{... | collective-permute-start | bytes 491528 | tf_op jit(solution)/shard_map/ppermute | solution.py:376
  44.0 8.7 %collective-permute-start.13 = (bf16[128,640]{1,0:T(8,128)(2,1)S(1)}, bf16[128,640]{1,0:T(8,128)(2,1)S(1)}, u32[]{:S(2)}, u32[]{:S(2)}) collective-permute-start(bf16[128,640]{1,0:T(8,128)(2,1)S(1)} %shard_map.126), channel_id=1, source_target_pairs={{0,2},{2,0},{1,3},{3,1},{4,6},{6,4},{5,7},{7,5},{8,10},{10,8},{9,1... | collective-permute-start | bytes 491528 | tf_op jit(solution)/shard_map/ppermute | solution.py:390
  46.4 6.6 %collective-permute-start.12 = (bf16[128,640]{1,0:T(8,128)(2,1)S(1)}, bf16[128,640]{1,0:T(8,128)(2,1)S(1)}, u32[]{:S(2)}, u32[]{:S(2)}) collective-permute-start(bf16[128,640]{1,0:T(8,128)(2,1)S(1)} %shard_map.125), channel_id=1, source_target_pairs={{0,2},{2,0},{1,3},{3,1},{4,6},{6,4},{5,7},{7,5},{8,10},{10,8},{9,1... | collective-permute-start | bytes 491528 | tf_op jit(solution)/shard_map/ppermute | solution.py:390
  47.4 2.8 %copy-start.2 = (bf16[1,1,128,2560]{3,2,1,0:T(8,128)(2,1)S(1)}, bf16[1,1,128,2560]{3,2,1,0:T(8,128)(2,1)}, u32[]{:S(2)}) copy-start(bf16[1,1,128,2560]{3,2,1,0:T(8,128)(2,1)} %param.15) | copy-start | bytes 1966084
  47.4 2.8 %copy-start.3 = (f32[1,2560]{1,0:T(1,128)S(1)}, f32[1,2560]{1,0:T(1,128)}, u32[]{:S(2)}) copy-start(f32[1,2560]{1,0:T(1,128)} %refs_2_.7) | copy-start | bytes 30724
  47.4 6.1 %collective-permute-start.11 = (bf16[128,640]{1,0:T(8,128)(2,1)S(1)}, bf16[128,640]{1,0:T(8,128)(2,1)S(1)}, u32[]{:S(2)}, u32[]{:S(2)}) collective-permute-start(bf16[128,640]{1,0:T(8,128)(2,1)S(1)} %shard_map.124), channel_id=1, source_target_pairs={{0,2},{2,0},{1,3},{3,1},{4,6},{6,4},{5,7},{7,5},{8,10},{10,8},{9,1... | collective-permute-start | bytes 491528 | tf_op jit(solution)/shard_map/ppermute | solution.py:390
  49.9 5.7 %collective-permute-start.10 = (bf16[128,640]{1,0:T(8,128)(2,1)S(1)}, bf16[128,640]{1,0:T(8,128)(2,1)S(1)}, u32[]{:S(2)}, u32[]{:S(2)}) collective-permute-start(bf16[128,640]{1,0:T(8,128)(2,1)S(1)} %shard_map.123), channel_id=1, source_target_pairs={{0,2},{2,0},{1,3},{3,1},{4,6},{6,4},{5,7},{7,5},{8,10},{10,8},{9,1... | collective-permute-start | bytes 491528 | tf_op jit(solution)/shard_map/ppermute | solution.py:390
  50.2 2.4 %copy-start.5 = (f32[1,2560]{1,0:T(1,128)S(1)}, f32[1,2560]{1,0:T(1,128)}, u32[]{:S(2)}) copy-start(f32[1,2560]{1,0:T(1,128)} %refs_3_.7) | copy-start | bytes 30724
  52.6 26.4 %copy-start.6 = (f32[1,1,128,32]{2,3,1,0:T(8,128)S(1)}, f32[1,1,128,32]{2,3,1,0:T(8,128)}, u32[]{:S(2)}) copy-start(f32[1,1,128,32]{2,3,1,0:T(8,128)} %param.21) | copy-start | bytes 49156
  55.9 5.1 %collective-permute-start.14 = (f32[72,128]{1,0:T(8,128)S(1)}, f32[72,128]{1,0:T(8,128)S(1)}, u32[]{:S(2)}, u32[]{:S(2)}) collective-permute-start(f32[72,128]{1,0:T(8,128)S(1)} %shard_map.130.own_ref), channel_id=1, source_target_pairs={{0,2},{2,0},{1,3},{3,1},{4,6},{6,4},{5,7},{7,5},{8,10},{10,8},{9,1... | collective-permute-start | bytes 110600 | tf_op jit(solution)/shard_map/ppermute | solution.py:411
  56.8 4.3 %collective-permute-start.15 = (f32[64,128]{1,0:T(8,128)S(1)}, f32[64,128]{1,0:T(8,128)S(1)}, u32[]{:S(2)}, u32[]{:S(2)}) collective-permute-start(f32[64,128]{1,0:T(8,128)S(1)} %get-tuple-element.52.rows_own_ref), channel_id=1, source_target_pairs={{0,2},{2,0},{1,3},{3,1},{4,6},{6,4},{5,7},{7,5},{8,10},{10,8},{9,1... | collective-permute-start | bytes 98312 | tf_op jit(solution)/shard_map/ppermute | solution.py:366
  61.1 6.9 %collective-permute-start.16 = (f32[32,128]{1,0:T(8,128)S(1)}, f32[32,128]{1,0:T(8,128)S(1)}, u32[]{:S(2)}, u32[]{:S(2)}) collective-permute-start(f32[32,128]{1,0:T(8,128)S(1)} %get-tuple-element.54), channel_id=1, source_target_pairs={{0,1},{1,0},{2,3},{3,2},{4,5},{5,4},{6,7},{7,6},{8,9},{9,8},{10,11... | collective-permute-start | bytes 49160 | tf_op jit(solution)/shard_map/ppermute | solution.py:418
  68.1 6.5 %collective-permute-start.17 = (f32[8,128]{1,0:T(8,128)S(1)}, f32[8,128]{1,0:T(8,128)S(1)}, u32[]{:S(2)}, u32[]{:S(2)}) collective-permute-start(f32[8,128]{1,0:T(8,128)S(1)} %get-tuple-element.56), channel_id=1, source_target_pairs={{0,4},{4,0},{8,12},{12,8},{1,5},{5,1},{9,13},{13,9},{2,6},{6,2},{1... | collective-permute-start | bytes 12296 | tf_op jit(solution)/shard_map/ppermute | solution.py:426
  70.8 4.5 %collective-permute-start.18 = (f32[8,128]{1,0:T(8,128)S(1)}, f32[8,128]{1,0:T(8,128)S(1)}, u32[]{:S(2)}, u32[]{:S(2)}) collective-permute-start(f32[8,128]{1,0:T(8,128)S(1)} %get-tuple-element.57), channel_id=1, source_target_pairs={{0,8},{4,12},{8,0},{12,4},{1,9},{5,13},{9,1},{13,5},{2,10},{6,14},... | collective-permute-start | bytes 12296 | tf_op jit(solution)/shard_map/ppermute | solution.py:426
  73.6 5.4 %collective-permute-start.19 = (f32[8,128]{1,0:T(8,128)S(1)}, f32[8,128]{1,0:T(8,128)S(1)}, u32[]{:S(2)}, u32[]{:S(2)}) collective-permute-start(f32[8,128]{1,0:T(8,128)S(1)} %get-tuple-element.58), channel_id=1, source_target_pairs={{0,12},{4,8},{8,4},{12,0},{1,13},{5,9},{9,5},{13,1},{2,14},{6,10},... | collective-permute-start | bytes 12296 | tf_op jit(solution)/shard_map/ppermute | solution.py:426
  (5 other events, 5.4 us)

commit v4 on v3

--- a/solution.py
+++ b/solution.py
@@ -120,23 +120,28 @@
         copy.wait()
 
 
-def attend_kernel(parts, *refs):
-    q_refs = refs[:parts]
-    kv_refs = refs[parts : 3 * parts]
-    o_refs = refs[3 * parts :]
-    rows = q_refs[0].shape[1]
-    for i in range(q_refs[0].shape[2] // HEAD_DIM):
+def attend_kernel(blocks, q_ref, *refs):
+    kv_refs, out_ref, score_scr, total_scr = refs[:blocks], refs[blocks], refs[blocks + 1], refs[blocks + 2]
+    heads = q_ref.shape[2] // HEAD_DIM
+    rows = kv_refs[0].shape[1]
+    for i in range(heads):
         cols = slice(i * HEAD_DIM, (i + 1) * HEAD_DIM)
-        q = jnp.concatenate([r[0, :, cols] for r in q_refs], axis=0)
-        k = jnp.concatenate([r[0, :, cols] for r in kv_refs], axis=0)
-        v = jnp.concatenate([r[1, :, cols] for r in kv_refs], axis=0)
-        scores = lax.dot_general(q, k, (((1,), (1,)), ((), ())), preferred_element_type=F32)
-        scores = scores * (HEAD_DIM ** (-0.5) * LOG2E)
+        q = q_ref[0, :, cols]
+        for b in range(blocks):
+            scores = lax.dot_general(
+                q, kv_refs[b][0, :, cols], (((1,), (1,)), ((), ())), preferred_element_type=F32
+            )
+            score_scr[i, :, b * rows : (b + 1) * rows] = scores * (HEAD_DIM ** (-0.5) * LOG2E)
+    for i in range(heads):
+        scores = score_scr[i]
         expo = jnp.exp2(scores - jnp.max(scores, axis=1, keepdims=True))
-        total = jnp.sum(expo, axis=1, keepdims=True)
-        mixed = jnp.dot(expo.astype(BF16), v, preferred_element_type=F32) / total
-        for j in range(parts):
-            o_refs[j][:, cols] = mixed[j * rows : (j + 1) * rows].astype(BF16)
+        score_scr[i] = expo
+        total_scr[i] = jnp.broadcast_to(jnp.sum(expo, axis=1, keepdims=True), total_scr.shape[1:])
+    for i in range(heads):
+        cols = slice(i * HEAD_DIM, (i + 1) * HEAD_DIM)
+        values = jnp.concatenate([r[1, :, cols] for r in kv_refs], axis=0)
+        mixed = jnp.dot(score_scr[i].astype(BF16), values, preferred_element_type=F32)
+        out_ref[:, cols] = (mixed / total_scr[i]).astype(BF16)
 
 
 def project(parts, half, o_refs, w_ref, cols):
@@ -364,28 +369,34 @@
         moved=4 * width_shard * LANES,
     )
     rows_got = lax.ppermute(rows_own, "shard", both)
-    *q_own, rows_own = lax.optimization_barrier((*q_own, rows_own))
-
-    mixed = call(
-        functools.partial(attend_kernel, parts),
-        [((rows, half), BF16)] * parts,
-        q_own + kv_own + kv_other,
-        flops=8 * rows * parts * rows * parts * half,
-        moved=2 * rows * half * parts * 6,
-    )
-    mixed = [lax.ppermute(mixed[j], axes, back[j]) for j in range(parts)]
+    q_own[0], rows_own = lax.optimization_barrier((q_own[0], rows_own))
+
+    mixed = []
+    for j in range(parts):
+        block = call(
+            functools.partial(attend_kernel, 2 * parts),
+            [((rows, half), BF16)],
+            [q_own[j]] + kv_own + kv_other,
+            scratch=[
+                pltpu.VMEM((half // HEAD_DIM, rows, 2 * parts * rows), F32),
+                pltpu.VMEM((half // HEAD_DIM, rows, HEAD_DIM), F32),
+            ],
+            flops=8 * rows * rows * parts * half,
+            moved=2 * rows * half * parts * 5,
+        )[0]
+        mixed.append(lax.ppermute(block, axes, back[j]))
 
     chunk = 128
-    pieces = 4
-    width_piece = width_shard // pieces
+    quarter = width_shard // 4
+    pieces = [(0, quarter), (quarter, 2 * quarter), (3 * quarter, quarter)]
     got = []
-    for i in range(pieces):
+    for start, width in pieces:
         partial = call(
-            functools.partial(send_kernel, parts, half, chunk, i * width_piece),
-            [((rows, width_piece), BF16)],
+            functools.partial(send_kernel, parts, half, chunk, start),
+            [((rows, width), BF16)],
             mixed + [near_w, far_w],
-            flops=2 * rows * width_local * width_piece,
-            moved=2 * width_local * width_piece,
+            flops=2 * rows * width_local * width,
+            moved=2 * width_local * width,
         )[0]
         got.append(lax.ppermute(partial, "shard", both))
     hidden = call(
@@ -396,16 +407,16 @@
         moved=2 * width_local * width_shard,
     )[0]
     state = []
-    for i in range(pieces):
-        first, last = i == 0, i == pieces - 1
+    for i, (start, width) in enumerate(pieces):
+        first, last = i == 0, i == len(pieces) - 1
         state = call(
-            functools.partial(head_kernel, first, last, chunk, i * width_piece),
+            functools.partial(head_kernel, first, last, chunk, start),
             [((channels + SUBLANES, rows), F32)]
             if last
             else [((channels, rows), F32), ((rows, LANES), F32), ((rows, LANES), F32)],
             [hidden, got[i], attn_gate, norm_scale, head_t] + list(state),
-            flops=4 * rows * channels * width_piece,
-            moved=6 * rows * width_piece,
+            flops=4 * rows * channels * width,
+            moved=6 * rows * width,
         )
     sums = state[0]
     sums_got = lax.ppermute(sums, "shard", both)

time: 80.1 us -> 84.4 us (1.054)
  starting transfers between devices: 48.2 us -> 51.6 us
  waiting for transfers between devices: 15.2 us -> 16.8 us
    ppermute x1, starting transfers between devices: 6.08 us -> 9.22 us  [fast_plan(): eps_got = lax.ppermute(send, 'guide', both)]
    ppermute x1, starting transfers between devices: 0.86 us -> 2.08 us  [fast_plan(): sums_got = lax.ppermute(sums, 'shard', both)]
    ppermute x1, waiting for transfers between devices: 3.02 us -> 4.19 us  [fast_plan(): rows_got = lax.ppermute(rows_own, 'shard', both)]
    ppermute x1, starting transfers between devices: 1.24 us -> 0.08 us  [fast_plan(): rows_got = lax.ppermute(rows_own, 'shard', both)]
    pallas_call x16 -> x15, Pallas kernels: 12.3 us -> 11.7 us  [call(): pl.pallas_call(kernel, out_shape=shapes, in_specs=specs or [VMEM_SPEC] *...]
    ppermute x4 -> x3, waiting for transfers between devices: 1.87 us -> 2.27 us  [fast_plan(): got.append(lax.ppermute(partial, 'shard', both))]
    ppermute x4 -> x3, starting transfers between devices: 4.31 us -> 4.24 us  [fast_plan(): got.append(lax.ppermute(partial, 'shard', both))]
  transfers between devices with their start and end apart: 20 -> 19, of which waited for: 7 -> 7; matrix products, arithmetic and copies ran while one was open for 0% -> 0% of each run, Pallas kernels for 13% -> 11%
where the time goes in v4:
time: 84.4 us; the launch traced here: 84 us
  starting transfers between devices  51.6 us (61%)
  waiting for transfers between devices  16.8 us (20%)
  Pallas kernels  11.7 us (14%)
  local copies, waits for them, and re-layouts  3.05 us (4%)
  between operations  0.87 us (1%)
    ppermute x2, starting transfers between devices, fast_plan(): kv_other = [lax.ppermute(block, 'guide', both) for block in kv_own]  14.1 us
    pallas_call x15, Pallas kernels, call(): pl.pallas_call(kernel, out_shape=shapes, in_specs=specs or [VMEM_SPEC] *...  11.7 us
    ppermute x1, starting transfers between devices, fast_plan(): eps_got = lax.ppermute(send, 'guide', both)  9.22 us
    ppermute x3, starting transfers between devices, fast_plan(): lax.ppermute(frames[k], 'seq', [(z, z ^ k) for z in range(seq_count)])  6.95 us
    ppermute x2, waiting for transfers between devices, fast_plan(): mixed.append(lax.ppermute(block, axes, back[j]))  5.41 us
    ppermute x2, starting transfers between devices, fast_plan(): q_own = [lax.ppermute(q_sent[j], axes, there[j]) for j in range(parts)]  4.97 us
    ppermute x3, starting transfers between devices, fast_plan(): got.append(lax.ppermute(partial, 'shard', both))  4.24 us
    ppermute x1, waiting for transfers between devices, fast_plan(): rows_got = lax.ppermute(rows_own, 'shard', both)  4.19 us
  transfers between devices with their start and end apart: 19, of which 7 were waited for; matrix products, arithmetic and copies ran while one was open for 0% of the time, Pallas kernels for 11%

profile of v4, /device:TPU:0, one launch (start us, length us, event | category | flops | bytes accessed | tf_op | source)
XLA Modules:
  0.0 84.0 jit_solution(6184933674042933327)
XLA Ops:
  0.0 2.4 %collective-permute-start.9 = (bf16[1280,2560]{1,0:T(8,128)(2,1)}, bf16[1280,2560]{1,0:T(8,128)(2,1)S(1)}, u32[]{:S(2)}, u32[]{:S(2)}) collective-permute-start(bf16[1280,2560]{1,0:T(8,128)(2,1)} %param.16), channel_id=1, source_target_pairs={{0,1},{1,0},{2,2},{3,3},{4,5},{5,4},{6,6},{7,7},{8,9},{9,8},{10,10... | collective-permute-start | bytes 19660808 | tf_op jit(solution)/shard_map/ppermute | solution.py:360
  2.4 3.5 %collective-permute-start.8 = (bf16[1280,2560]{1,0:T(8,128)(2,1)}, bf16[1280,2560]{1,0:T(8,128)(2,1)S(1)}, u32[]{:S(2)}, u32[]{:S(2)}) collective-permute-start(bf16[1280,2560]{1,0:T(8,128)(2,1)} %param.16), channel_id=1, source_target_pairs={{0,0},{1,1},{2,3},{3,2},{4,4},{5,5},{6,7},{7,6},{8,8},{9,9},{10,11... | collective-permute-start | bytes 19660808 | tf_op jit(solution)/shard_map/ppermute | solution.py:359
  5.9 1.2 %shard_map.120 = (bf16[2,128,640]{2,1,0:T(8,128)(2,1)S(1)}, bf16[2,128,640]{2,1,0:T(8,128)(2,1)S(1)}) custom-call(bf16[128,1280]{1,0:T(8,128)(2,1)} %bitcast.17, bf16[128,1280]{1,0:T(8,128)(2,1)} %bitcast.18), custom_call_target="tpu_custom_call" | custom-call | bytes 1310720 | tf_op jit(solution)/shard_map/pallas_call | solution.py:307
  7.8 2.6 %collective-permute-start.2 = (bf16[2,128,640]{2,1,0:T(8,128)(2,1)S(1)}, bf16[2,128,640]{2,1,0:T(8,128)(2,1)S(1)}, u32[]{:S(2)}, u32[]{:S(2)}) collective-permute-start(bf16[2,128,640]{2,1,0:T(8,128)(2,1)S(1)} %get-tuple-element.32), channel_id=1, source_target_pairs={{0,4},{1,12},{4,0},{5,8},{8,5},{9,13},{12,1},{13,9},{2,6},{3,14},{... | collective-permute-start | bytes 983048 | tf_op jit(solution)/shard_map/ppermute | solution.py:356
  10.4 14.1 %collective-permute-start.3 = (bf16[2,128,640]{2,1,0:T(8,128)(2,1)S(1)}, bf16[2,128,640]{2,1,0:T(8,128)(2,1)S(1)}, u32[]{:S(2)}, u32[]{:S(2)}) collective-permute-start(bf16[2,128,640]{2,1,0:T(8,128)(2,1)S(1)} %collective-permute-done.1.refs_0_), channel_id=1, source_target_pairs={{0,1},{1,0},{2,3},{3,2},{4,5},{5,4},{6,7},{7,6},{8,9},{9,8},{10,11... | collective-permute-start | bytes 983048 | tf_op jit(solution)/shard_map/ppermute | solution.py:361
  24.5 1.0 %shard_map.119 = (bf16[1,128,640]{2,1,0:T(8,128)(2,1)S(1)}, bf16[1,128,640]{2,1,0:T(8,128)(2,1)S(1)}) custom-call(bf16[128,1280]{1,0:T(8,128)(2,1)} %bitcast.19), custom_call_target="tpu_custom_call" | custom-call | bytes 655360 | tf_op jit(solution)/shard_map/pallas_call | solution.py:307
  26.2 4.3 %collective-permute-start.6 = (bf16[1,128,640]{2,1,0:T(8,128)(2,1)S(1)}, bf16[1,128,640]{2,1,0:T(8,128)(2,1)S(1)}, u32[]{:S(2)}, u32[]{:S(2)}) collective-permute-start(bf16[1,128,640]{2,1,0:T(8,128)(2,1)S(1)} %get-tuple-element.33), channel_id=1, source_target_pairs={{0,4},{1,12},{4,0},{5,8},{8,5},{9,13},{12,1},{13,9},{2,6},{3,14},{... | collective-permute-start | bytes 491528 | tf_op jit(solution)/shard_map/ppermute | solution.py:358
  31.2 1.0 %copy-done = bf16[2560,64]{0,1:T(8,128)(2,1)S(1)} copy-done((bf16[2560,64]{0,1:T(8,128)(2,1)S(1)}, bf16[2560,64]{0,1:T(8,128)(2,1)}, u32[]{:S(2)}) %copy-start) | copy-done | bytes 327704
  34.2 1.3 %shard_map.118 = (f32[64,128]{1,0:T(8,128)S(1)}, f32[16,128]{1,0:T(8,128)S(1)}, f32[8,128]{1,0:T(8,128)S(1)}) custom-call(f32[1,2560]{1,0:T(1,128)S(1)} %copy-done.4, f32[1,2560]{1,0:T(1,128)S(1)} %copy-done.7, bf16[64,2560]{1,0:T(8,128)(2,1)S(1)} %bitcast.11, s32[1,4]{1,0:T(1,128)S(1)} %copy-done.8, s32[1]{0:T(128)S(6)} %copy.13.steps_ref), custom_call_target="tpu_custom_call" | custom-call | bytes 1310720 | tf_op jit(solution)/shard_map/pallas_call | solution.py:307
  35.6 0.9 %shard_map.121 = bf16[128,640]{1,0:T(8,128)(2,1)S(1)} custom-call(bf16[1,128,640]{2,1,0:T(8,128)(2,1)S(1)} %collective-permute-done.q_ref, bf16[2,128,640]{2,1,0:T(8,128)(2,1)S(1)} %collective-permute-done.1.refs_0_, bf16[2,128,640]{2,1,0:T(8,128)(2,1)S(1)} %collective-permute-done.2.refs_1_, bf16[2,128,640]{2,1,0:T(8,128)(2,1)S(1)} %collective-permute-done.3.refs_2_, ...), custom_call_target="tpu_custom_call" | custom-call | flops 167772160 | bytes 1638400 | tf_op jit(solution)/shard_map/pallas_call | solution.py:307
  37.2 0.9 %shard_map.122 = bf16[128,640]{1,0:T(8,128)(2,1)S(1)} custom-call(bf16[1,128,640]{2,1,0:T(8,128)(2,1)S(1)} %collective-permute-done.6.q_ref, bf16[2,128,640]{2,1,0:T(8,128)(2,1)S(1)} %collective-permute-done.1.refs_0_, bf16[2,128,640]{2,1,0:T(8,128)(2,1)S(1)} %collective-permute-done.2.refs_1_, bf16[2,128,640]{2,1,0:T(8,128)(2,1)S(1)} %collective-permute-done.3.refs_2_, ...), custom_call_target="tpu_custom_call" | custom-call | flops 167772160 | bytes 1638400 | tf_op jit(solution)/shard_map/pallas_call | solution.py:307
  38.2 5.4 %collective-permute-done.7.refs_1_ = bf16[128,640]{1,0:T(8,128)(2,1)S(1)} collective-permute-done((bf16[128,640]{1,0:T(8,128)(2,1)S(1)}, bf16[128,640]{1,0:T(8,128)(2,1)S(1)}, u32[]{:S(2)}, u32[]{:S(2)}) %collective-permute-start.7) | collective-permute-done | bytes 163872 | tf_op jit(solution)/shard_map/ppermute | solution.py:387
  43.6 1.1 %shard_map.125 = bf16[128,1280]{1,0:T(8,128)(2,1)S(1)} custom-call(bf16[128,640]{1,0:T(8,128)(2,1)S(1)} %collective-permute-done.5.refs_0_, bf16[128,640]{1,0:T(8,128)(2,1)S(1)} %collective-permute-done.7.refs_1_, bf16[1280,2560]{1,0:T(8,128)(2,1)S(1)} %collective-permute-done.8.refs_2_, bf16[1280,2560]{1,0:T(8,128)(2,1)S(1)} %collective-permute-done.9.refs_3_), custom_call_target="tpu_custom_call" | custom-call | flops 419430400 | bytes 3276800 | tf_op jit(solution)/shard_map/pallas_call | solution.py:307
  44.7 2.1 %collective-permute-start.11 = (bf16[128,1280]{1,0:T(8,128)(2,1)S(1)}, bf16[128,1280]{1,0:T(8,128)(2,1)S(1)}, u32[]{:S(2)}, u32[]{:S(2)}) collective-permute-start(bf16[128,1280]{1,0:T(8,128)(2,1)S(1)} %shard_map.125), channel_id=1, source_target_pairs={{0,2},{2,0},{1,3},{3,1},{4,6},{6,4},{5,7},{7,5},{8,10},{10,8},{9,1... | collective-permute-start | bytes 983048 | tf_op jit(solution)/shard_map/ppermute | solution.py:401
  48.2 2.0 %collective-permute-start.10 = (bf16[128,640]{1,0:T(8,128)(2,1)S(1)}, bf16[128,640]{1,0:T(8,128)(2,1)S(1)}, u32[]{:S(2)}, u32[]{:S(2)}) collective-permute-start(bf16[128,640]{1,0:T(8,128)(2,1)S(1)} %shard_map.124), channel_id=1, source_target_pairs={{0,2},{2,0},{1,3},{3,1},{4,6},{6,4},{5,7},{7,5},{8,10},{10,8},{9,1... | collective-permute-start | bytes 491528 | tf_op jit(solution)/shard_map/ppermute | solution.py:401
  50.3 1.9 %shard_map.123.refs_0_ = f32[128,2560]{1,0:T(8,128)S(1)} custom-call(bf16[128,640]{1,0:T(8,128)(2,1)S(1)} %collective-permute-done.5.refs_0_, bf16[128,640]{1,0:T(8,128)(2,1)S(1)} %collective-permute-done.7.refs_1_, bf16[1280,2560]{1,0:T(8,128)(2,1)S(1)} %collective-permute-done.8.refs_2_, bf16[1280,2560]{1,0:T(8,128)(2,1)S(1)} %collective-permute-done.9.refs_3_, ...), custom_call_target="tpu_custom_call" | custom-call | flops 838860800 | bytes 6553600 | tf_op jit(solution)/shard_map/pallas_call | solution.py:307
  52.2 1.4 %collective-permute-done.12.refs_1_ = bf16[128,640]{1,0:T(8,128)(2,1)S(1)} collective-permute-done((bf16[128,640]{1,0:T(8,128)(2,1)S(1)}, bf16[128,640]{1,0:T(8,128)(2,1)S(1)}, u32[]{:S(2)}, u32[]{:S(2)}) %collective-permute-start.12) | collective-permute-done | bytes 163872 | tf_op jit(solution)/shard_map/ppermute | solution.py:401
  55.7 2.1 %collective-permute-start.13 = (f32[72,128]{1,0:T(8,128)S(1)}, f32[72,128]{1,0:T(8,128)S(1)}, u32[]{:S(2)}, u32[]{:S(2)}) collective-permute-start(f32[72,128]{1,0:T(8,128)S(1)} %shard_map.129.own_ref), channel_id=1, source_target_pairs={{0,2},{2,0},{1,3},{3,1},{4,6},{6,4},{5,7},{7,5},{8,10},{10,8},{9,1... | collective-permute-start | bytes 110600 | tf_op jit(solution)/shard_map/ppermute | solution.py:422
  57.9 4.2 %collective-permute-done.14.rows_got_ref = f32[64,128]{1,0:T(8,128)S(1)} collective-permute-done((f32[64,128]{1,0:T(8,128)S(1)}, f32[64,128]{1,0:T(8,128)S(1)}, u32[]{:S(2)}, u32[]{:S(2)}) %collective-permute-start.14) | collective-permute-done | bytes 32800 | tf_op jit(solution)/shard_map/ppermute | solution.py:371
  62.1 9.2 %collective-permute-start.15 = (f32[32,128]{1,0:T(8,128)S(1)}, f32[32,128]{1,0:T(8,128)S(1)}, u32[]{:S(2)}, u32[]{:S(2)}) collective-permute-start(f32[32,128]{1,0:T(8,128)S(1)} %get-tuple-element.42), channel_id=1, source_target_pairs={{0,1},{1,0},{2,3},{3,2},{4,5},{5,4},{6,7},{7,6},{8,9},{9,8},{10,11... | collective-permute-start | bytes 49160 | tf_op jit(solution)/shard_map/ppermute | solution.py:429
  72.3 1.5 %collective-permute-start.16 = (f32[8,128]{1,0:T(8,128)S(1)}, f32[8,128]{1,0:T(8,128)S(1)}, u32[]{:S(2)}, u32[]{:S(2)}) collective-permute-start(f32[8,128]{1,0:T(8,128)S(1)} %get-tuple-element.44), channel_id=1, source_target_pairs={{0,4},{4,0},{8,12},{12,8},{1,5},{5,1},{9,13},{13,9},{2,6},{6,2},{1... | collective-permute-start | bytes 12296 | tf_op jit(solution)/shard_map/ppermute | solution.py:437
  73.8 4.0 %collective-permute-start.17 = (f32[8,128]{1,0:T(8,128)S(1)}, f32[8,128]{1,0:T(8,128)S(1)}, u32[]{:S(2)}, u32[]{:S(2)}) collective-permute-start(f32[8,128]{1,0:T(8,128)S(1)} %get-tuple-element.45), channel_id=1, source_target_pairs={{0,8},{4,12},{8,0},{12,4},{1,9},{5,13},{9,1},{13,5},{2,10},{6,14},... | collective-permute-start | bytes 12296 | tf_op jit(solution)/shard_map/ppermute | solution.py:437
  77.9 1.4 %collective-permute-start.18 = (f32[8,128]{1,0:T(8,128)S(1)}, f32[8,128]{1,0:T(8,128)S(1)}, u32[]{:S(2)}, u32[]{:S(2)}) collective-permute-start(f32[8,128]{1,0:T(8,128)S(1)} %get-tuple-element.46), channel_id=1, source_target_pairs={{0,12},{4,8},{8,4},{12,0},{1,13},{5,9},{9,5},{13,1},{2,14},{6,10},... | collective-permute-start | bytes 12296 | tf_op jit(solution)/shard_map/ppermute | solution.py:437
  79.5 3.8 %collective-permute-done.18.refs_3_ = f32[8,128]{1,0:T(8,128)S(1)} collective-permute-done((f32[8,128]{1,0:T(8,128)S(1)}, f32[8,128]{1,0:T(8,128)S(1)}, u32[]{:S(2)}, u32[]{:S(2)}) %collective-permute-start.18) | collective-permute-done | bytes 4128 | tf_op jit(solution)/shard_map/ppermute | solution.py:437
  (47 shorter events, 9.7 us)
Async XLA Ops:
  0.0 43.6 %collective-permute-start.9 = (bf16[1280,2560]{1,0:T(8,128)(2,1)}, bf16[1280,2560]{1,0:T(8,128)(2,1)S(1)}, u32[]{:S(2)}, u32[]{:S(2)}) collective-permute-start(bf16[1280,2560]{1,0:T(8,128)(2,1)} %param.16), channel_id=1, source_target_pairs={{0,1},{1,0},{2,2},{3,3},{4,5},{5,4},{6,6},{7,7},{8,9},{9,8},{10,10... | collective-permute-start | bytes 19660808 | tf_op jit(solution)/shard_map/ppermute | solution.py:360
  2.4 41.2 %collective-permute-start.8 = (bf16[1280,2560]{1,0:T(8,128)(2,1)}, bf16[1280,2560]{1,0:T(8,128)(2,1)S(1)}, u32[]{:S(2)}, u32[]{:S(2)}) collective-permute-start(bf16[1280,2560]{1,0:T(8,128)(2,1)} %param.16), channel_id=1, source_target_pairs={{0,0},{1,1},{2,3},{3,2},{4,4},{5,5},{6,7},{7,6},{8,8},{9,9},{10,11... | collective-permute-start | bytes 19660808 | tf_op jit(solution)/shard_map/ppermute | solution.py:359
  7.1 3.3 %collective-permute-start.1 = (bf16[2,128,640]{2,1,0:T(8,128)(2,1)S(1)}, bf16[2,128,640]{2,1,0:T(8,128)(2,1)S(1)}, u32[]{:S(2)}, u32[]{:S(2)}) collective-permute-start(bf16[2,128,640]{2,1,0:T(8,128)(2,1)S(1)} %get-tuple-element.31), channel_id=1, source_target_pairs={{0,0},{1,8},{4,4},{5,12},{8,1},{9,9},{12,5},{13,13},{2,2},{3,10},{... | collective-permute-start | bytes 983048 | tf_op jit(solution)/shard_map/ppermute | solution.py:356
  7.8 16.7 %collective-permute-start.2 = (bf16[2,128,640]{2,1,0:T(8,128)(2,1)S(1)}, bf16[2,128,640]{2,1,0:T(8,128)(2,1)S(1)}, u32[]{:S(2)}, u32[]{:S(2)}) collective-permute-start(bf16[2,128,640]{2,1,0:T(8,128)(2,1)S(1)} %get-tuple-element.32), channel_id=1, source_target_pairs={{0,4},{1,12},{4,0},{5,8},{8,5},{9,13},{12,1},{13,9},{2,6},{3,14},{... | collective-permute-start | bytes 983048 | tf_op jit(solution)/shard_map/ppermute | solution.py:356
  10.4 25.1 %collective-permute-start.3 = (bf16[2,128,640]{2,1,0:T(8,128)(2,1)S(1)}, bf16[2,128,640]{2,1,0:T(8,128)(2,1)S(1)}, u32[]{:S(2)}, u32[]{:S(2)}) collective-permute-start(bf16[2,128,640]{2,1,0:T(8,128)(2,1)S(1)} %collective-permute-done.1.refs_0_), channel_id=1, source_target_pairs={{0,1},{1,0},{2,3},{3,2},{4,5},{5,4},{6,7},{7,6},{8,9},{9,8},{10,11... | collective-permute-start | bytes 983048 | tf_op jit(solution)/shard_map/ppermute | solution.py:361
  24.5 11.0 %collective-permute-start.4 = (bf16[2,128,640]{2,1,0:T(8,128)(2,1)S(1)}, bf16[2,128,640]{2,1,0:T(8,128)(2,1)S(1)}, u32[]{:S(2)}, u32[]{:S(2)}) collective-permute-start(bf16[2,128,640]{2,1,0:T(8,128)(2,1)S(1)} %collective-permute-done.2.refs_1_), channel_id=1, source_target_pairs={{0,1},{1,0},{2,3},{3,2},{4,5},{5,4},{6,7},{7,6},{8,9},{9,8},{10,11... | collective-permute-start | bytes 983048 | tf_op jit(solution)/shard_map/ppermute | solution.py:361
  25.6 0.7 collective-permute-start
  26.2 10.9 %collective-permute-start.6 = (bf16[1,128,640]{2,1,0:T(8,128)(2,1)S(1)}, bf16[1,128,640]{2,1,0:T(8,128)(2,1)S(1)}, u32[]{:S(2)}, u32[]{:S(2)}) collective-permute-start(bf16[1,128,640]{2,1,0:T(8,128)(2,1)S(1)} %get-tuple-element.33), channel_id=1, source_target_pairs={{0,4},{1,12},{4,0},{5,8},{8,5},{9,13},{12,1},{13,9},{2,6},{3,14},{... | collective-permute-start | bytes 491528 | tf_op jit(solution)/shard_map/ppermute | solution.py:358
  36.5 1.7 %collective-permute-start.5 = (bf16[128,640]{1,0:T(8,128)(2,1)S(1)}, bf16[128,640]{1,0:T(8,128)(2,1)S(1)}, u32[]{:S(2)}, u32[]{:S(2)}) collective-permute-start(bf16[128,640]{1,0:T(8,128)(2,1)S(1)} %shard_map.121), channel_id=1, source_target_pairs={{0,0},{8,1},{4,4},{12,5},{1,8},{9,9},{5,12},{13,13},{2,2},{10,3},{... | collective-permute-start | bytes 491528 | tf_op jit(solution)/shard_map/ppermute | solution.py:387
  38.1 5.5 %collective-permute-start.7 = (bf16[128,640]{1,0:T(8,128)(2,1)S(1)}, bf16[128,640]{1,0:T(8,128)(2,1)S(1)}, u32[]{:S(2)}, u32[]{:S(2)}) collective-permute-start(bf16[128,640]{1,0:T(8,128)(2,1)S(1)} %shard_map.122), channel_id=1, source_target_pairs={{4,0},{12,1},{0,4},{8,5},{5,8},{13,9},{1,12},{9,13},{6,2},{14,3},{... | collective-permute-start | bytes 491528 | tf_op jit(solution)/shard_map/ppermute | solution.py:387
  44.7 9.2 %collective-permute-start.11 = (bf16[128,1280]{1,0:T(8,128)(2,1)S(1)}, bf16[128,1280]{1,0:T(8,128)(2,1)S(1)}, u32[]{:S(2)}, u32[]{:S(2)}) collective-permute-start(bf16[128,1280]{1,0:T(8,128)(2,1)S(1)} %shard_map.125), channel_id=1, source_target_pairs={{0,2},{2,0},{1,3},{3,1},{4,6},{6,4},{5,7},{7,5},{8,10},{10,8},{9,1... | collective-permute-start | bytes 983048 | tf_op jit(solution)/shard_map/ppermute | solution.py:401
  47.4 2.8 %copy-start.2 = (bf16[1,1,128,2560]{3,2,1,0:T(8,128)(2,1)S(1)}, bf16[1,1,128,2560]{3,2,1,0:T(8,128)(2,1)}, u32[]{:S(2)}) copy-start(bf16[1,1,128,2560]{3,2,1,0:T(8,128)(2,1)} %param.15) | copy-start | bytes 1966084
  47.4 2.8 %copy-start.3 = (f32[1,2560]{1,0:T(1,128)S(1)}, f32[1,2560]{1,0:T(1,128)}, u32[]{:S(2)}) copy-start(f32[1,2560]{1,0:T(1,128)} %refs_2_.5) | copy-start | bytes 30724
  47.5 6.1 %collective-permute-start.12 = (bf16[128,640]{1,0:T(8,128)(2,1)S(1)}, bf16[128,640]{1,0:T(8,128)(2,1)S(1)}, u32[]{:S(2)}, u32[]{:S(2)}) collective-permute-start(bf16[128,640]{1,0:T(8,128)(2,1)S(1)} %shard_map.126), channel_id=1, source_target_pairs={{0,2},{2,0},{1,3},{3,1},{4,6},{6,4},{5,7},{7,5},{8,10},{10,8},{9,1... | collective-permute-start | bytes 491528 | tf_op jit(solution)/shard_map/ppermute | solution.py:401
  48.2 7.1 %collective-permute-start.10 = (bf16[128,640]{1,0:T(8,128)(2,1)S(1)}, bf16[128,640]{1,0:T(8,128)(2,1)S(1)}, u32[]{:S(2)}, u32[]{:S(2)}) collective-permute-start(bf16[128,640]{1,0:T(8,128)(2,1)S(1)} %shard_map.124), channel_id=1, source_target_pairs={{0,2},{2,0},{1,3},{3,1},{4,6},{6,4},{5,7},{7,5},{8,10},{10,8},{9,1... | collective-permute-start | bytes 491528 | tf_op jit(solution)/shard_map/ppermute | solution.py:401
  50.3 3.4 %copy-start.1 = (bf16[2560,64]{0,1:T(8,128)(2,1)S(1)}, bf16[2560,64]{0,1:T(8,128)(2,1)}, u32[]{:S(2)}) copy-start(bf16[2560,64]{0,1:T(8,128)(2,1)} %param.20) | copy-start | bytes 983044
  50.3 3.4 %copy-start.5 = (f32[1,2560]{1,0:T(1,128)S(1)}, f32[1,2560]{1,0:T(1,128)}, u32[]{:S(2)}) copy-start(f32[1,2560]{1,0:T(1,128)} %refs_3_.5) | copy-start | bytes 30724
  50.3 33.0 %copy-start.6 = (f32[1,1,128,32]{2,3,1,0:T(8,128)S(1)}, f32[1,1,128,32]{2,3,1,0:T(8,128)}, u32[]{:S(2)}) copy-start(f32[1,1,128,32]{2,3,1,0:T(8,128)} %param.21) | copy-start | bytes 49156
  55.7 6.4 %collective-permute-start.13 = (f32[72,128]{1,0:T(8,128)S(1)}, f32[72,128]{1,0:T(8,128)S(1)}, u32[]{:S(2)}, u32[]{:S(2)}) collective-permute-start(f32[72,128]{1,0:T(8,128)S(1)} %shard_map.129.own_ref), channel_id=1, source_target_pairs={{0,2},{2,0},{1,3},{3,1},{4,6},{6,4},{5,7},{7,5},{8,10},{10,8},{9,1... | collective-permute-start | bytes 110600 | tf_op jit(solution)/shard_map/ppermute | solution.py:422
  57.8 4.3 %collective-permute-start.14 = (f32[64,128]{1,0:T(8,128)S(1)}, f32[64,128]{1,0:T(8,128)S(1)}, u32[]{:S(2)}, u32[]{:S(2)}) collective-permute-start(f32[64,128]{1,0:T(8,128)S(1)} %get-tuple-element.40.rows_own_ref), channel_id=1, source_target_pairs={{0,2},{2,0},{1,3},{3,1},{4,6},{6,4},{5,7},{7,5},{8,10},{10,8},{9,1... | collective-permute-start | bytes 98312 | tf_op jit(solution)/shard_map/ppermute | solution.py:371
  62.1 10.1 %collective-permute-start.15 = (f32[32,128]{1,0:T(8,128)S(1)}, f32[32,128]{1,0:T(8,128)S(1)}, u32[]{:S(2)}, u32[]{:S(2)}) collective-permute-start(f32[32,128]{1,0:T(8,128)S(1)} %get-tuple-element.42), channel_id=1, source_target_pairs={{0,1},{1,0},{2,3},{3,2},{4,5},{5,4},{6,7},{7,6},{8,9},{9,8},{10,11... | collective-permute-start | bytes 49160 | tf_op jit(solution)/shard_map/ppermute | solution.py:429
  72.3 7.0 %collective-permute-start.16 = (f32[8,128]{1,0:T(8,128)S(1)}, f32[8,128]{1,0:T(8,128)S(1)}, u32[]{:S(2)}, u32[]{:S(2)}) collective-permute-start(f32[8,128]{1,0:T(8,128)S(1)} %get-tuple-element.44), channel_id=1, source_target_pairs={{0,4},{4,0},{8,12},{12,8},{1,5},{5,1},{9,13},{13,9},{2,6},{6,2},{1... | collective-permute-start | bytes 12296 | tf_op jit(solution)/shard_map/ppermute | solution.py:437
  73.8 5.6 %collective-permute-start.17 = (f32[8,128]{1,0:T(8,128)S(1)}, f32[8,128]{1,0:T(8,128)S(1)}, u32[]{:S(2)}, u32[]{:S(2)}) collective-permute-start(f32[8,128]{1,0:T(8,128)S(1)} %get-tuple-element.45), channel_id=1, source_target_pairs={{0,8},{4,12},{8,0},{12,4},{1,9},{5,13},{9,1},{13,5},{2,10},{6,14},... | collective-permute-start | bytes 12296 | tf_op jit(solution)/shard_map/ppermute | solution.py:437
  77.9 5.4 %collective-permute-start.18 = (f32[8,128]{1,0:T(8,128)S(1)}, f32[8,128]{1,0:T(8,128)S(1)}, u32[]{:S(2)}, u32[]{:S(2)}) collective-permute-start(f32[8,128]{1,0:T(8,128)S(1)} %get-tuple-element.46), channel_id=1, source_target_pairs={{0,12},{4,8},{8,4},{12,0},{1,13},{5,9},{9,5},{13,1},{2,14},{6,10},... | collective-permute-start | bytes 12296 | tf_op jit(solution)/shard_map/ppermute | solution.py:437
  (4 other events, 3.0 us)
